TPU v7x, 512 devices: a whole 4x4x16 slice. The times are simulated.
512 devices in a mesh: dp: 4 (over y), outer: 32 (over z, core), inner: 4 (over x).
Axes of the slice: x: 4, y: 4, z: 16, core: 2. Of those that a mesh axis runs over, the one named last changes fastest.
Arguments:
- query_rows: bfloat16 [65536, 256], P(('dp', 'outer', 'inner')), parts along dimension 0, may hold values from -8 to 8
- key_rows: bfloat16 [65536, 256], P(('dp', 'outer', 'inner')), parts along dimension 0, may hold values from -8 to 8
- value_rows: bfloat16 [65536, 1024], P(('dp', 'outer', 'inner')), parts along dimension 0, may hold values from -6 to 6
- conv_weight: float32 [3, 1024], replicated, may hold values from -1 to 1
- norm_gain: float32 [1024], replicated, may hold values from 0.1 to 1.9
Outputs:
- layer_out: bfloat16 [65536, 1024], P(('dp', 'outer', 'inner')), parts along dimension 0
There are 4 independent parts, one for each index of `dp`. A program takes and returns all parts, laid end to end along the dimension named above; an argument that names none is the same for every part. Nothing has to cross between parts.
All inputs are finite; a program needn't handle non-finite values.
Results may differ from a plain program's by a relative error of at most 0.013.
Values may be sent and summed in bfloat16 or wider, within the bound.
No kernel may reach another device: no remote copies, remote signals or barrier semaphores. Data moves between devices by JAX's collectives and lax.ppermute only.
A program may use at most 128 MiB of HBM per device.

v0:
```python
import math

import jax
import jax.numpy as jnp
from jax import lax
from jax.sharding import PartitionSpec as P

HEADS = 16
FEAT = 16
VDIM = 64
PHI = 273
TAPS = 3
WIN = 64
BLK = 128


def shifted(value, axis, steps):
    count = lax.axis_size(axis)
    initial, last = (max(0, -steps), min(count, count - steps))
    return lax.ppermute(value, axis, [(source, source + steps) for source in range(initial, last)])


def carried_in(shard, axis, combine, identity):
    count, position = (lax.axis_size(axis), lax.axis_index(axis))
    everything = lax.all_gather(shard.astype(jnp.bfloat16), axis)
    start = jnp.broadcast_to(jnp.asarray(identity, shard.dtype), shard.shape)

    def hop(k, before):
        reached = k < position
        new = combine(before, everything[k].astype(shard.dtype))
        return jnp.where(reached, new, before)

    return lax.fori_loop(0, count, hop, start)


def features(rows_in):
    entries = rows_in.astype(jnp.float32)
    leading = entries.shape[:-1]
    pair_terms = (entries[..., :, None] * entries[..., None, :]).reshape(leading + (FEAT * FEAT,))
    const_term = jnp.ones(leading + (1,), jnp.float32)
    joined = jnp.concatenate(
        [const_term, entries * (1.0 / FEAT**0.25), pair_terms * (1.0 / math.sqrt(2.0 * FEAT))],
        axis=-1,
    )
    return joined.astype(jnp.bfloat16)


def convolve(padded, conv_weight, out_rows):
    conv_sum = jnp.zeros((out_rows, padded.shape[1]), jnp.float32)
    for tap_index in range(TAPS):
        offset = TAPS - 1 - tap_index
        conv_sum = conv_sum + conv_weight[tap_index][None, :] * padded[
            offset : offset + out_rows
        ].astype(jnp.float32)
    return conv_sum.astype(jnp.bfloat16)


def add_states(earlier_part, later_part):
    return earlier_part + later_part


def on_device(query_rows, key_rows, value_rows, conv_weight, norm_gain):
    local_rows = query_rows.shape[0]
    lag_rows = TAPS - 1
    score_scale = 1.0 / math.sqrt(FEAT)
    block_index = lax.axis_index(("outer", "inner"))
    tail_conv = convolve(value_rows[local_rows - WIN - lag_rows :], conv_weight, WIN)
    prev_keys, prev_conv, prev_raw = shifted(
        (key_rows[local_rows - WIN :], tail_conv, value_rows[local_rows - lag_rows :]),
        ("outer", "inner"),
        1,
    )
    conv_rows = convolve(jnp.concatenate([prev_raw, value_rows], 0), conv_weight, local_rows)
    block_total = local_rows // BLK
    query_blocks = query_rows.reshape(block_total, BLK, HEADS, FEAT)
    key_blocks = key_rows.reshape(block_total, BLK, HEADS, FEAT)
    value_blocks = conv_rows.reshape(block_total, BLK, HEADS, VDIM)
    phi_key = features(key_blocks)
    block_states = jnp.einsum(
        "ntaf,ntac->nfac", phi_key, value_blocks, preferred_element_type=jnp.float32
    )
    local_before = jnp.concatenate(
        [jnp.zeros_like(block_states), jnp.cumsum(block_states[:-1], axis=0)], 0
    )
    local_total = local_before[-1] + block_states[-1]
    scores = (
        jnp.einsum("niaf,njaf->naij", query_blocks, key_blocks, preferred_element_type=jnp.float32)
        * score_scale
    )
    causal = jnp.arange(BLK)[:, None] >= jnp.arange(BLK)[None, :]
    intra_weights = jnp.where(causal[None, None], 1.0 + scores + 0.5 * scores * scores, 0.0).astype(
        jnp.bfloat16
    )
    own_part = jnp.einsum(
        "naij,njac->niac", intra_weights, value_blocks, preferred_element_type=jnp.float32
    )
    win_blocks = local_rows // WIN
    ext_keys = jnp.concatenate([prev_keys, key_rows], 0).reshape(win_blocks + 1, WIN, HEADS, FEAT)
    ext_conv = jnp.concatenate([prev_conv, conv_rows], 0).reshape(win_blocks + 1, WIN, HEADS, VDIM)
    near_keys = jnp.concatenate([ext_keys[:-1], ext_keys[1:]], axis=1)
    near_values = jnp.concatenate([ext_conv[:-1], ext_conv[1:]], axis=1)
    query_windows = query_rows.reshape(win_blocks, WIN, HEADS, FEAT)
    window_scores = (
        jnp.einsum("niaf,njaf->naij", query_windows, near_keys, preferred_element_type=jnp.float32)
        * score_scale
    )
    offset_rows = jnp.arange(2 * WIN)[None, :] - jnp.arange(WIN)[:, None]
    inside = (offset_rows >= 0) & (offset_rows <= WIN)
    position = (
        block_index * local_rows
        + jnp.arange(win_blocks, dtype=jnp.int32)[:, None] * WIN
        + jnp.arange(2 * WIN, dtype=jnp.int32)[None, :]
        - WIN
    )
    allowed = inside[None, None] & (position >= 0)[:, None, None, :]
    masked = jnp.where(allowed, window_scores, -1e30)
    row_max = jnp.max(masked, axis=-1, keepdims=True)
    exp_scores = jnp.where(allowed, jnp.exp(masked - row_max), 0.0)
    window_probs = (exp_scores / jnp.sum(exp_scores, axis=-1, keepdims=True)).astype(jnp.bfloat16)
    window_out = jnp.einsum(
        "naij,njac->niac", window_probs, near_values, preferred_element_type=jnp.float32
    )
    sent_state = local_total.reshape(PHI, HEADS * VDIM)
    zero_state = jnp.zeros(sent_state.shape, jnp.float32)
    group_sum = None
    inner_prefix = carried_in(sent_state, "inner", add_states, zero_state)
    group_sum = lax.psum(sent_state, "inner")
    outer_before = carried_in(group_sum, "outer", add_states, zero_state)
    carried = inner_prefix + outer_before
    carried = carried.reshape(PHI, HEADS, VDIM)
    state_rounded = (carried[None] + local_before).astype(jnp.bfloat16)
    phi_query = features(query_blocks)
    earlier_part = jnp.einsum(
        "ntaf,nfac->ntac", phi_query, state_rounded, preferred_element_type=jnp.float32
    )
    numerator = (own_part + earlier_part).reshape(local_rows, HEADS, VDIM)
    mean_square = jnp.mean(numerator * numerator, axis=-1, keepdims=True)
    linear_out = numerator * lax.rsqrt(mean_square + 1e-06) * norm_gain.reshape(HEADS, VDIM)
    mixed_heads = linear_out + window_out.reshape(local_rows, HEADS, VDIM)
    return mixed_heads.astype(jnp.bfloat16).reshape(local_rows, HEADS * VDIM)


def solution(mesh):
    in_specs = (
        P(("dp", "outer", "inner"), None),
        P(("dp", "outer", "inner"), None),
        P(("dp", "outer", "inner"), None),
        P(),
        P(),
    )
    out_specs = P(("dp", "outer", "inner"), None)
    return jax.shard_map(
        on_device, mesh=mesh, in_specs=in_specs, out_specs=out_specs, check_vma=False
    )
```

profile of v0, /device:TPU:1, one launch (start us, length us, event | category | flops | bytes accessed | tf_op | source)
XLA Modules:
  0.0 259.6 jit_solution(5805641317175301192)
XLA Ops:
  7.5 3.9 %collective-permute-start = (bf16[2,1024]{0,1:T(8,128)(2,1)S(1)}, bf16[2,1024]{0,1:T(8,128)(2,1)S(1)}, u32[]{:S(2)}, u32[]{:S(2)}) collective-permute-start(bf16[2,1024]{0,1:T(8,128)(2,1)S(1)} %copy.66), channel_id=1, source_target_pairs={{0,1},{1,2},{2,3},{3,4},{4,5},{5,6},{6,7},{7,8},{8,9},{9,10},{10,1... | collective-permute-start | bytes 12296 | tf_op jit(solution)/shard_map/ppermute | solution.py:20
  13.0 4.3 %collective-permute-done = bf16[2,1024]{0,1:T(8,128)(2,1)S(1)} collective-permute-done((bf16[2,1024]{0,1:T(8,128)(2,1)S(1)}, bf16[2,1024]{0,1:T(8,128)(2,1)S(1)}, u32[]{:S(2)}, u32[]{:S(2)}) %collective-permute-start) | collective-permute-done | bytes 4128 | tf_op jit(solution)/shard_map/ppermute | solution.py:20
  19.6 2.2 copy.70
  22.3 29.1 %all-reduce.1 = bf16[273,1024]{1,0:T(8,128)(2,1)} all-reduce(f32[273,1024]{1,0:T(8,128)S(1)} %copy.71), channel_id=1, replica_groups=mesh['dp'=4,'outer'=32,'inner'=4] {'inner'}, use_global_device_ids=true, to_apply=%region_2.3 | all-reduce | flops 279552 | bytes 1677312 | tf_op jit(solution)/shard_map/psum | solution.py:127
  52.8 2.1 collective-permute-start.1
  55.0 2.3 collective-permute-start.2
  63.2 10.6 %collective-permute-done.2 = bf16[64,256]{1,0:T(8,128)(2,1)S(1)} collective-permute-done((bf16[64,256]{1,0:T(8,128)(2,1)S(1)}, bf16[64,256]{1,0:T(8,128)(2,1)S(1)}, u32[]{:S(2)}, u32[]{:S(2)}) %collective-permute-start.2) | collective-permute-done | bytes 32800 | tf_op jit(solution)/shard_map/ppermute | solution.py:20
  74.1 1.9 fusion.77
  77.5 6.4 %convolution_bitcast_fusion = f32[2,64,16,64]{1,3,2,0:T(8,128)} fusion(bf16[2,64,16,64]{1,3,2,0:T(8,128)(2,1)} %copy.79, bf16[2,64,16,64]{1,3,2,0:T(8,128)(2,1)S(1)} %copy.78, f32[2,16,64]{2,1,0:T(8,128)S(1)} %fusion.77, pred[2,64,128]{2,1,0:T(8,128)(4,1)S(1)} %broadcast_and_fusion, bf16[2,64,16,16]{1,3,2,0:T(8,128)(2,1)} %copy.83, ...), kind=kOutput, calls=%fused_computation.9 | convolution fusion | flops 44828800 | bytes 1269760 | tf_op jit(solution)/shard_map/naij,njac->niac/dot_general | solution.py:120
  83.9 2.0 copy.93
  87.3 6.8 %while.28 = (s32[]{:T(128)}, f32[273,1024]{1,0:T(8,128)S(1)}, s32[]{:T(128)}, bf16[4,273,1024]{2,1,0:T(8,128)(2,1)}, s32[]{:T(128)}, /*index=5*/s32[]{:T(128)}) while((s32[]{:T(128)}, f32[273,1024]{1,0:T(8,128)S(1)}, s32[]{:T(128)}, bf16[4,273,1024]{2,1,0:T(8,128)(2,1)}, s32[]{:T(128)}, /*index=5*/s32[]{:T(128)}) %tuple.63), condition=%wide.region_1.2_spmd.clone, body=%wide.region_0.1_spmd.clone.sunk | while | flops 1118212 | bytes 2795613 | solution.py:33
  87.3 1.7 add_select_fusion.4
  89.0 1.7 add_select_fusion.4
  90.7 1.7 add_select_fusion.4
  92.4 1.7 add_select_fusion.4
  94.1 100.6 %all-gather.7.cloned.1.call-done = bf16[32,273,1024]{2,1,0:T(8,128)(2,1)} async-done(((bf16[1,273,1024]{2,1,0:T(8,128)(2,1)}), bf16[32,273,1024]{2,1,0:T(8,128)(2,1)}) %all-gather.7.cloned.1.call-update) | async-done | bytes 17891344 | tf_op jit(solution)/shard_map/all_gather | solution.py:25
  194.8 54.4 %while.29 = (s32[]{:T(128)}, f32[273,1024]{1,0:T(8,128)S(1)}, s32[]{:T(128)}, bf16[32,273,1024]{2,1,0:T(8,128)(2,1)}, s32[]{:T(128)}, /*index=5*/s32[]{:T(128)}) while((s32[]{:T(128)}, f32[273,1024]{1,0:T(8,128)S(1)}, s32[]{:T(128)}, bf16[32,273,1024]{2,1,0:T(8,128)(2,1)}, s32[]{:T(128)}, /*index=5*/s32[]{:T(128)}) %tuple.66), condition=%wide.region_4.5_spmd.clone, body=%wide.region_3.4_spmd.clone.sunk | while | flops 1118212 | bytes 2795613 | solution.py:33
  196.5 1.7 add_select_fusion.5
  198.2 1.7 add_select_fusion.5
  199.9 1.7 add_select_fusion.5
  201.6 1.7 add_select_fusion.5
  203.3 1.7 add_select_fusion.5
  205.0 1.7 add_select_fusion.5
  206.7 1.7 add_select_fusion.5
  208.4 1.7 add_select_fusion.5
  210.1 1.7 add_select_fusion.5
  211.8 1.7 add_select_fusion.5
  213.5 1.7 add_select_fusion.5
  215.2 1.7 add_select_fusion.5
  216.9 1.7 add_select_fusion.5
  218.6 1.7 add_select_fusion.5
  220.3 1.7 add_select_fusion.5
  222.0 1.7 add_select_fusion.5
  223.7 1.7 add_select_fusion.5
  225.4 1.7 add_select_fusion.5
  227.1 1.7 add_select_fusion.5
  228.8 1.7 add_select_fusion.5
  230.5 1.7 add_select_fusion.5
  232.2 1.7 add_select_fusion.5
  233.9 1.7 add_select_fusion.5
  235.6 1.7 add_select_fusion.5
  237.3 1.7 add_select_fusion.5
  239.0 1.7 add_select_fusion.5
  240.7 1.7 add_select_fusion.5
  242.4 1.7 add_select_fusion.5
  244.1 1.7 add_select_fusion.5
  245.8 1.7 add_select_fusion.5
  247.5 1.7 add_select_fusion.5
  (74 shorter events, 20.7 us)
Async XLA Ops:
  6.5 6.3 %copy-start.3 = (bf16[128,1024]{1,0:T(8,128)(2,1)S(1)}, bf16[128,1024]{1,0:T(8,128)(2,1)}, u32[]{:S(2)}) copy-start(bf16[128,1024]{1,0:T(8,128)(2,1)} %param.11) | copy-start | bytes 786436
  6.5 6.3 %copy-start.8 = (f32[3,1024]{1,0:T(4,128)S(1)}, f32[3,1024]{1,0:T(4,128)}, u32[]{:S(2)}) copy-start(f32[3,1024]{1,0:T(4,128)} %param.12) | copy-start | bytes 36868
  6.5 80.8 %all-gather.5.cloned.1.call-start = ((), (), s32[]{:S(2)}) async-start(), calls=%async_computation | async-start | bytes 2867200 | tf_op jit(solution)/shard_map/all_gather | solution.py:25
  7.5 9.8 %collective-permute-start = (bf16[2,1024]{0,1:T(8,128)(2,1)S(1)}, bf16[2,1024]{0,1:T(8,128)(2,1)S(1)}, u32[]{:S(2)}, u32[]{:S(2)}) collective-permute-start(bf16[2,1024]{0,1:T(8,128)(2,1)S(1)} %copy.66), channel_id=1, source_target_pairs={{0,1},{1,2},{2,3},{3,4},{4,5},{5,6},{6,7},{7,8},{8,9},{9,10},{10,1... | collective-permute-start | bytes 12296 | tf_op jit(solution)/shard_map/ppermute | solution.py:20
  21.9 172.9 %all-gather.7.cloned.1.call-start = ((), (), s32[]{:S(2)}) async-start(), calls=%async_computation.1 | async-start | bytes 18923520 | tf_op jit(solution)/shard_map/all_gather | solution.py:25
  51.4 3.6 %copy-start.2 = (bf16[128,256]{1,0:T(8,128)(2,1)S(1)}, bf16[128,256]{1,0:T(8,128)(2,1)}, u32[]{:S(2)}) copy-start(bf16[128,256]{1,0:T(8,128)(2,1)} %param.10) | copy-start | bytes 196612
  51.4 6.0 %copy-start.6 = (bf16[128,256]{1,0:T(8,128)(2,1)S(1)}, bf16[128,256]{1,0:T(8,128)(2,1)}, u32[]{:S(2)}) copy-start(bf16[128,256]{1,0:T(8,128)(2,1)} %param.9) | copy-start | bytes 196612
  52.8 23.2 %collective-permute-start.1 = (bf16[64,1024]{0,1:T(8,128)(2,1)}, bf16[64,1024]{0,1:T(8,128)(2,1)}, u32[]{:S(2)}, u32[]{:S(2)}) collective-permute-start(bf16[64,1024]{0,1:T(8,128)(2,1)} %add_convert_fusion.1), channel_id=1, source_target_pairs={{0,1},{1,2},{2,3},{3,4},{4,5},{5,6},{6,7},{7,8},{8,9},{9,10},{10,1... | collective-permute-start | bytes 393224 | tf_op jit(solution)/shard_map/ppermute | solution.py:20
  55.0 18.8 %collective-permute-start.2 = (bf16[64,256]{1,0:T(8,128)(2,1)S(1)}, bf16[64,256]{1,0:T(8,128)(2,1)S(1)}, u32[]{:S(2)}, u32[]{:S(2)}) collective-permute-start(bf16[64,256]{1,0:T(8,128)(2,1)S(1)} %slice.69), channel_id=1, source_target_pairs={{0,1},{1,2},{2,3},{3,4},{4,5},{5,6},{6,7},{7,8},{8,9},{9,10},{10,1... | collective-permute-start | bytes 98312 | tf_op jit(solution)/shard_map/ppermute | solution.py:20
  57.7 16.4 %copy-start.4 = (bf16[2,64,16,16]{1,0,3,2:T(2,128)(2,1)}, bf16[2,64,16,16]{1,0,3,2:T(2,128)(2,1)S(1)}, u32[]{:S(2)}) copy-start(bf16[2,64,16,16]{1,0,3,2:T(2,128)(2,1)S(1)} %reshape.244) | copy-start | bytes 196612
  74.1 1.9 copy-start.5
  249.2 1.0 copy-start.10
  249.4 1.3 copy-start.1
  249.4 1.3 copy-start.7
  250.7 1.0 copy-start
  250.7 1.0 copy-start.9
Sparse Core Ops, SparseCore 0:
  22.0 51.1 all-gather.4
  75.2 119.4 all-gather.6
where the time goes:
time: 262 us; the launch traced here: 260 us
  waiting for transfers between devices  116 us (44%)
  other arithmetic  66.4 us (25%)
  blocking collectives  29.1 us (11%)
  between operations  13.8 us (5%)
  local copies, waits for them, and re-layouts  13.5 us (5%)
  matrix products  12 us (5%)
  starting transfers between devices  8.44 us (3%)
    all_gather x2, waiting for transfers between devices, carried_in(): everything = lax.all_gather(shard.astype(jnp.bfloat16), axis)  101 us
    select_n x36, other arithmetic, hop(): return jnp.where(reached, new, before)  60.4 us
    psum x1, blocking collectives, on_device(): group_sum = lax.psum(sent_state, 'inner')  29.1 us
    ppermute x3, waiting for transfers between devices, shifted(): lax.ppermute(value, axis, [(source, source + steps) for source in range(i...  15 us
    ppermute x3, starting transfers between devices, shifted(): lax.ppermute(value, axis, [(source, source + steps) for source in range(i...  8.4 us
    dot_general x1, matrix products, on_device(): jnp.einsum('naij,njac->niac', window_probs, near_values, preferred_elemen...  6.4 us
  transfers between devices with their start and end apart: 5, of which 3 were waited for; matrix products, arithmetic and copies ran while one was open for 11% of the time, Pallas kernels for 0%

commit v1 on v0

v1 whole, which is shorter than its diff:
```python
import jax
import jax.numpy as jnp
import numpy as np
from jax import lax
from jax.experimental import pallas as pl
from jax.experimental.pallas import tpu as pltpu
from jax.sharding import Mesh, PartitionSpec as P

HEADS = 16
FEAT = 16
VDIM = 64
TAPS = 3
WIN = 64
BLK = 128
NPHI = 160
SPLIT = 128
STATE_ROWS = VDIM + (NPHI - SPLIT)
PART = FEAT + FEAT + VDIM
F32 = jnp.float32
BF16 = jnp.bfloat16


def nt(lhs, rhs):
    return lax.dot_general(lhs, rhs, (((1,), (1,)), ((), ())), preferred_element_type=F32)


def tn(lhs, rhs):
    return lax.dot_general(lhs, rhs, (((0,), (0,)), ((), ())), preferred_element_type=F32)


def nn(lhs, rhs):
    return lax.dot_general(lhs, rhs, (((1,), (0,)), ((), ())), preferred_element_type=F32)


def features(entries, weighted):
    lin, diag, off = (0.25, 1.0 / 32.0, 1.0 / 16.0) if weighted else (1.0, 1.0, 1.0)
    rows = [entries * lin if weighted else entries]
    base = entries * off if weighted else entries
    rows.append(entries * entries * diag if weighted else entries * entries)
    for step in range(1, FEAT // 2):
        rolled = jnp.concatenate([entries[step:], entries[:step]], axis=0)
        rows.append(base * rolled)
    rows.append(base[: FEAT // 2] * entries[FEAT // 2 :])
    tail = lax.broadcasted_iota(jnp.int32, (8, entries.shape[1]), 0)
    rows.append(jnp.where(tail == 0, 1.0, 0.0).astype(F32))
    return jnp.concatenate(rows, axis=0).astype(BF16)


def pack_kernel(q_ref, k_ref, v_ref, halo_ref, w_ref, out_ref):
    value = v_ref[...].astype(F32)
    halo = halo_ref[...].astype(F32)
    row = lax.broadcasted_iota(jnp.int32, value.shape, 0)
    last = halo[1:2, :]
    before = halo[0:1, :]
    one = jnp.where(row == 0, last, pltpu.roll(value, 1, 0))
    two = jnp.where(row == 0, before, jnp.where(row == 1, last, pltpu.roll(value, 2, 0)))
    conv = w_ref[0:1, :] * value + w_ref[1:2, :] * one + w_ref[2:3, :] * two
    out_ref[:, 0:FEAT, :] = q_ref[...].T.reshape(HEADS, FEAT, BLK)
    out_ref[:, FEAT : 2 * FEAT, :] = k_ref[...].T.reshape(HEADS, FEAT, BLK)
    out_ref[:, 2 * FEAT :, :] = conv.astype(BF16).T.reshape(HEADS, VDIM, BLK)


def state_kernel(x_ref, sent_ref, own_ref):
    count = x_ref.shape[0]
    total = jnp.zeros((VDIM, NPHI), F32)
    for blk in range(count):
        phi = features(x_ref[blk, FEAT : 2 * FEAT, :].astype(F32), True)
        total = total + nt(x_ref[blk, 2 * FEAT :, :], phi)
    rest = total[:, SPLIT:].T
    state = jnp.concatenate([total[:, :SPLIT], jnp.concatenate([rest, rest], axis=1)], axis=0)
    own_ref[...] = state
    sent_ref[0:STATE_ROWS, :] = state.astype(BF16)
    sent_ref[STATE_ROWS:, :] = x_ref[count - 1, FEAT:, :]


def local_kernel(first_ref, x_ref, recv_ref, num_ref, win_ref, phi_ref):
    count = x_ref.shape[0]
    key_row = lax.broadcasted_iota(jnp.int32, (BLK, BLK), 0)
    query_lane = lax.broadcasted_iota(jnp.int32, (BLK, BLK), 1)
    causal = key_row <= query_lane
    span = WIN + BLK
    near_row = lax.broadcasted_iota(jnp.int32, (span, BLK), 0)
    near_lane = lax.broadcasted_iota(jnp.int32, (span, BLK), 1)
    inside = (near_row >= near_lane) & (near_row <= near_lane + WIN)
    inside_first = inside & ((near_row >= WIN) | (first_ref[0] == 0))
    before_key = recv_ref[STATE_ROWS : STATE_ROWS + FEAT, :]
    before_val = recv_ref[STATE_ROWS + FEAT :, :]
    state = jnp.zeros((VDIM, NPHI), F32)
    blank = jnp.zeros((BLK - WIN, BLK), BF16)
    for blk in range(count):
        query = x_ref[blk, 0:FEAT, :]
        key = x_ref[blk, FEAT : 2 * FEAT, :]
        value = x_ref[blk, 2 * FEAT :, :]
        phi_query = features(query.astype(F32), False)
        phi_ref[:, blk * BLK : (blk + 1) * BLK] = phi_query
        scores = tn(jnp.concatenate([before_key, key], axis=1), query) * 0.25
        own = scores[BLK:]
        weights = jnp.where(causal, 1.0 + own + 0.5 * own * own, 0.0).astype(BF16)
        num = nn(value, weights)
        if blk > 0:
            num = num + nn(state.astype(BF16), phi_query)
        num_ref[blk] = num
        masked = jnp.where(inside_first if blk == 0 else inside, scores[BLK - WIN :], -1e30)
        row_max = jnp.max(masked, axis=0, keepdims=True)
        exp_scores = jnp.exp(masked - row_max)
        row_sum = jnp.sum(exp_scores, axis=0, keepdims=True)
        probs = jnp.concatenate([blank, exp_scores.astype(BF16)], axis=0)
        win = nn(jnp.concatenate([before_val, value], axis=1), probs)
        win_ref[blk] = win / row_sum
        if blk + 1 < count:
            state = state + nt(value, features(key.astype(F32), True))
        before_key, before_val = key, value


def final_kernel(quad_ref, recv_ref, others_ref, num_ref, win_ref, phi_ref, gain_ref, out_ref):
    carried = recv_ref[0:STATE_ROWS, :].astype(F32)
    for quad in range(others_ref.shape[0]):
        reached = quad < quad_ref[0]
        carried = carried + jnp.where(reached, others_ref[quad].astype(F32), 0.0)
    state = jnp.concatenate([carried[:VDIM], carried[VDIM:, :VDIM].T], axis=1).astype(BF16)
    gain = gain_ref[...]
    for blk in range(num_ref.shape[0]):
        num = num_ref[blk] + nn(state, phi_ref[:, blk * BLK : (blk + 1) * BLK])
        mean_square = jnp.sum(num * num, axis=0, keepdims=True) * (1.0 / VDIM)
        linear = num * lax.rsqrt(mean_square + 1e-06) * gain
        out_ref[blk] = (linear + win_ref[blk]).astype(BF16)


def unpack_kernel(x_ref, out_ref):
    out_ref[...] = x_ref[...].reshape(HEADS * VDIM, BLK).T


SMEM = pl.BlockSpec(memory_space=pltpu.SMEM)
VMEM = pl.BlockSpec(memory_space=pltpu.VMEM)


def call(kernel, shapes, scalars, arrays):
    outs = tuple(jax.ShapeDtypeStruct(shape, dtype) for shape, dtype in shapes)
    single = len(outs) == 1
    return pl.pallas_call(
        kernel,
        out_shape=outs[0] if single else outs,
        in_specs=[SMEM] * len(scalars) + [VMEM] * len(arrays),
        out_specs=VMEM if single else tuple(VMEM for _ in outs),
    )(*scalars, *arrays)


def on_device(query_rows, key_rows, value_rows, conv_weight, norm_gain):
    seq = ("quad", "half", "pair", "core", "inner")
    group = ("pair", "core", "inner")
    members = lax.axis_size(group)
    blocks = lax.axis_size(seq)
    halo = lax.ppermute(value_rows[BLK - (TAPS - 1) :], seq, [(i, i + 1) for i in range(blocks - 1)])
    packed = call(
        pack_kernel,
        [((HEADS, PART, BLK), BF16)],
        [],
        [query_rows, key_rows, value_rows, halo, conv_weight],
    )
    mine = lax.all_to_all(packed, group, 0, 0)
    sent, own_state = call(
        state_kernel,
        [((STATE_ROWS + FEAT + VDIM, BLK), BF16), ((STATE_ROWS, BLK), F32)],
        [],
        [mine],
    )
    groups = lax.axis_size(("quad", "half"))
    recv = lax.ppermute(sent, ("quad", "half"), [(i, i + 1) for i in range(groups - 1)])
    two = (own_state + recv[:STATE_ROWS].astype(F32)).astype(BF16)
    quads = lax.axis_size("quad")
    others = lax.all_to_all(jnp.broadcast_to(two[None], (quads, STATE_ROWS, BLK)), "quad", 0, 0)
    first = (lax.axis_index(("quad", "half")) == 0).astype(jnp.int32).reshape(1)
    tokens = members * BLK
    num, win, phi = call(
        local_kernel,
        [((members, VDIM, BLK), F32), ((members, VDIM, BLK), F32), ((NPHI, tokens), BF16)],
        [first],
        [mine, recv],
    )
    head = lax.axis_index(group)
    gain = lax.dynamic_slice(norm_gain, (head * VDIM,), (VDIM,))
    gain = jnp.broadcast_to(gain[:, None], (VDIM, BLK))
    done = call(
        final_kernel,
        [((members, VDIM, BLK), BF16)],
        [lax.axis_index("quad").astype(jnp.int32).reshape(1)],
        [recv, others, num, win, phi, gain],
    )
    heads = lax.all_to_all(done, group, 0, 0)
    return call(unpack_kernel, [((BLK, HEADS * VDIM), BF16)], [], [heads])


def solution(mesh):
    outer, inner = mesh.shape["outer"], mesh.shape["inner"]
    pair = 16 // inner // 2
    shape = (mesh.shape["dp"], outer // (2 * 2 * pair), 2, pair, 2, inner)
    split = Mesh(
        np.asarray(mesh.devices).reshape(shape), ("dp", "quad", "half", "pair", "core", "inner")
    )
    rows = P(("dp", "quad", "half", "pair", "core", "inner"), None)
    return jax.shard_map(
        on_device,
        mesh=split,
        in_specs=(rows, rows, rows, P(), P()),
        out_specs=rows,
        check_vma=False,
    )
```

time: 262 us -> 84.3 us (0.32)
  waiting for transfers between devices: 116 us -> 10 us
  other arithmetic: 66.4 us -> 0.82 us
  starting transfers between devices: 8.44 us -> 24.7 us
  Pallas kernels: 0 us -> 14.5 us
  between operations: 13.8 us -> 0.03 us
  matrix products: 12 us -> 0 us
  local copies, waits for them, and re-layouts: 13.5 us -> 3.42 us
    all_gather x2 -> x0, waiting for transfers between devices: 101 us -> none  [carried_in(): everything = lax.all_gather(shard.astype(jnp.bfloat16), axis)]
    select_n x36 -> x0, other arithmetic: 60.4 us -> none  [hop(): return jnp.where(reached, new, before)]
    all_to_all x0 -> x2, blocking collectives: none -> 30.1 us  [the longest x1 15.4 us: on_device(): mine = lax.all_to_all(packed, group, 0, 0)]
    psum x1 -> x0, blocking collectives: 29.1 us -> none  [on_device(): group_sum = lax.psum(sent_state, 'inner')]
    all_to_all x0 -> x1, starting transfers between devices: none -> 16.7 us  [on_device(): lax.all_to_all(jnp.broadcast_to(two[None], (quads, STATE_ROWS, BLK)), 'qu...]
    pallas_call x0 -> x5, Pallas kernels: none -> 14.5 us  [call(): pl.pallas_call(kernel, out_shape=outs[0] if single else outs, in_specs=[S...]
    ppermute x3 -> x2, waiting for transfers between devices: 15 us -> 4.54 us  [the longest x1 3.1 us: on_device(): lax.ppermute(value_rows[BLK - (TAPS - 1):], seq, [(i, i + 1) for i in ran...]
    dot_general x4 -> x0, matrix products: 10.1 us -> none  [the longest x1 6.4 us: on_device(): jnp.einsum('naij,njac->niac', window_probs, near_values, preferred_elemen...]
  transfers between devices with their start and end apart: 5 -> 3, of which waited for: 3 -> 3; matrix products, arithmetic and copies ran while one was open for 11% -> 1% of each run, Pallas kernels for 0% -> 7%
where the time goes in v1:
time: 84.3 us; the launch traced here: 83.6 us
  blocking collectives  30.1 us (36%)
  starting transfers between devices  24.7 us (29%)
  Pallas kernels  14.5 us (17%)
  waiting for transfers between devices  10 us (12%)
  local copies, waits for them, and re-layouts  3.42 us (4%)
    all_to_all x1, starting transfers between devices, on_device(): lax.all_to_all(jnp.broadcast_to(two[None], (quads, STATE_ROWS, BLK)), 'qu...  16.7 us
    all_to_all x1, blocking collectives, on_device(): mine = lax.all_to_all(packed, group, 0, 0)  15.4 us
    all_to_all x1, blocking collectives, on_device(): heads = lax.all_to_all(done, group, 0, 0)  14.6 us
    pallas_call x5, Pallas kernels, call(): pl.pallas_call(kernel, out_shape=outs[0] if single else outs, in_specs=[S...  14.5 us
    all_to_all x1, waiting for transfers between devices, on_device(): lax.all_to_all(jnp.broadcast_to(two[None], (quads, STATE_ROWS, BLK)), 'qu...  5.5 us
    ppermute x1, starting transfers between devices, on_device(): lax.ppermute(sent, ('quad', 'half'), [(i, i + 1) for i in range(groups -...  4.05 us
    ppermute x1, starting transfers between devices, on_device(): lax.ppermute(value_rows[BLK - (TAPS - 1):], seq, [(i, i + 1) for i in ran...  3.94 us
    ppermute x1, waiting for transfers between devices, on_device(): lax.ppermute(value_rows[BLK - (TAPS - 1):], seq, [(i, i + 1) for i in ran...  3.1 us
  transfers between devices with their start and end apart: 3, of which 3 were waited for; matrix products, arithmetic and copies ran while one was open for 1% of the time, Pallas kernels for 7%

profile of v1, /device:TPU:1, one launch (start us, length us, event | category | flops | bytes accessed | tf_op | source)
XLA Modules:
  0.0 83.6 jit_solution(13489215650005679920)
XLA Ops:
  0.0 0.7 slice.6
  0.7 3.9 %collective-permute-start = (bf16[2,1024]{1,0:T(2,128)(2,1)S(1)}, bf16[2,1024]{1,0:T(2,128)(2,1)S(1)}, u32[]{:S(2)}, u32[]{:S(2)}) collective-permute-start(bf16[2,1024]{1,0:T(2,128)(2,1)S(1)} %slice.6), channel_id=1, source_target_pairs={{0,1},{1,2},{2,3},{3,4},{4,5},{5,6},{6,7},{7,8},{8,9},{9,10},{10,1... | collective-permute-start | bytes 12296 | tf_op jit(solution)/shard_map/ppermute | solution.py:153
  4.7 3.1 %collective-permute-done.halo_ref = bf16[2,1024]{1,0:T(2,128)(2,1)S(1)} collective-permute-done((bf16[2,1024]{1,0:T(2,128)(2,1)S(1)}, bf16[2,1024]{1,0:T(2,128)(2,1)S(1)}, u32[]{:S(2)}, u32[]{:S(2)}) %collective-permute-start) | collective-permute-done | bytes 4128 | tf_op jit(solution)/shard_map/ppermute | solution.py:153
  7.8 0.0 copy-start.2
  7.8 0.6 copy-done.2
  8.4 2.0 %shard_map.55 = bf16[16,96,128]{2,1,0:T(8,128)(2,1)} custom-call(bf16[128,256]{1,0:T(8,128)(2,1)} %q_ref.1, bf16[128,256]{1,0:T(8,128)(2,1)} %k_ref.1, bf16[128,1024]{1,0:T(8,128)(2,1)} %v_ref.1, bf16[2,1024]{1,0:T(2,128)(2,1)} %copy-done.2, f32[3,1024]{1,0:T(4,128)} %w_ref.1), custom_call_target="tpu_custom_call" | custom-call | tf_op jit(solution)/shard_map/pallas_call | solution.py:140
  10.4 15.4 %all_to_all.15.x_ref = bf16[16,96,128]{2,1,0:T(8,128)(2,1)} all-to-all(bf16[16,96,128]{2,1,0:T(8,128)(2,1)} %shard_map.55), channel_id=1, replica_groups=mesh['dp'=4,'quad'=4,'half'=2,'pair'=2,'core'=2,'inner'=4] {'pair','core..., dimensions={0} | all-to-all | bytes 786432 | tf_op jit(solution)/shard_map/all_to_all | solution.py:160
  25.8 2.3 %shard_map.56 = (bf16[176,128]{1,0:T(8,128)(2,1)}, f32[96,128]{1,0:T(8,128)}) custom-call(bf16[16,96,128]{2,1,0:T(8,128)(2,1)} %all_to_all.15.x_ref), custom_call_target="tpu_custom_call" | custom-call | tf_op jit(solution)/shard_map/pallas_call | solution.py:140
  28.2 4.1 %collective-permute-start.1 = (bf16[176,128]{1,0:T(8,128)(2,1)}, bf16[176,128]{1,0:T(8,128)(2,1)S(1)}, u32[]{:S(2)}, u32[]{:S(2)}) collective-permute-start(bf16[176,128]{1,0:T(8,128)(2,1)} %get-tuple-element.10), channel_id=1, source_target_pairs={{0,16},{16,32},{32,48},{48,64},{64,80},{80,96},{96,112},{1,17},{17... | collective-permute-start | bytes 135176 | tf_op jit(solution)/shard_map/ppermute | solution.py:168
  32.2 1.4 %collective-permute-done.1.recv_ref = bf16[176,128]{1,0:T(8,128)(2,1)S(1)} collective-permute-done((bf16[176,128]{1,0:T(8,128)(2,1)}, bf16[176,128]{1,0:T(8,128)(2,1)S(1)}, u32[]{:S(2)}, u32[]{:S(2)}) %collective-permute-start.1) | collective-permute-done | bytes 45088 | tf_op jit(solution)/shard_map/ppermute | solution.py:168
  33.6 0.0 copy-start.1
  33.7 0.8 add_convert_fusion
  34.5 0.0 copy-done.1
  34.5 0.7 broadcast_in_dim.4
  35.1 16.7 %all-to-all-start.1 = ((bf16[4,96,128]{2,1,0:T(8,128)(2,1)}), bf16[4,96,128]{2,1,0:T(8,128)(2,1)S(1)}, u32[]{:S(2)}, u32[]{:S(2)}) async-start(bf16[4,96,128]{2,1,0:T(8,128)(2,1)} %broadcast_in_dim.4), calls=%async_computation.1 | async-start | bytes 196608 | tf_op jit(solution)/shard_map/all_to_all | solution.py:171
  51.8 0.8 dynamic_slice.3
  52.6 5.7 %shard_map.57 = (f32[16,64,128]{2,1,0:T(8,128)}, f32[16,64,128]{2,1,0:T(8,128)}, bf16[160,2048]{1,0:T(8,128)(2,1)}) custom-call(s32[1]{0:T(128)} %bitcast.1.first_ref, bf16[16,96,128]{2,1,0:T(8,128)(2,1)} %all_to_all.15.x_ref, bf16[176,128]{1,0:T(8,128)(2,1)} %copy-done.1), custom_call_target="tpu_custom_call" | custom-call | tf_op jit(solution)/shard_map/pallas_call | solution.py:140
  58.3 5.5 %all-to-all-done.1.others_ref = bf16[4,96,128]{2,1,0:T(8,128)(2,1)S(1)} async-done(((bf16[4,96,128]{2,1,0:T(8,128)(2,1)}), bf16[4,96,128]{2,1,0:T(8,128)(2,1)S(1)}, u32[]{:S(2)}, u32[]{:S(2)}) %all-to-all-start.1) | async-done | bytes 98336 | tf_op jit(solution)/shard_map/all_to_all | solution.py:171
  63.8 0.0 copy-start
  63.8 0.7 broadcast_in_dim.5.gain_ref
  64.5 0.0 copy-done
  64.5 2.6 %shard_map.58 = bf16[16,64,128]{2,1,0:T(8,128)(2,1)} custom-call(s32[1]{0:T(128)} %bitcast.quad_ref, bf16[176,128]{1,0:T(8,128)(2,1)} %copy-done.1, bf16[4,96,128]{2,1,0:T(8,128)(2,1)} %copy-done, f32[16,64,128]{2,1,0:T(8,128)} %get-tuple-element.12.num_ref, f32[16,64,128]{2,1,0:T(8,128)} %get-tuple-element.13.win_ref, ...), custom_call_target="tpu_custom_call" | custom-call | tf_op jit(solution)/shard_map/pallas_call | solution.py:140
  67.1 14.6 %all_to_all.16.x_ref = bf16[16,64,128]{2,1,0:T(8,128)(2,1)} all-to-all(bf16[16,64,128]{2,1,0:T(8,128)(2,1)} %shard_map.58), channel_id=1, replica_groups=mesh['dp'=4,'quad'=4,'half'=2,'pair'=2,'core'=2,'inner'=4] {'pair','core..., dimensions={0} | all-to-all | bytes 524288 | tf_op jit(solution)/shard_map/all_to_all | solution.py:189
  81.8 1.8 %shard_map.59 = bf16[128,1024]{1,0:T(8,128)(2,1)} custom-call(bf16[16,64,128]{2,1,0:T(8,128)(2,1)} %all_to_all.16.x_ref), custom_call_target="tpu_custom_call" | custom-call | tf_op jit(solution)/shard_map/pallas_call | solution.py:140
Async XLA Ops:
  0.7 7.0 %collective-permute-start = (bf16[2,1024]{1,0:T(2,128)(2,1)S(1)}, bf16[2,1024]{1,0:T(2,128)(2,1)S(1)}, u32[]{:S(2)}, u32[]{:S(2)}) collective-permute-start(bf16[2,1024]{1,0:T(2,128)(2,1)S(1)} %slice.6), channel_id=1, source_target_pairs={{0,1},{1,2},{2,3},{3,4},{4,5},{5,6},{6,7},{7,8},{8,9},{9,10},{10,1... | collective-permute-start | bytes 12296 | tf_op jit(solution)/shard_map/ppermute | solution.py:153
  7.8 0.6 copy-start.2
  28.2 5.5 %collective-permute-start.1 = (bf16[176,128]{1,0:T(8,128)(2,1)}, bf16[176,128]{1,0:T(8,128)(2,1)S(1)}, u32[]{:S(2)}, u32[]{:S(2)}) collective-permute-start(bf16[176,128]{1,0:T(8,128)(2,1)} %get-tuple-element.10), channel_id=1, source_target_pairs={{0,16},{16,32},{32,48},{48,64},{64,80},{80,96},{96,112},{1,17},{17... | collective-permute-start | bytes 135176 | tf_op jit(solution)/shard_map/ppermute | solution.py:168
  33.6 0.8 copy-start.1
  35.1 28.7 %all-to-all-start.1 = ((bf16[4,96,128]{2,1,0:T(8,128)(2,1)}), bf16[4,96,128]{2,1,0:T(8,128)(2,1)S(1)}, u32[]{:S(2)}, u32[]{:S(2)}) async-start(bf16[4,96,128]{2,1,0:T(8,128)(2,1)} %broadcast_in_dim.4), calls=%async_computation.1 | async-start | bytes 196608 | tf_op jit(solution)/shard_map/all_to_all | solution.py:171
  63.8 0.7 copy-start

commit v2 on v1

v2 whole, which is shorter than its diff:
```python
import jax
import jax.numpy as jnp
import numpy as np
from jax import lax
from jax.experimental import pallas as pl
from jax.experimental.pallas import tpu as pltpu
from jax.sharding import Mesh, PartitionSpec as P

HEADS = 16
FEAT = 16
VDIM = 64
TAPS = 3
WIN = 64
BLK = 128
NPHI = 160
LANES = 128
EDGE = NPHI - LANES
HALF = VDIM // 2
STATE_ROWS = VDIM + HALF
PART = FEAT + FEAT + VDIM
F32 = jnp.float32
BF16 = jnp.bfloat16


def nt(lhs, rhs):
    return lax.dot_general(lhs, rhs, (((1,), (1,)), ((), ())), preferred_element_type=F32)


def tn(lhs, rhs):
    return lax.dot_general(lhs, rhs, (((0,), (0,)), ((), ())), preferred_element_type=F32)


def nn(lhs, rhs):
    return lax.dot_general(lhs, rhs, (((1,), (0,)), ((), ())), preferred_element_type=F32)


def lanes(rows):
    return lax.broadcasted_iota(jnp.int32, (rows, LANES), 1)


def features(entries, weighted):
    lin, diag, off = (0.25, 1.0 / 32.0, 1.0 / 16.0) if weighted else (1.0, 1.0, 1.0)
    rows = [entries * lin if weighted else entries]
    base = entries * off if weighted else entries
    rows.append(entries * entries * diag if weighted else entries * entries)
    for step in range(1, FEAT // 2):
        rolled = jnp.concatenate([entries[step:], entries[:step]], axis=0)
        rows.append(base * rolled)
    rows.append(base[: FEAT // 2] * entries[FEAT // 2 :])
    tail = lax.broadcasted_iota(jnp.int32, (8, entries.shape[1]), 0)
    rows.append(jnp.where(tail == 0, 1.0, 0.0).astype(F32))
    return jnp.concatenate(rows, axis=0).astype(BF16)


def convolve(taps, raw, before):
    lane = lanes(VDIM)
    one = jnp.where(lane < 1, pltpu.roll(before, 1, 1), pltpu.roll(raw, 1, 1))
    two = jnp.where(lane < 2, pltpu.roll(before, 2, 1), pltpu.roll(raw, 2, 1))
    return (taps[0] * raw + taps[1] * one + taps[2] * two).astype(BF16)


def fold(main, rest):
    both = rest[:HALF] + pltpu.roll(rest[HALF:], LANES // 2, 1)
    return jnp.concatenate([main, both], axis=0).astype(BF16)


def unfold(packed):
    wide = packed.astype(F32)
    both = wide[VDIM:STATE_ROWS]
    low = lanes(HALF) < LANES // 2
    upper = jnp.where(low, both, 0.0)
    lower = jnp.where(low, pltpu.roll(both, LANES // 2, 1), 0.0)
    return wide[:VDIM], jnp.concatenate([upper, lower], axis=0)


def edge_state(taps, key_rest, tail_rest):
    lane = lanes(VDIM)
    same = pltpu.roll(tail_rest, LANES - EDGE, 1)
    last = pltpu.roll(tail_rest, LANES - EDGE - 1, 1)
    first = jnp.where(lane == 0, taps[1] * last + taps[2] * same, 0.0)
    missing = jnp.where(lane == 1, taps[2] * same, first).astype(BF16)
    keys = pltpu.roll(key_rest[:FEAT], LANES - EDGE - 2, 1)
    keys = jnp.where(lanes(FEAT) < 2, keys, 0.0)
    state = nt(missing, features(keys, True))
    blank = jnp.zeros((VDIM, LANES - EDGE), F32)
    return state[:, :LANES], jnp.concatenate([state[:, LANES:], blank], axis=1)


def joined(rest, tail_rest, key_rest):
    lane = lanes(VDIM)
    return jnp.where(lane < EDGE, rest, jnp.where(lane < EDGE + 2, tail_rest, key_rest))


def pack_kernel(head_ref, q_ref, k_ref, v_ref, w_ref, gain_ref, out_ref, taps_ref):
    out_ref[:, 0:FEAT, :] = q_ref[...].T.reshape(HEADS, FEAT, BLK)
    out_ref[:, FEAT : 2 * FEAT, :] = k_ref[...].T.reshape(HEADS, FEAT, BLK)
    out_ref[:, 2 * FEAT :, :] = v_ref[...].T.reshape(HEADS, VDIM, BLK)
    rows = jnp.concatenate([w_ref[...], gain_ref[...], jnp.zeros((4, HEADS * VDIM), F32)], axis=0)
    mine = jnp.zeros((8, VDIM), F32)
    for head in range(HEADS):
        mine = jnp.where(head_ref[0] == head, rows[:, head * VDIM : (head + 1) * VDIM], mine)
    columns = mine.T
    for index in range(TAPS + 1):
        taps_ref[index] = jnp.broadcast_to(columns[:, index : index + 1], (VDIM, LANES))


def state_kernel(x_ref, taps_ref, sent_ref, own_ref, conv_ref):
    count = x_ref.shape[0]
    taps = [taps_ref[index] for index in range(TAPS)]
    total = jnp.zeros((VDIM, NPHI), F32)
    before = jnp.zeros((VDIM, BLK), F32)
    for blk in range(count):
        raw = x_ref[blk, 2 * FEAT :, :].astype(F32)
        conv = convolve(taps, raw, before)
        conv_ref[blk] = conv
        phi = features(x_ref[blk, FEAT : 2 * FEAT, :].astype(F32), True)
        total = total + nt(conv, phi)
        before = raw
    lane = lanes(VDIM)
    blank = jnp.zeros((VDIM, LANES - EDGE), F32)
    rest = jnp.concatenate([total[:, LANES:], blank], axis=1)
    tail = pltpu.roll(before, EDGE + 2, 1)
    first = x_ref[0, FEAT : 2 * FEAT, :].astype(F32)
    first = jnp.concatenate([first, jnp.zeros((VDIM - FEAT, BLK), F32)], axis=0)
    first = jnp.where(lane < EDGE + 4, pltpu.roll(first, EDGE + 2, 1), 0.0)
    rest = joined(rest, tail, first)
    main = total[:, :LANES]
    own_ref[0] = main
    own_ref[1] = rest
    sent_ref[0:STATE_ROWS, :] = fold(main, rest)
    sent_ref[STATE_ROWS:, :] = x_ref[count - 1, FEAT:, :]


def merge_one_kernel(own_ref, recv_ref, taps_ref, sent_ref, pair_ref):
    main, rest = own_ref[0], own_ref[1]
    recv_main, recv_rest = unfold(recv_ref[0:STATE_ROWS, :])
    edge_main, edge_rest = edge_state(taps_ref, rest, recv_rest)
    main = main + recv_main + edge_main
    rest = joined(rest + recv_rest + edge_rest, rest, recv_rest)
    pair_ref[0] = main
    pair_ref[1] = rest
    sent_ref[...] = fold(main, rest)


def merge_two_kernel(pair_ref, near_ref, recv_ref, taps_ref, sent_ref, carried_ref):
    main, rest = pair_ref[0], pair_ref[1]
    recv_main, recv_rest = unfold(recv_ref[...])
    edge_main, edge_rest = edge_state(taps_ref, rest, recv_rest)
    far_main, far_rest = recv_main + edge_main, recv_rest + edge_rest
    near_main, near_rest = unfold(near_ref[0:STATE_ROWS, :])
    carried_ref[0] = near_main + far_main
    carried_ref[1] = joined(near_rest + far_rest, recv_rest, recv_rest)
    sent_ref[...] = fold(main + far_main, joined(rest + far_rest, rest, recv_rest))


def local_kernel(
    first_ref, x_ref, conv_ref, halo_ref, taps_ref, carried_ref, num_ref, win_ref, phi_ref
):
    count = x_ref.shape[0]
    taps = [taps_ref[index] for index in range(TAPS)]
    key_row = lax.broadcasted_iota(jnp.int32, (BLK, BLK), 0)
    query_lane = lax.broadcasted_iota(jnp.int32, (BLK, BLK), 1)
    causal = key_row <= query_lane
    span = WIN + BLK
    near_row = lax.broadcasted_iota(jnp.int32, (span, BLK), 0)
    near_lane = lax.broadcasted_iota(jnp.int32, (span, BLK), 1)
    inside = (near_row >= near_lane) & (near_row <= near_lane + WIN)
    inside_first = inside & ((near_row >= WIN) | (first_ref[0] == 0))
    before_key = halo_ref[STATE_ROWS : STATE_ROWS + FEAT, :]
    before_raw = halo_ref[STATE_ROWS + FEAT :, :].astype(F32)
    before_val = convolve(taps, before_raw, jnp.zeros((VDIM, BLK), F32))
    first_val = convolve(taps, x_ref[0, 2 * FEAT :, :].astype(F32), before_raw)
    state = jnp.concatenate([carried_ref[0], carried_ref[1][:, :EDGE]], axis=1)
    blank = jnp.zeros((BLK - WIN, BLK), BF16)
    for blk in range(count):
        query = x_ref[blk, 0:FEAT, :]
        key = x_ref[blk, FEAT : 2 * FEAT, :]
        value = first_val if blk == 0 else conv_ref[blk]
        phi_query = features(query.astype(F32), False)
        phi_ref[:, blk * BLK : (blk + 1) * BLK] = phi_query
        scores = tn(jnp.concatenate([before_key, key], axis=1), query) * 0.25
        own = scores[BLK:]
        weights = jnp.where(causal, 1.0 + own + 0.5 * own * own, 0.0).astype(BF16)
        num_ref[blk] = nn(value, weights) + nn(state.astype(BF16), phi_query)
        masked = jnp.where(inside_first if blk == 0 else inside, scores[BLK - WIN :], -1e30)
        row_max = jnp.max(masked, axis=0, keepdims=True)
        exp_scores = jnp.exp(masked - row_max)
        row_sum = jnp.sum(exp_scores, axis=0, keepdims=True)
        probs = jnp.concatenate([blank, exp_scores.astype(BF16)], axis=0)
        win = nn(jnp.concatenate([before_val, value], axis=1), probs)
        win_ref[blk] = win / row_sum
        if blk + 1 < count:
            state = state + nt(value, features(key.astype(F32), True))
        before_key, before_val = key, value


def final_kernel(carried_ref, recv_ref, taps_ref, num_ref, win_ref, phi_ref, out_ref):
    recv_main, recv_rest = unfold(recv_ref[...])
    edge_main, edge_rest = edge_state(taps_ref, carried_ref[1], recv_rest)
    rest = (recv_rest + edge_rest)[:, :EDGE]
    state = jnp.concatenate([recv_main + edge_main, rest], axis=1).astype(BF16)
    gain = taps_ref[TAPS]
    for blk in range(num_ref.shape[0]):
        num = num_ref[blk] + nn(state, phi_ref[:, blk * BLK : (blk + 1) * BLK])
        mean_square = jnp.sum(num * num, axis=0, keepdims=True) * (1.0 / VDIM)
        linear = num * lax.rsqrt(mean_square + 1e-06) * gain
        out_ref[blk] = (linear + win_ref[blk]).astype(BF16)


def unpack_kernel(x_ref, out_ref):
    out_ref[...] = x_ref[...].reshape(HEADS * VDIM, BLK).T


SMEM = pl.BlockSpec(memory_space=pltpu.SMEM)
VMEM = pl.BlockSpec(memory_space=pltpu.VMEM)


def call(kernel, outs, scalars, outer_arrays, arrays):
    arrays = [pltpu.with_memory_space_constraint(array, pltpu.VMEM) for array in arrays]
    count = len(outer_arrays) + len(arrays)
    single = len(outs) == 1
    return pl.pallas_call(
        kernel,
        out_shape=outs[0] if single else tuple(outs),
        in_specs=[SMEM] * len(scalars) + [VMEM] * count,
        out_specs=VMEM if single else tuple(VMEM for _ in outs),
    )(*scalars, *outer_arrays, *arrays)


def scalar(value):
    return jnp.asarray(value).astype(jnp.int32).reshape(1)


def on_device(query_rows, key_rows, value_rows, conv_weight, norm_gain):
    group = ("pair", "core", "inner")
    stack = ("quad", "half")
    members = lax.axis_size(group)
    groups = lax.axis_size(stack)
    tokens = members * BLK

    def upward(value, step):
        return lax.ppermute(value, stack, [(i, i + step) for i in range(groups - step)])

    packed, taps = call(
        pack_kernel,
        [pltpu.VMEM((HEADS, PART, BLK), BF16), pltpu.VMEM((TAPS + 1, VDIM, LANES), F32)],
        [scalar(lax.axis_index(group))],
        [query_rows, key_rows, value_rows, conv_weight, norm_gain.reshape(1, HEADS * VDIM)],
        [],
    )
    mine = lax.all_to_all(packed, group, 0, 0)
    sent, own, conv = call(
        state_kernel,
        [
            pltpu.VMEM((STATE_ROWS + FEAT + VDIM, BLK), BF16),
            pltpu.VMEM((2, VDIM, LANES), F32),
            pltpu.VMEM((members, VDIM, BLK), BF16),
        ],
        [],
        [],
        [mine, taps],
    )
    near = upward(sent, 1)
    state_shapes = [pltpu.VMEM((STATE_ROWS, LANES), BF16), pltpu.VMEM((2, VDIM, LANES), F32)]
    sent, pair = call(merge_one_kernel, state_shapes, [], [], [own, near, taps])
    far = upward(sent, 2)
    sent, carried = call(merge_two_kernel, state_shapes, [], [], [pair, near, far, taps])
    farthest = upward(sent, 4)
    num, win, phi = call(
        local_kernel,
        [
            pltpu.VMEM((members, VDIM, BLK), F32),
            pltpu.VMEM((members, VDIM, BLK), F32),
            pltpu.VMEM((NPHI, tokens), BF16),
        ],
        [scalar(lax.axis_index(stack) == 0)],
        [],
        [mine, conv, near, taps, carried],
    )
    done = call(
        final_kernel,
        [pltpu.VMEM((members, VDIM, BLK), BF16)],
        [],
        [],
        [carried, farthest, taps, num, win, phi],
    )
    heads = lax.all_to_all(done, group, 0, 0)
    out = jax.ShapeDtypeStruct((BLK, HEADS * VDIM), BF16)
    return call(unpack_kernel, [out], [], [], [heads])


def solution(mesh):
    outer, inner = mesh.shape["outer"], mesh.shape["inner"]
    pair = HEADS // inner // 2
    shape = (mesh.shape["dp"], outer // (2 * 2 * pair), 2, pair, 2, inner)
    split = Mesh(
        np.asarray(mesh.devices).reshape(shape), ("dp", "quad", "half", "pair", "core", "inner")
    )
    rows = P(("dp", "quad", "half", "pair", "core", "inner"), None)
    return jax.shard_map(
        on_device,
        mesh=split,
        in_specs=(rows, rows, rows, P(), P()),
        out_specs=rows,
        check_vma=False,
    )
```

time: 84.3 us -> 74.5 us (0.88)
  waiting for transfers between devices: 10 us -> 2.05 us
  Pallas kernels: 14.5 us -> 8.66 us
  blocking collectives: 30.1 us -> 32.3 us
  local copies, waits for them, and re-layouts: 3.42 us -> 5.6 us
    ppermute x2 -> x3, starting transfers between devices: 7.99 us -> 25.5 us  [upward(): lax.ppermute(value, stack, [(i, i + step) for i in range(groups - step)])]
    all_to_all x1 -> x0, starting transfers between devices: 16.7 us -> none  [on_device(): lax.all_to_all(jnp.broadcast_to(two[None], (quads, STATE_ROWS, BLK)), 'qu...]
    pallas_call x5 -> x7, Pallas kernels: 14.5 us -> 8.66 us  [call(): pl.pallas_call(kernel, out_shape=outs[0] if single else tuple(outs), in_s...]
    all_to_all x1 -> x0, waiting for transfers between devices: 5.5 us -> none  [on_device(): lax.all_to_all(jnp.broadcast_to(two[None], (quads, STATE_ROWS, BLK)), 'qu...]
    unnamed x6 -> x12, local copies, waits for them, and re-layouts: 0.6 us -> 5.6 us
    all_to_all x1, blocking collectives: 15.4 us -> 18.3 us  [on_device(): mine = lax.all_to_all(packed, group, 0, 0)]
    ppermute x2 -> x3, waiting for transfers between devices: 4.54 us -> 2.05 us  [upward(): lax.ppermute(value, stack, [(i, i + step) for i in range(groups - step)])]
    broadcast_in_dim x2 -> x0, local copies, waits for them, and re-layouts: 1.34 us -> none  [the longest x1 0.69 us: on_device(): gain = jnp.broadcast_to(gain[:, None], (VDIM, BLK))]
  transfers between devices with their start and end apart: 3 -> 3, of which waited for: 3 -> 2; matrix products, arithmetic and copies ran while one was open for 1% -> 0% of each run, Pallas kernels for 7% -> 5%
where the time goes in v2:
time: 74.5 us; the launch traced here: 74.1 us
  blocking collectives  32.3 us (43%)
  starting transfers between devices  25.5 us (34%)
  Pallas kernels  8.66 us (12%)
  local copies, waits for them, and re-layouts  5.6 us (8%)
  waiting for transfers between devices  2.05 us (3%)
    ppermute x3, starting transfers between devices, upward(): lax.ppermute(value, stack, [(i, i + step) for i in range(groups - step)])  25.5 us
    all_to_all x1, blocking collectives, on_device(): mine = lax.all_to_all(packed, group, 0, 0)  18.3 us
    all_to_all x1, blocking collectives, on_device(): heads = lax.all_to_all(done, group, 0, 0)  14 us
    pallas_call x7, Pallas kernels, call(): pl.pallas_call(kernel, out_shape=outs[0] if single else tuple(outs), in_s...  8.66 us
    unnamed x12, local copies, waits for them, and re-layouts  5.6 us
    ppermute x3, waiting for transfers between devices, upward(): lax.ppermute(value, stack, [(i, i + step) for i in range(groups - step)])  2.05 us
  transfers between devices with their start and end apart: 3, of which 2 were waited for; matrix products, arithmetic and copies ran while one was open for 0% of the time, Pallas kernels for 5%

profile of v2, /device:TPU:1, one launch (start us, length us, event | category | flops | bytes accessed | tf_op | source)
XLA Modules:
  0.0 74.1 jit_solution(5689163934156746089)
XLA Ops:
  0.0 2.3 %shard_map.55 = (bf16[16,96,128]{2,1,0:T(8,128)(2,1)S(1)}, f32[4,64,128]{2,1,0:T(8,128)S(1)}) custom-call(s32[1]{0:T(128)} %bitcast.head_ref, bf16[128,256]{1,0:T(8,128)(2,1)} %q_ref.1, bf16[128,256]{1,0:T(8,128)(2,1)} %k_ref.1, bf16[128,1024]{1,0:T(8,128)(2,1)} %v_ref.1, f32[3,1024]{1,0:T(4,128)} %w_ref.1, f32[1,1024]{1,0:T(1,128)} %bitcast.3), custom_call_target="tpu_custom_call" | custom-call | tf_op jit(solution)/shard_map/pallas_call | solution.py:222
  2.3 18.3 %all_to_all.10.x_ref = bf16[16,96,128]{2,1,0:T(8,128)(2,1)S(1)} all-to-all(bf16[16,96,128]{2,1,0:T(8,128)(2,1)S(1)} %get-tuple-element.17), channel_id=1, replica_groups=mesh['dp'=4,'quad'=4,'half'=2,'pair'=2,'core'=2,'inner'=4] {'pair','core..., dimensions={0} | all-to-all | bytes 786432 | tf_op jit(solution)/shard_map/all_to_all | solution.py:251
  20.6 0.7 shard_map.56
  21.3 2.5 %collective-permute-start = (bf16[176,128]{1,0:T(8,128)(2,1)S(1)}, bf16[176,128]{1,0:T(8,128)(2,1)S(1)}, u32[]{:S(2)}, u32[]{:S(2)}) collective-permute-start(bf16[176,128]{1,0:T(8,128)(2,1)S(1)} %get-tuple-element.20), channel_id=1, source_target_pairs={{0,16},{16,32},{32,48},{48,64},{64,80},{80,96},{96,112},{1,17},{17... | collective-permute-start | bytes 135176 | tf_op jit(solution)/shard_map/ppermute | solution.py:242
  23.8 1.1 %collective-permute-done.recv_ref.near_ref.halo_ref = bf16[176,128]{1,0:T(8,128)(2,1)S(1)} collective-permute-done((bf16[176,128]{1,0:T(8,128)(2,1)S(1)}, bf16[176,128]{1,0:T(8,128)(2,1)S(1)}, u32[]{:S(2)}, u32[]{:S(2)}) %collective-permute-start) | collective-permute-done | bytes 45088 | tf_op jit(solution)/shard_map/ppermute | solution.py:242
  24.9 0.3 shard_map.57
  25.2 9.7 %collective-permute-start.1 = (bf16[96,128]{1,0:T(8,128)(2,1)S(1)}, bf16[96,128]{1,0:T(8,128)(2,1)S(1)}, u32[]{:S(2)}, u32[]{:S(2)}) collective-permute-start(bf16[96,128]{1,0:T(8,128)(2,1)S(1)} %get-tuple-element.22), channel_id=1, source_target_pairs={{0,32},{16,48},{32,64},{48,80},{64,96},{80,112},{1,33},{17,49},{33... | collective-permute-start | bytes 73736 | tf_op jit(solution)/shard_map/ppermute | solution.py:242
  35.0 0.9 %collective-permute-done.1.recv_ref = bf16[96,128]{1,0:T(8,128)(2,1)S(1)} collective-permute-done((bf16[96,128]{1,0:T(8,128)(2,1)S(1)}, bf16[96,128]{1,0:T(8,128)(2,1)S(1)}, u32[]{:S(2)}, u32[]{:S(2)}) %collective-permute-start.1) | collective-permute-done | bytes 24608 | tf_op jit(solution)/shard_map/ppermute | solution.py:242
  35.9 0.3 shard_map.58
  36.2 13.3 %collective-permute-start.2 = (bf16[96,128]{1,0:T(8,128)(2,1)S(1)}, bf16[96,128]{1,0:T(8,128)(2,1)S(1)}, u32[]{:S(2)}, u32[]{:S(2)}) collective-permute-start(bf16[96,128]{1,0:T(8,128)(2,1)S(1)} %get-tuple-element.24), channel_id=1, source_target_pairs={{0,64},{16,80},{32,96},{48,112},{1,65},{17,81},{33,97},{49,113},{2... | collective-permute-start | bytes 73736 | tf_op jit(solution)/shard_map/ppermute | solution.py:242
  49.5 3.5 %shard_map.59 = (f32[16,64,128]{2,1,0:T(8,128)S(1)}, f32[16,64,128]{2,1,0:T(8,128)S(1)}, bf16[160,2048]{1,0:T(8,128)(2,1)S(1)}) custom-call(s32[1]{0:T(128)} %bitcast.2.first_ref, bf16[16,96,128]{2,1,0:T(8,128)(2,1)S(1)} %all_to_all.10.x_ref, bf16[16,64,128]{2,1,0:T(8,128)(2,1)S(1)} %get-tuple-element.25.conv_ref, ...), custom_call_target="tpu_custom_call" | custom-call | tf_op jit(solution)/shard_map/pallas_call | solution.py:222
  53.1 0.0 copy-start
  53.1 0.8 %copy-done = bf16[160,2048]{1,0:T(8,128)(2,1)} copy-done((bf16[160,2048]{1,0:T(8,128)(2,1)}, bf16[160,2048]{1,0:T(8,128)(2,1)S(1)}, u32[]{:S(2)}) %copy-start) | copy-done | bytes 655384
  53.9 0.0 copy-start.2
  53.9 0.8 %copy-done.2 = f32[16,64,128]{2,1,0:T(8,128)} copy-done((f32[16,64,128]{2,1,0:T(8,128)}, f32[16,64,128]{2,1,0:T(8,128)S(1)}, u32[]{:S(2)}) %copy-start.2) | copy-done | bytes 524312
  54.7 0.0 copy-start.4
  54.7 0.8 %copy-done.4 = f32[16,64,128]{2,1,0:T(8,128)} copy-done((f32[16,64,128]{2,1,0:T(8,128)}, f32[16,64,128]{2,1,0:T(8,128)S(1)}, u32[]{:S(2)}) %copy-start.4) | copy-done | bytes 524312
  55.5 0.0 collective-permute-done.2.recv_ref
  55.5 0.0 copy-start.1
  55.5 1.1 %copy-done.1 = bf16[160,2048]{1,0:T(8,128)(2,1)S(1)} copy-done((bf16[160,2048]{1,0:T(8,128)(2,1)S(1)}, bf16[160,2048]{1,0:T(8,128)(2,1)}, u32[]{:S(2)}) %copy-start.1) | copy-done | bytes 655384
  56.6 0.0 copy-start.3
  56.6 1.0 %copy-done.3 = f32[16,64,128]{2,1,0:T(8,128)S(1)} copy-done((f32[16,64,128]{2,1,0:T(8,128)S(1)}, f32[16,64,128]{2,1,0:T(8,128)}, u32[]{:S(2)}) %copy-start.3) | copy-done | bytes 524312
  57.7 0.0 copy-start.5
  57.7 1.0 %copy-done.5 = f32[16,64,128]{2,1,0:T(8,128)S(1)} copy-done((f32[16,64,128]{2,1,0:T(8,128)S(1)}, f32[16,64,128]{2,1,0:T(8,128)}, u32[]{:S(2)}) %copy-start.5) | copy-done | bytes 524312
  58.7 0.6 shard_map.60
  59.3 14.0 %all_to_all.11.x_ref = bf16[16,64,128]{2,1,0:T(8,128)(2,1)S(1)} all-to-all(bf16[16,64,128]{2,1,0:T(8,128)(2,1)S(1)} %shard_map.60), channel_id=1, replica_groups=mesh['dp'=4,'quad'=4,'half'=2,'pair'=2,'core'=2,'inner'=4] {'pair','core..., dimensions={0} | all-to-all | bytes 524288 | tf_op jit(solution)/shard_map/all_to_all | solution.py:287
  73.3 0.8 %shard_map.61 = bf16[128,1024]{1,0:T(8,128)(2,1)} custom-call(bf16[16,64,128]{2,1,0:T(8,128)(2,1)S(1)} %all_to_all.11.x_ref), custom_call_target="tpu_custom_call" | custom-call | tf_op jit(solution)/shard_map/pallas_call | solution.py:222
Async XLA Ops:
  21.3 3.6 %collective-permute-start = (bf16[176,128]{1,0:T(8,128)(2,1)S(1)}, bf16[176,128]{1,0:T(8,128)(2,1)S(1)}, u32[]{:S(2)}, u32[]{:S(2)}) collective-permute-start(bf16[176,128]{1,0:T(8,128)(2,1)S(1)} %get-tuple-element.20), channel_id=1, source_target_pairs={{0,16},{16,32},{32,48},{48,64},{64,80},{80,96},{96,112},{1,17},{17... | collective-permute-start | bytes 135176 | tf_op jit(solution)/shard_map/ppermute | solution.py:242
  25.2 10.7 %collective-permute-start.1 = (bf16[96,128]{1,0:T(8,128)(2,1)S(1)}, bf16[96,128]{1,0:T(8,128)(2,1)S(1)}, u32[]{:S(2)}, u32[]{:S(2)}) collective-permute-start(bf16[96,128]{1,0:T(8,128)(2,1)S(1)} %get-tuple-element.22), channel_id=1, source_target_pairs={{0,32},{16,48},{32,64},{48,80},{64,96},{80,112},{1,33},{17,49},{33... | collective-permute-start | bytes 73736 | tf_op jit(solution)/shard_map/ppermute | solution.py:242
  36.2 19.3 %collective-permute-start.2 = (bf16[96,128]{1,0:T(8,128)(2,1)S(1)}, bf16[96,128]{1,0:T(8,128)(2,1)S(1)}, u32[]{:S(2)}, u32[]{:S(2)}) collective-permute-start(bf16[96,128]{1,0:T(8,128)(2,1)S(1)} %get-tuple-element.24), channel_id=1, source_target_pairs={{0,64},{16,80},{32,96},{48,112},{1,65},{17,81},{33,97},{49,113},{2... | collective-permute-start | bytes 73736 | tf_op jit(solution)/shard_map/ppermute | solution.py:242
  53.1 0.9 %copy-start = (bf16[160,2048]{1,0:T(8,128)(2,1)}, bf16[160,2048]{1,0:T(8,128)(2,1)S(1)}, u32[]{:S(2)}) copy-start(bf16[160,2048]{1,0:T(8,128)(2,1)S(1)} %get-tuple-element.28.phi_ref) | copy-start | bytes 1966084
  53.9 0.8 %copy-start.2 = (f32[16,64,128]{2,1,0:T(8,128)}, f32[16,64,128]{2,1,0:T(8,128)S(1)}, u32[]{:S(2)}) copy-start(f32[16,64,128]{2,1,0:T(8,128)S(1)} %get-tuple-element.26.num_ref) | copy-start | bytes 1572868
  54.7 0.8 %copy-start.4 = (f32[16,64,128]{2,1,0:T(8,128)}, f32[16,64,128]{2,1,0:T(8,128)S(1)}, u32[]{:S(2)}) copy-start(f32[16,64,128]{2,1,0:T(8,128)S(1)} %get-tuple-element.27.win_ref) | copy-start | bytes 1572868
  55.5 1.1 %copy-start.1 = (bf16[160,2048]{1,0:T(8,128)(2,1)S(1)}, bf16[160,2048]{1,0:T(8,128)(2,1)}, u32[]{:S(2)}) copy-start(bf16[160,2048]{1,0:T(8,128)(2,1)} %copy-done) | copy-start | bytes 1966084
  56.6 1.0 %copy-start.3 = (f32[16,64,128]{2,1,0:T(8,128)S(1)}, f32[16,64,128]{2,1,0:T(8,128)}, u32[]{:S(2)}) copy-start(f32[16,64,128]{2,1,0:T(8,128)} %copy-done.2) | copy-start | bytes 1572868
  57.7 1.0 %copy-start.5 = (f32[16,64,128]{2,1,0:T(8,128)S(1)}, f32[16,64,128]{2,1,0:T(8,128)}, u32[]{:S(2)}) copy-start(f32[16,64,128]{2,1,0:T(8,128)} %copy-done.4) | copy-start | bytes 1572868

commit v3 on v2

--- a/solution.py
+++ b/solution.py
@@ -224,6 +224,7 @@
         out_shape=outs[0] if single else tuple(outs),
         in_specs=[SMEM] * len(scalars) + [VMEM] * count,
         out_specs=VMEM if single else tuple(VMEM for _ in outs),
+        compiler_params=pltpu.CompilerParams(vmem_limit_bytes=8 * 1024 * 1024),
     )(*scalars, *outer_arrays, *arrays)
 
 

time: 74.5 us -> 71.2 us (0.956)
  local copies, waits for them, and re-layouts: 5.6 us -> 3.35 us
  Pallas kernels: 8.66 us -> 7.61 us
    unnamed x12 -> x10, local copies, waits for them, and re-layouts: 5.6 us -> 3.35 us
    pallas_call x7, Pallas kernels: 8.66 us -> 7.61 us  [call(): pl.pallas_call(kernel, out_shape=outs[0] if single else tuple(outs), in_s...]
where the time goes in v3:
time: 71.2 us; the launch traced here: 70.8 us
  blocking collectives  32.3 us (45%)
  starting transfers between devices  25.5 us (36%)
  Pallas kernels  7.61 us (11%)
  local copies, waits for them, and re-layouts  3.35 us (5%)
  waiting for transfers between devices  2.05 us (3%)
    ppermute x3, starting transfers between devices, upward(): lax.ppermute(value, stack, [(i, i + step) for i in range(groups - step)])  25.5 us
    all_to_all x1, blocking collectives, on_device(): mine = lax.all_to_all(packed, group, 0, 0)  18.3 us
    all_to_all x1, blocking collectives, on_device(): heads = lax.all_to_all(done, group, 0, 0)  14 us
    pallas_call x7, Pallas kernels, call(): pl.pallas_call(kernel, out_shape=outs[0] if single else tuple(outs), in_s...  7.61 us
    unnamed x10, local copies, waits for them, and re-layouts  3.35 us
    ppermute x3, waiting for transfers between devices, upward(): lax.ppermute(value, stack, [(i, i + step) for i in range(groups - step)])  2.05 us
  transfers between devices with their start and end apart: 3, of which 2 were waited for; matrix products, arithmetic and copies ran while one was open for 0% of the time, Pallas kernels for 5%

profile of v3, /device:TPU:1, one launch (start us, length us, event | category | flops | bytes accessed | tf_op | source)
XLA Modules:
  0.0 70.8 jit_solution(16511157766539116779)
XLA Ops:
  0.0 0.0 copy-start.3
  0.0 0.0 copy-start.4
  0.0 0.7 %copy-done.3 = f32[3,1024]{1,0:T(4,128)S(1)} copy-done((f32[3,1024]{1,0:T(4,128)S(1)}, f32[3,1024]{1,0:T(4,128)}, u32[]{:S(2)}) %copy-start.3) | copy-done | bytes 12312
  0.7 0.0 copy-done.4
  0.7 0.0 copy-start
  0.7 0.9 %copy-done = bf16[128,1024]{1,0:T(8,128)(2,1)S(1)} copy-done((bf16[128,1024]{1,0:T(8,128)(2,1)S(1)}, bf16[128,1024]{1,0:T(8,128)(2,1)}, u32[]{:S(2)}) %copy-start) | copy-done | bytes 262168
  1.7 0.0 copy-start.1
  1.7 0.8 %copy-done.1 = bf16[128,256]{1,0:T(8,128)(2,1)S(1)} copy-done((bf16[128,256]{1,0:T(8,128)(2,1)S(1)}, bf16[128,256]{1,0:T(8,128)(2,1)}, u32[]{:S(2)}) %copy-start.1) | copy-done | bytes 65560
  2.5 0.0 copy-start.2
  2.5 0.8 %copy-done.2 = bf16[128,256]{1,0:T(8,128)(2,1)S(1)} copy-done((bf16[128,256]{1,0:T(8,128)(2,1)S(1)}, bf16[128,256]{1,0:T(8,128)(2,1)}, u32[]{:S(2)}) %copy-start.2) | copy-done | bytes 65560
  3.4 1.3 %shard_map.55 = (bf16[16,96,128]{2,1,0:T(8,128)(2,1)S(1)}, f32[4,64,128]{2,1,0:T(8,128)S(1)}) custom-call(s32[1]{0:T(128)} %bitcast.head_ref, bf16[128,256]{1,0:T(8,128)(2,1)S(1)} %copy-done.1, bf16[128,256]{1,0:T(8,128)(2,1)S(1)} %copy-done.2, bf16[128,1024]{1,0:T(8,128)(2,1)S(1)} %copy-done, f32[3,1024]{1,0:T(4,128)S(1)} %copy-done.3, f32[1,1024]{1,0:T(1,128)S(1)} %bitcast.3), custom_call_target="tpu_custom_call" | custom-call | tf_op jit(solution)/shard_map/pallas_call | solution.py:222
  4.6 18.3 %all_to_all.10.x_ref = bf16[16,96,128]{2,1,0:T(8,128)(2,1)S(1)} all-to-all(bf16[16,96,128]{2,1,0:T(8,128)(2,1)S(1)} %get-tuple-element.17), channel_id=1, replica_groups=mesh['dp'=4,'quad'=4,'half'=2,'pair'=2,'core'=2,'inner'=4] {'pair','core..., dimensions={0} | all-to-all | bytes 786432 | tf_op jit(solution)/shard_map/all_to_all | solution.py:252
  22.9 0.7 %shard_map.56 = (bf16[176,128]{1,0:T(8,128)(2,1)S(1)}, f32[2,64,128]{2,1,0:T(8,128)S(1)}, bf16[16,64,128]{2,1,0:T(8,128)(2,1)S(1)}) custom-call(bf16[16,96,128]{2,1,0:T(8,128)(2,1)S(1)} %all_to_all.10.x_ref, f32[4,64,128]{2,1,0:T(8,128)S(1)} %get-tuple-element.18.taps_ref), custom_call_target="tpu_custom_call" | custom-call | tf_op jit(solution)/shard_map/pallas_call | solution.py:222
  23.6 2.5 %collective-permute-start = (bf16[176,128]{1,0:T(8,128)(2,1)S(1)}, bf16[176,128]{1,0:T(8,128)(2,1)S(1)}, u32[]{:S(2)}, u32[]{:S(2)}) collective-permute-start(bf16[176,128]{1,0:T(8,128)(2,1)S(1)} %get-tuple-element.20), channel_id=1, source_target_pairs={{0,16},{16,32},{32,48},{48,64},{64,80},{80,96},{96,112},{1,17},{17... | collective-permute-start | bytes 135176 | tf_op jit(solution)/shard_map/ppermute | solution.py:243
  26.1 1.1 %collective-permute-done.recv_ref.near_ref.halo_ref = bf16[176,128]{1,0:T(8,128)(2,1)S(1)} collective-permute-done((bf16[176,128]{1,0:T(8,128)(2,1)S(1)}, bf16[176,128]{1,0:T(8,128)(2,1)S(1)}, u32[]{:S(2)}, u32[]{:S(2)}) %collective-permute-start) | collective-permute-done | bytes 45088 | tf_op jit(solution)/shard_map/ppermute | solution.py:243
  27.2 0.3 shard_map.57
  27.5 9.7 %collective-permute-start.1 = (bf16[96,128]{1,0:T(8,128)(2,1)S(1)}, bf16[96,128]{1,0:T(8,128)(2,1)S(1)}, u32[]{:S(2)}, u32[]{:S(2)}) collective-permute-start(bf16[96,128]{1,0:T(8,128)(2,1)S(1)} %get-tuple-element.22), channel_id=1, source_target_pairs={{0,32},{16,48},{32,64},{48,80},{64,96},{80,112},{1,33},{17,49},{33... | collective-permute-start | bytes 73736 | tf_op jit(solution)/shard_map/ppermute | solution.py:243
  37.3 0.9 %collective-permute-done.1.recv_ref = bf16[96,128]{1,0:T(8,128)(2,1)S(1)} collective-permute-done((bf16[96,128]{1,0:T(8,128)(2,1)S(1)}, bf16[96,128]{1,0:T(8,128)(2,1)S(1)}, u32[]{:S(2)}, u32[]{:S(2)}) %collective-permute-start.1) | collective-permute-done | bytes 24608 | tf_op jit(solution)/shard_map/ppermute | solution.py:243
  38.2 0.3 shard_map.58
  38.5 13.3 %collective-permute-start.2 = (bf16[96,128]{1,0:T(8,128)(2,1)S(1)}, bf16[96,128]{1,0:T(8,128)(2,1)S(1)}, u32[]{:S(2)}, u32[]{:S(2)}) collective-permute-start(bf16[96,128]{1,0:T(8,128)(2,1)S(1)} %get-tuple-element.24), channel_id=1, source_target_pairs={{0,64},{16,80},{32,96},{48,112},{1,65},{17,81},{33,97},{49,113},{2... | collective-permute-start | bytes 73736 | tf_op jit(solution)/shard_map/ppermute | solution.py:243
  51.8 3.5 %shard_map.59 = (f32[16,64,128]{2,1,0:T(8,128)S(1)}, f32[16,64,128]{2,1,0:T(8,128)S(1)}, bf16[160,2048]{1,0:T(8,128)(2,1)S(1)}) custom-call(s32[1]{0:T(128)} %bitcast.2.first_ref, bf16[16,96,128]{2,1,0:T(8,128)(2,1)S(1)} %all_to_all.10.x_ref, bf16[16,64,128]{2,1,0:T(8,128)(2,1)S(1)} %get-tuple-element.25.conv_ref, ...), custom_call_target="tpu_custom_call" | custom-call | tf_op jit(solution)/shard_map/pallas_call | solution.py:222
  55.4 0.0 collective-permute-done.2.recv_ref
  55.4 0.6 shard_map.60
  56.0 14.0 %all_to_all.11.x_ref = bf16[16,64,128]{2,1,0:T(8,128)(2,1)S(1)} all-to-all(bf16[16,64,128]{2,1,0:T(8,128)(2,1)S(1)} %shard_map.60), channel_id=1, replica_groups=mesh['dp'=4,'quad'=4,'half'=2,'pair'=2,'core'=2,'inner'=4] {'pair','core..., dimensions={0} | all-to-all | bytes 524288 | tf_op jit(solution)/shard_map/all_to_all | solution.py:288
  70.0 0.8 %shard_map.61 = bf16[128,1024]{1,0:T(8,128)(2,1)} custom-call(bf16[16,64,128]{2,1,0:T(8,128)(2,1)S(1)} %all_to_all.11.x_ref), custom_call_target="tpu_custom_call" | custom-call | tf_op jit(solution)/shard_map/pallas_call | solution.py:222
Async XLA Ops:
  0.0 0.7 %copy-start.3 = (f32[3,1024]{1,0:T(4,128)S(1)}, f32[3,1024]{1,0:T(4,128)}, u32[]{:S(2)}) copy-start(f32[3,1024]{1,0:T(4,128)} %w_ref.1) | copy-start | bytes 36868
  0.0 0.7 %copy-start.4 = (f32[1024]{0:T(1024)S(1)}, f32[1024]{0:T(1024)}, u32[]{:S(2)}) copy-start(f32[1024]{0:T(1024)} %param.9) | copy-start | bytes 12292
  0.7 1.0 %copy-start = (bf16[128,1024]{1,0:T(8,128)(2,1)S(1)}, bf16[128,1024]{1,0:T(8,128)(2,1)}, u32[]{:S(2)}) copy-start(bf16[128,1024]{1,0:T(8,128)(2,1)} %v_ref.1) | copy-start | bytes 786436
  1.7 0.8 %copy-start.1 = (bf16[128,256]{1,0:T(8,128)(2,1)S(1)}, bf16[128,256]{1,0:T(8,128)(2,1)}, u32[]{:S(2)}) copy-start(bf16[128,256]{1,0:T(8,128)(2,1)} %q_ref.1) | copy-start | bytes 196612
  2.5 0.8 %copy-start.2 = (bf16[128,256]{1,0:T(8,128)(2,1)S(1)}, bf16[128,256]{1,0:T(8,128)(2,1)}, u32[]{:S(2)}) copy-start(bf16[128,256]{1,0:T(8,128)(2,1)} %k_ref.1) | copy-start | bytes 196612
  23.6 3.6 %collective-permute-start = (bf16[176,128]{1,0:T(8,128)(2,1)S(1)}, bf16[176,128]{1,0:T(8,128)(2,1)S(1)}, u32[]{:S(2)}, u32[]{:S(2)}) collective-permute-start(bf16[176,128]{1,0:T(8,128)(2,1)S(1)} %get-tuple-element.20), channel_id=1, source_target_pairs={{0,16},{16,32},{32,48},{48,64},{64,80},{80,96},{96,112},{1,17},{17... | collective-permute-start | bytes 135176 | tf_op jit(solution)/shard_map/ppermute | solution.py:243
  27.5 10.7 %collective-permute-start.1 = (bf16[96,128]{1,0:T(8,128)(2,1)S(1)}, bf16[96,128]{1,0:T(8,128)(2,1)S(1)}, u32[]{:S(2)}, u32[]{:S(2)}) collective-permute-start(bf16[96,128]{1,0:T(8,128)(2,1)S(1)} %get-tuple-element.22), channel_id=1, source_target_pairs={{0,32},{16,48},{32,64},{48,80},{64,96},{80,112},{1,33},{17,49},{33... | collective-permute-start | bytes 73736 | tf_op jit(solution)/shard_map/ppermute | solution.py:243
  38.5 16.9 %collective-permute-start.2 = (bf16[96,128]{1,0:T(8,128)(2,1)S(1)}, bf16[96,128]{1,0:T(8,128)(2,1)S(1)}, u32[]{:S(2)}, u32[]{:S(2)}) collective-permute-start(bf16[96,128]{1,0:T(8,128)(2,1)S(1)} %get-tuple-element.24), channel_id=1, source_target_pairs={{0,64},{16,80},{32,96},{48,112},{1,65},{17,81},{33,97},{49,113},{2... | collective-permute-start | bytes 73736 | tf_op jit(solution)/shard_map/ppermute | solution.py:243

commit v4 on v2

--- a/solution.py
+++ b/solution.py
@@ -73,15 +73,23 @@
     return wide[:VDIM], jnp.concatenate([upper, lower], axis=0)
 
 
-def edge_state(taps, key_rest, tail_rest):
+def edge_state(taps_ref, edges):
     lane = lanes(VDIM)
-    same = pltpu.roll(tail_rest, LANES - EDGE, 1)
-    last = pltpu.roll(tail_rest, LANES - EDGE - 1, 1)
-    first = jnp.where(lane == 0, taps[1] * last + taps[2] * same, 0.0)
-    missing = jnp.where(lane == 1, taps[2] * same, first).astype(BF16)
-    keys = pltpu.roll(key_rest[:FEAT], LANES - EDGE - 2, 1)
-    keys = jnp.where(lanes(FEAT) < 2, keys, 0.0)
-    state = nt(missing, features(keys, True))
+    values = jnp.zeros((VDIM, LANES), F32)
+    keys = jnp.zeros((FEAT, LANES), F32)
+    for index, (key_rest, tail_rest, counts) in enumerate(edges):
+        at = 2 * index
+        same = pltpu.roll(tail_rest, (LANES - EDGE + at) % LANES, 1)
+        last = pltpu.roll(tail_rest, (LANES - EDGE - 1 + at) % LANES, 1)
+        missing = jnp.where(lane == at, taps_ref[1] * last + taps_ref[2] * same, 0.0)
+        missing = jnp.where(lane == at + 1, taps_ref[2] * same, missing)
+        if counts is not None:
+            missing = jnp.where(counts, missing, 0.0)
+        values = values + missing
+        moved = pltpu.roll(key_rest[:FEAT], (LANES - EDGE - 2 + at) % LANES, 1)
+        place = lanes(FEAT)
+        keys = keys + jnp.where((place >= at) & (place < at + 2), moved, 0.0)
+    state = nt(values.astype(BF16), features(keys, True))
     blank = jnp.zeros((VDIM, LANES - EDGE), F32)
     return state[:, :LANES], jnp.concatenate([state[:, LANES:], blank], axis=1)
 
@@ -131,77 +139,113 @@
     sent_ref[STATE_ROWS:, :] = x_ref[count - 1, FEAT:, :]
 
 
-def merge_one_kernel(own_ref, recv_ref, taps_ref, sent_ref, pair_ref):
-    main, rest = own_ref[0], own_ref[1]
-    recv_main, recv_rest = unfold(recv_ref[0:STATE_ROWS, :])
-    edge_main, edge_rest = edge_state(taps_ref, rest, recv_rest)
-    main = main + recv_main + edge_main
-    rest = joined(rest + recv_rest + edge_rest, rest, recv_rest)
-    pair_ref[0] = main
-    pair_ref[1] = rest
-    sent_ref[...] = fold(main, rest)
-
-
-def merge_two_kernel(pair_ref, near_ref, recv_ref, taps_ref, sent_ref, carried_ref):
-    main, rest = pair_ref[0], pair_ref[1]
-    recv_main, recv_rest = unfold(recv_ref[...])
-    edge_main, edge_rest = edge_state(taps_ref, rest, recv_rest)
-    far_main, far_rest = recv_main + edge_main, recv_rest + edge_rest
-    near_main, near_rest = unfold(near_ref[0:STATE_ROWS, :])
-    carried_ref[0] = near_main + far_main
-    carried_ref[1] = joined(near_rest + far_rest, recv_rest, recv_rest)
-    sent_ref[...] = fold(main + far_main, joined(rest + far_rest, rest, recv_rest))
-
-
-def local_kernel(
-    first_ref, x_ref, conv_ref, halo_ref, taps_ref, carried_ref, num_ref, win_ref, phi_ref
-):
-    count = x_ref.shape[0]
-    taps = [taps_ref[index] for index in range(TAPS)]
+def inside_window(first):
+    row = lax.broadcasted_iota(jnp.int32, (WIN + BLK, BLK), 0)
+    lane = lax.broadcasted_iota(jnp.int32, (WIN + BLK, BLK), 1)
+    inside = (row >= lane) & (row <= lane + WIN)
+    return inside if first is None else inside & ((row >= WIN) | (first == 0))
+
+
+def block_parts(query, key, value, before_key, before_value, inside):
+    scores = tn(jnp.concatenate([before_key, key], axis=1), query) * 0.25
+    own = scores[BLK:]
     key_row = lax.broadcasted_iota(jnp.int32, (BLK, BLK), 0)
     query_lane = lax.broadcasted_iota(jnp.int32, (BLK, BLK), 1)
-    causal = key_row <= query_lane
-    span = WIN + BLK
-    near_row = lax.broadcasted_iota(jnp.int32, (span, BLK), 0)
-    near_lane = lax.broadcasted_iota(jnp.int32, (span, BLK), 1)
-    inside = (near_row >= near_lane) & (near_row <= near_lane + WIN)
-    inside_first = inside & ((near_row >= WIN) | (first_ref[0] == 0))
-    before_key = halo_ref[STATE_ROWS : STATE_ROWS + FEAT, :]
-    before_raw = halo_ref[STATE_ROWS + FEAT :, :].astype(F32)
-    before_val = convolve(taps, before_raw, jnp.zeros((VDIM, BLK), F32))
-    first_val = convolve(taps, x_ref[0, 2 * FEAT :, :].astype(F32), before_raw)
-    state = jnp.concatenate([carried_ref[0], carried_ref[1][:, :EDGE]], axis=1)
+    weights = 1.0 + own + 0.5 * own * own
+    weights = jnp.where(key_row <= query_lane, weights, 0.0).astype(BF16)
+    masked = jnp.where(inside, scores[BLK - WIN :], -1e30)
+    row_max = jnp.max(masked, axis=0, keepdims=True)
+    exp_scores = jnp.exp(masked - row_max)
+    row_sum = jnp.sum(exp_scores, axis=0, keepdims=True)
     blank = jnp.zeros((BLK - WIN, BLK), BF16)
+    probs = jnp.concatenate([blank, exp_scores.astype(BF16)], axis=0)
+    window = nn(jnp.concatenate([before_value, value], axis=1), probs)
+    return nn(value, weights), window / row_sum
+
+
+def local_kernel(x_ref, conv_ref, num_ref, win_ref, phi_ref):
+    count = x_ref.shape[0]
+    inside = inside_window(None)
+    state = jnp.zeros((VDIM, NPHI), F32)
     for blk in range(count):
         query = x_ref[blk, 0:FEAT, :]
         key = x_ref[blk, FEAT : 2 * FEAT, :]
-        value = first_val if blk == 0 else conv_ref[blk]
+        value = conv_ref[blk]
         phi_query = features(query.astype(F32), False)
         phi_ref[:, blk * BLK : (blk + 1) * BLK] = phi_query
-        scores = tn(jnp.concatenate([before_key, key], axis=1), query) * 0.25
-        own = scores[BLK:]
-        weights = jnp.where(causal, 1.0 + own + 0.5 * own * own, 0.0).astype(BF16)
-        num_ref[blk] = nn(value, weights) + nn(state.astype(BF16), phi_query)
-        masked = jnp.where(inside_first if blk == 0 else inside, scores[BLK - WIN :], -1e30)
-        row_max = jnp.max(masked, axis=0, keepdims=True)
-        exp_scores = jnp.exp(masked - row_max)
-        row_sum = jnp.sum(exp_scores, axis=0, keepdims=True)
-        probs = jnp.concatenate([blank, exp_scores.astype(BF16)], axis=0)
-        win = nn(jnp.concatenate([before_val, value], axis=1), probs)
-        win_ref[blk] = win / row_sum
+        if blk > 0:
+            own, win = block_parts(query, key, value, before_key, before_value, inside)
+            num_ref[blk] = own + nn(state.astype(BF16), phi_query)
+            win_ref[blk] = win
         if blk + 1 < count:
             state = state + nt(value, features(key.astype(F32), True))
-        before_key, before_val = key, value
-
-
-def final_kernel(carried_ref, recv_ref, taps_ref, num_ref, win_ref, phi_ref, out_ref):
-    recv_main, recv_rest = unfold(recv_ref[...])
-    edge_main, edge_rest = edge_state(taps_ref, carried_ref[1], recv_rest)
-    rest = (recv_rest + edge_rest)[:, :EDGE]
-    state = jnp.concatenate([recv_main + edge_main, rest], axis=1).astype(BF16)
+        before_key, before_value = key, value
+
+
+def merge_kernel(
+    first_ref,
+    own_ref,
+    near_ref,
+    taps_ref,
+    x_ref,
+    num_in_ref,
+    win_in_ref,
+    sent_ref,
+    edge_ref,
+    num_ref,
+    win_ref,
+):
+    main, rest = own_ref[0], own_ref[1]
+    near_main, near_rest = unfold(near_ref[0:STATE_ROWS, :])
+    edge_main, edge_rest = edge_state(taps_ref, [(rest, near_rest, None)])
+    edge_ref[0] = edge_main
+    edge_ref[1] = edge_rest
+    both = fold(main + near_main + edge_main, joined(rest + near_rest + edge_rest, rest, near_rest))
+    for quad in range(sent_ref.shape[0]):
+        sent_ref[quad] = both
+    taps = [taps_ref[index] for index in range(TAPS)]
+    raw = near_ref[STATE_ROWS + FEAT :, :].astype(F32)
+    before_value = convolve(taps, raw, jnp.zeros((VDIM, BLK), F32))
+    value = convolve(taps, x_ref[0, 2 * FEAT :, :].astype(F32), raw)
+    num_ref[0], win_ref[0] = block_parts(
+        x_ref[0, 0:FEAT, :],
+        x_ref[0, FEAT : 2 * FEAT, :],
+        value,
+        near_ref[STATE_ROWS : STATE_ROWS + FEAT, :],
+        before_value,
+        inside_window(first_ref[0]),
+    )
+
+
+def final_kernel(
+    quad_ref,
+    near_ref,
+    others_ref,
+    taps_ref,
+    edge_ref,
+    num_ref,
+    win_ref,
+    phi_ref,
+    out_ref,
+):
+    quads = others_ref.shape[0]
+    parts = [unfold(others_ref[quad]) for quad in range(quads)]
+    main, rest = unfold(near_ref[0:STATE_ROWS, :])
+    edges = []
+    for quad in range(quads - 1):
+        reached = quad < quad_ref[0]
+        main = main + jnp.where(reached, parts[quad][0], 0.0)
+        rest = rest + jnp.where(reached, parts[quad][1], 0.0)
+        edges.append((parts[quad + 1][1], parts[quad][1], reached))
+    edge_main, edge_rest = edge_state(taps_ref, edges)
+    state = jnp.concatenate([main + edge_main, (rest + edge_rest)[:, :EDGE]], axis=1)
+    group_edge = jnp.concatenate([edge_ref[0], edge_ref[1][:, :EDGE]], axis=1)
+    later = (state + group_edge).astype(BF16)
+    state = state.astype(BF16)
     gain = taps_ref[TAPS]
     for blk in range(num_ref.shape[0]):
-        num = num_ref[blk] + nn(state, phi_ref[:, blk * BLK : (blk + 1) * BLK])
+        phi = phi_ref[:, blk * BLK : (blk + 1) * BLK]
+        num = num_ref[blk] + nn(state if blk == 0 else later, phi)
         mean_square = jnp.sum(num * num, axis=0, keepdims=True) * (1.0 / VDIM)
         linear = num * lax.rsqrt(mean_square + 1e-06) * gain
         out_ref[blk] = (linear + win_ref[blk]).astype(BF16)
@@ -215,7 +259,8 @@
 VMEM = pl.BlockSpec(memory_space=pltpu.VMEM)
 
 
-def call(kernel, outs, scalars, outer_arrays, arrays):
+def call(kernel, outs, scalars, outer_arrays, arrays, aliases=None):
+    limit = None if outer_arrays else 8 * 1024 * 1024
     arrays = [pltpu.with_memory_space_constraint(array, pltpu.VMEM) for array in arrays]
     count = len(outer_arrays) + len(arrays)
     single = len(outs) == 1
@@ -224,6 +269,8 @@
         out_shape=outs[0] if single else tuple(outs),
         in_specs=[SMEM] * len(scalars) + [VMEM] * count,
         out_specs=VMEM if single else tuple(VMEM for _ in outs),
+        input_output_aliases=aliases or {},
+        compiler_params=pltpu.CompilerParams(vmem_limit_bytes=limit),
     )(*scalars, *outer_arrays, *arrays)
 
 
@@ -236,10 +283,10 @@
     stack = ("quad", "half")
     members = lax.axis_size(group)
     groups = lax.axis_size(stack)
-    tokens = members * BLK
-
-    def upward(value, step):
-        return lax.ppermute(value, stack, [(i, i + step) for i in range(groups - step)])
+    quads = lax.axis_size("quad")
+
+    def upward(value):
+        return lax.ppermute(value, stack, [(i, i + 1) for i in range(groups - 1)])
 
     packed, taps = call(
         pack_kernel,
@@ -260,29 +307,39 @@
         [],
         [mine, taps],
     )
-    near = upward(sent, 1)
-    state_shapes = [pltpu.VMEM((STATE_ROWS, LANES), BF16), pltpu.VMEM((2, VDIM, LANES), F32)]
-    sent, pair = call(merge_one_kernel, state_shapes, [], [], [own, near, taps])
-    far = upward(sent, 2)
-    sent, carried = call(merge_two_kernel, state_shapes, [], [], [pair, near, far, taps])
-    farthest = upward(sent, 4)
+    near = upward(sent)
+    block = (VDIM, BLK)
     num, win, phi = call(
         local_kernel,
         [
-            pltpu.VMEM((members, VDIM, BLK), F32),
-            pltpu.VMEM((members, VDIM, BLK), F32),
-            pltpu.VMEM((NPHI, tokens), BF16),
+            pltpu.VMEM((members, *block), F32),
+            pltpu.VMEM((members, *block), F32),
+            pltpu.VMEM((NPHI, members * BLK), BF16),
+        ],
+        [],
+        [],
+        [mine, conv],
+    )
+    sent, edge, num, win = call(
+        merge_kernel,
+        [
+            pltpu.VMEM((quads, STATE_ROWS, LANES), BF16),
+            pltpu.VMEM((2, VDIM, LANES), F32),
+            pltpu.VMEM((members, *block), F32),
+            pltpu.VMEM((members, *block), F32),
         ],
         [scalar(lax.axis_index(stack) == 0)],
         [],
-        [mine, conv, near, taps, carried],
-    )
+        [own, near, taps, mine, num, win],
+        {5: 2, 6: 3},
+    )
+    others = lax.all_to_all(sent, "quad", 0, 0)
     done = call(
         final_kernel,
-        [pltpu.VMEM((members, VDIM, BLK), BF16)],
-        [],
-        [],
-        [carried, farthest, taps, num, win, phi],
+        [pltpu.VMEM((members, *block), BF16)],
+        [scalar(lax.axis_index("quad"))],
+        [],
+        [near, others, taps, edge, num, win, phi],
     )
     heads = lax.all_to_all(done, group, 0, 0)
     out = jax.ShapeDtypeStruct((BLK, HEADS * VDIM), BF16)

time: 74.5 us -> 68.4 us (0.918)
  blocking collectives: 32.3 us -> 57.7 us
  starting transfers between devices: 25.5 us -> 2.48 us
  local copies, waits for them, and re-layouts: 5.6 us -> 0 us
  waiting for transfers between devices: 2.05 us -> 0.01 us
    all_to_all x0 -> x1, blocking collectives: none -> 25 us  [on_device(): others = lax.all_to_all(sent, 'quad', 0, 0)]
    ppermute x3 -> x1, starting transfers between devices: 25.5 us -> 2.48 us  [upward(): return lax.ppermute(value, stack, [(i, i + 1) for i in range(groups - 1)])]
    unnamed x12 -> x0, local copies, waits for them, and re-layouts: 5.6 us -> none
    ppermute x3 -> x1, waiting for transfers between devices: 2.05 us -> 0.01 us  [upward(): return lax.ppermute(value, stack, [(i, i + 1) for i in range(groups - 1)])]
    pallas_call x7 -> x6, Pallas kernels: 8.66 us -> 7.96 us  [call(): pl.pallas_call(kernel, out_shape=outs[0] if single else tuple(outs), in_s...]
  transfers between devices with their start and end apart: 3 -> 1, of which waited for: 2 -> 0; matrix products, arithmetic and copies ran while one was open for 0% -> 0% of each run, Pallas kernels for 5% -> 5%
where the time goes in v4:
time: 68.4 us; the launch traced here: 68.2 us
  blocking collectives  57.7 us (84%)
  Pallas kernels  7.96 us (12%)
  starting transfers between devices  2.48 us (4%)
    all_to_all x1, blocking collectives, on_device(): others = lax.all_to_all(sent, 'quad', 0, 0)  25 us
    all_to_all x1, blocking collectives, on_device(): mine = lax.all_to_all(packed, group, 0, 0)  18.3 us
    all_to_all x1, blocking collectives, on_device(): heads = lax.all_to_all(done, group, 0, 0)  14.4 us
    pallas_call x6, Pallas kernels, call(): pl.pallas_call(kernel, out_shape=outs[0] if single else tuple(outs), in_s...  7.96 us
    ppermute x1, starting transfers between devices, upward(): return lax.ppermute(value, stack, [(i, i + 1) for i in range(groups - 1)])  2.48 us
  transfers between devices with their start and end apart: 1, of which 0 were waited for; matrix products, arithmetic and copies ran while one was open for 0% of the time, Pallas kernels for 5%

profile of v4, /device:TPU:1, one launch (start us, length us, event | category | flops | bytes accessed | tf_op | source)
XLA Modules:
  0.0 68.2 jit_solution(16222510381666658985)
XLA Ops:
  0.0 2.3 %shard_map.55 = (bf16[16,96,128]{2,1,0:T(8,128)(2,1)S(1)}, f32[4,64,128]{2,1,0:T(8,128)S(1)}) custom-call(s32[1]{0:T(128)} %bitcast.1.head_ref, bf16[128,256]{1,0:T(8,128)(2,1)} %q_ref.1, bf16[128,256]{1,0:T(8,128)(2,1)} %k_ref.1, bf16[128,1024]{1,0:T(8,128)(2,1)} %v_ref.1, f32[3,1024]{1,0:T(4,128)} %w_ref.1, f32[1,1024]{1,0:T(1,128)} %bitcast.4), custom_call_target="tpu_custom_call" | custom-call | tf_op jit(solution)/shard_map/pallas_call | solution.py:267
  2.3 18.3 %all_to_all.15.x_ref = bf16[16,96,128]{2,1,0:T(8,128)(2,1)S(1)} all-to-all(bf16[16,96,128]{2,1,0:T(8,128)(2,1)S(1)} %get-tuple-element.17), channel_id=1, replica_groups=mesh['dp'=4,'quad'=4,'half'=2,'pair'=2,'core'=2,'inner'=4] {'pair','core..., dimensions={0} | all-to-all | bytes 786432 | tf_op jit(solution)/shard_map/all_to_all | solution.py:298
  20.6 0.7 %shard_map.56 = (bf16[176,128]{1,0:T(8,128)(2,1)S(1)}, f32[2,64,128]{2,1,0:T(8,128)S(1)}, bf16[16,64,128]{2,1,0:T(8,128)(2,1)S(1)}) custom-call(bf16[16,96,128]{2,1,0:T(8,128)(2,1)S(1)} %all_to_all.15.x_ref, f32[4,64,128]{2,1,0:T(8,128)S(1)} %get-tuple-element.18.taps_ref), custom_call_target="tpu_custom_call" | custom-call | tf_op jit(solution)/shard_map/pallas_call | solution.py:267
  21.3 2.5 %collective-permute-start = (bf16[176,128]{1,0:T(8,128)(2,1)S(1)}, bf16[176,128]{1,0:T(8,128)(2,1)S(1)}, u32[]{:S(2)}, u32[]{:S(2)}) collective-permute-start(bf16[176,128]{1,0:T(8,128)(2,1)S(1)} %get-tuple-element.19), channel_id=1, source_target_pairs={{0,16},{16,32},{32,48},{48,64},{64,80},{80,96},{96,112},{1,17},{17... | collective-permute-start | bytes 135176 | tf_op jit(solution)/shard_map/ppermute | solution.py:289
  23.8 3.1 %shard_map.57 = (f32[16,64,128]{2,1,0:T(8,128)S(1)}, f32[16,64,128]{2,1,0:T(8,128)S(1)}, bf16[160,2048]{1,0:T(8,128)(2,1)S(1)}) custom-call(bf16[16,96,128]{2,1,0:T(8,128)(2,1)S(1)} %all_to_all.15.x_ref, bf16[16,64,128]{2,1,0:T(8,128)(2,1)S(1)} %get-tuple-element.21.conv_ref), custom_call_target="tpu_custom_call" | custom-call | tf_op jit(solution)/shard_map/pallas_call | solution.py:267
  26.9 0.0 collective-permute-done.near_ref
  26.9 0.4 shard_map.58
  27.3 25.0 %all_to_all.16.others_ref = bf16[4,96,128]{2,1,0:T(8,128)(2,1)S(1)} all-to-all(bf16[4,96,128]{2,1,0:T(8,128)(2,1)S(1)} %get-tuple-element.24), channel_id=1, replica_groups=mesh['dp'=4,'quad'=4,'half'=2,'pair'=2,'core'=2,'inner'=4] {'quad'}, dimensions={0} | all-to-all | bytes 196608 | tf_op jit(solution)/shard_map/all_to_all | solution.py:336
  52.3 0.6 shard_map.59
  52.9 14.4 %all_to_all.17.x_ref = bf16[16,64,128]{2,1,0:T(8,128)(2,1)S(1)} all-to-all(bf16[16,64,128]{2,1,0:T(8,128)(2,1)S(1)} %shard_map.59), channel_id=1, replica_groups=mesh['dp'=4,'quad'=4,'half'=2,'pair'=2,'core'=2,'inner'=4] {'pair','core..., dimensions={0} | all-to-all | bytes 524288 | tf_op jit(solution)/shard_map/all_to_all | solution.py:344
  67.3 0.8 %shard_map.60 = bf16[128,1024]{1,0:T(8,128)(2,1)} custom-call(bf16[16,64,128]{2,1,0:T(8,128)(2,1)S(1)} %all_to_all.17.x_ref), custom_call_target="tpu_custom_call" | custom-call | tf_op jit(solution)/shard_map/pallas_call | solution.py:267
Async XLA Ops:
  21.3 5.6 %collective-permute-start = (bf16[176,128]{1,0:T(8,128)(2,1)S(1)}, bf16[176,128]{1,0:T(8,128)(2,1)S(1)}, u32[]{:S(2)}, u32[]{:S(2)}) collective-permute-start(bf16[176,128]{1,0:T(8,128)(2,1)S(1)} %get-tuple-element.19), channel_id=1, source_target_pairs={{0,16},{16,32},{32,48},{48,64},{64,80},{80,96},{96,112},{1,17},{17... | collective-permute-start | bytes 135176 | tf_op jit(solution)/shard_map/ppermute | solution.py:289

commit v5 on v4

--- a/solution.py
+++ b/solution.py
@@ -217,17 +217,7 @@
     )
 
 
-def final_kernel(
-    quad_ref,
-    near_ref,
-    others_ref,
-    taps_ref,
-    edge_ref,
-    num_ref,
-    win_ref,
-    phi_ref,
-    out_ref,
-):
+def late_kernel(quad_ref, others_ref, near_ref, taps_ref, *refs):
     quads = others_ref.shape[0]
     parts = [unfold(others_ref[quad]) for quad in range(quads)]
     main, rest = unfold(near_ref[0:STATE_ROWS, :])
@@ -238,7 +228,16 @@
         rest = rest + jnp.where(reached, parts[quad][1], 0.0)
         edges.append((parts[quad + 1][1], parts[quad][1], reached))
     edge_main, edge_rest = edge_state(taps_ref, edges)
-    state = jnp.concatenate([main + edge_main, (rest + edge_rest)[:, :EDGE]], axis=1)
+    finish(main + edge_main, rest + edge_rest, taps_ref, *refs)
+
+
+def early_kernel(near_ref, taps_ref, *refs):
+    main, rest = unfold(near_ref[0:STATE_ROWS, :])
+    finish(main, rest, taps_ref, *refs)
+
+
+def finish(main, rest, taps_ref, edge_ref, num_ref, win_ref, phi_ref, out_ref):
+    state = jnp.concatenate([main, rest[:, :EDGE]], axis=1)
     group_edge = jnp.concatenate([edge_ref[0], edge_ref[1][:, :EDGE]], axis=1)
     later = (state + group_edge).astype(BF16)
     state = state.astype(BF16)
@@ -333,17 +332,27 @@
         [own, near, taps, mine, num, win],
         {5: 2, 6: 3},
     )
+    quad = lax.axis_index("quad")
+    parts = [near, taps, edge, num, win, phi]
+
+    def returned(kernel, scalars, arrays):
+        done = call(kernel, [pltpu.VMEM((members, *block), BF16)], scalars, [], arrays)
+        heads = lax.all_to_all(done, group, 0, 0)
+        return call(unpack_kernel, [jax.ShapeDtypeStruct((BLK, HEADS * VDIM), BF16)], [], [], [heads])
+
+    def early(sent):
+        return sent, returned(early_kernel, [], parts)
+
+    def nothing(sent):
+        return sent, jnp.zeros((BLK, HEADS * VDIM), BF16)
+
+    sent, out = lax.cond(quad == 0, early, nothing, sent)
     others = lax.all_to_all(sent, "quad", 0, 0)
-    done = call(
-        final_kernel,
-        [pltpu.VMEM((members, *block), BF16)],
-        [scalar(lax.axis_index("quad"))],
-        [],
-        [near, others, taps, edge, num, win, phi],
-    )
-    heads = lax.all_to_all(done, group, 0, 0)
-    out = jax.ShapeDtypeStruct((BLK, HEADS * VDIM), BF16)
-    return call(unpack_kernel, [out], [], [], [heads])
+
+    def late(out):
+        return returned(late_kernel, [scalar(quad)], [others, *parts])
+
+    return lax.cond(quad == 0, lambda out: out, late, out)
 
 
 def solution(mesh):

time: 68.4 us -> 61 us (0.89)
  the two profiles are of different devices: /device:TPU:1 before, /device:TPU:209 now
where the time goes in v5:
time: 61 us; the launch traced here: 60.7 us
  blocking collectives  47.5 us (78%)
  Pallas kernels  7.26 us (12%)
  starting transfers between devices  5.2 us (9%)
  local copies, waits for them, and re-layouts  0.72 us (1%)
    all_to_all x1, blocking collectives, on_device(): others = lax.all_to_all(sent, 'quad', 0, 0)  20.1 us
    all_to_all x1, blocking collectives, on_device(): mine = lax.all_to_all(packed, group, 0, 0)  15 us
    all_to_all x1, blocking collectives, returned(): heads = lax.all_to_all(done, group, 0, 0)  12.3 us
    pallas_call x6, Pallas kernels, call(): pl.pallas_call(kernel, out_shape=outs[0] if single else tuple(outs), in_s...  7.26 us
    ppermute x1, starting transfers between devices, upward(): return lax.ppermute(value, stack, [(i, i + 1) for i in range(groups - 1)])  5.2 us
  transfers between devices with their start and end apart: 1, of which 0 were waited for; matrix products, arithmetic and copies ran while one was open for 0% of the time, Pallas kernels for 5%

profile of v5, /device:TPU:209, one launch (start us, length us, event | category | flops | bytes accessed | tf_op | source)
XLA Modules:
  0.0 60.7 jit_solution(8333243727820326758)
XLA Ops:
  0.0 2.3 %shard_map.57 = (bf16[16,96,128]{2,1,0:T(8,128)(2,1)S(1)}, f32[4,64,128]{2,1,0:T(8,128)S(1)}) custom-call(s32[1]{0:T(128)} %bitcast.2.head_ref, bf16[128,256]{1,0:T(8,128)(2,1)} %q_ref.1, bf16[128,256]{1,0:T(8,128)(2,1)} %k_ref.1, bf16[128,1024]{1,0:T(8,128)(2,1)} %v_ref.1, f32[3,1024]{1,0:T(4,128)} %w_ref.1, f32[1,1024]{1,0:T(1,128)} %bitcast.4), custom_call_target="tpu_custom_call" | custom-call | tf_op jit(solution)/shard_map/pallas_call | solution.py:266
  2.3 15.0 %all_to_all.20.x_ref = bf16[16,96,128]{2,1,0:T(8,128)(2,1)S(1)} all-to-all(bf16[16,96,128]{2,1,0:T(8,128)(2,1)S(1)} %get-tuple-element.66), channel_id=1, replica_groups=mesh['dp'=4,'quad'=4,'half'=2,'pair'=2,'core'=2,'inner'=4] {'pair','core..., dimensions={0} | all-to-all | bytes 786432 | tf_op jit(solution)/shard_map/all_to_all | solution.py:297
  17.3 0.7 %shard_map.58 = (bf16[176,128]{1,0:T(8,128)(2,1)S(1)}, f32[2,64,128]{2,1,0:T(8,128)S(1)}, bf16[16,64,128]{2,1,0:T(8,128)(2,1)S(1)}) custom-call(bf16[16,96,128]{2,1,0:T(8,128)(2,1)S(1)} %all_to_all.20.x_ref, f32[4,64,128]{2,1,0:T(8,128)S(1)} %get-tuple-element.67.taps_ref), custom_call_target="tpu_custom_call" | custom-call | tf_op jit(solution)/shard_map/pallas_call | solution.py:266
  18.0 5.2 %collective-permute-start = (bf16[176,128]{1,0:T(8,128)(2,1)S(1)}, bf16[176,128]{1,0:T(8,128)(2,1)S(1)}, u32[]{:S(2)}, u32[]{:S(2)}) collective-permute-start(bf16[176,128]{1,0:T(8,128)(2,1)S(1)} %get-tuple-element.69), channel_id=1, source_target_pairs={{0,16},{16,32},{32,48},{48,64},{64,80},{80,96},{96,112},{1,17},{17... | collective-permute-start | bytes 135176 | tf_op jit(solution)/shard_map/ppermute | solution.py:288
  23.3 3.1 %shard_map.59 = (f32[16,64,128]{2,1,0:T(8,128)S(1)}, f32[16,64,128]{2,1,0:T(8,128)S(1)}, bf16[160,2048]{1,0:T(8,128)(2,1)S(1)}) custom-call(bf16[16,96,128]{2,1,0:T(8,128)(2,1)S(1)} %all_to_all.20.x_ref, bf16[16,64,128]{2,1,0:T(8,128)(2,1)S(1)} %get-tuple-element.70.conv_ref), custom_call_target="tpu_custom_call" | custom-call | tf_op jit(solution)/shard_map/pallas_call | solution.py:266
  26.4 0.0 collective-permute-done.near_ref
  26.4 0.4 shard_map.60
  26.9 20.1 %all_to_all.21 = bf16[4,96,128]{2,1,0:T(8,128)(2,1)S(1)} all-to-all(bf16[4,96,128]{2,1,0:T(8,128)(2,1)S(1)} %get-tuple-element.73), channel_id=1, replica_groups=mesh['dp'=4,'quad'=4,'half'=2,'pair'=2,'core'=2,'inner'=4] {'quad'}, dimensions={0} | all-to-all | bytes 196608 | tf_op jit(solution)/shard_map/all_to_all | solution.py:350
  47.0 13.1 %conditional.3 = (bf16[128,1024]{1,0:T(8,128)(2,1)S(1)}) conditional(s32[]{:T(128)} %convert_element_type.2, (s32[]{:T(128)}, bf16[4,96,128]{2,1,0:T(8,128)(2,1)S(1)}, bf16[176,128]{1,0:T(8,128)(2,1)S(1)}, f32[4,64,128]{2,1,0:T(8,128)S(1)}, f32[2,64,128]{2,1,0:T(8,128)S(1)}, /*index=5*/f32[16,64,128]{2,1,0:T(8,128)S(1)}, ...), branch_computations={%region_2.0_spmd, %region_3.0_spmd} | conditional | bytes 524296 | solution.py:355
  47.0 0.6 branch_0_fun.2
  47.6 12.3 %all_to_all.19.x_ref = bf16[16,64,128]{2,1,0:T(8,128)(2,1)S(1)} all-to-all(bf16[16,64,128]{2,1,0:T(8,128)(2,1)S(1)} %branch_0_fun.2), channel_id=1, replica_groups=mesh['dp'=4,'quad'=4,'half'=2,'pair'=2,'core'=2,'inner'=4] {'pair','core..., dimensions={0} | all-to-all | bytes 524288 | tf_op jit(solution)/shard_map/cond/branch_0_fun/all_to_all | solution.py:340
  59.9 0.1 branch_0_fun.3
  60.0 0.0 copy-start
  60.1 0.7 %copy-done = bf16[128,1024]{1,0:T(8,128)(2,1)} copy-done((bf16[128,1024]{1,0:T(8,128)(2,1)}, bf16[128,1024]{1,0:T(8,128)(2,1)S(1)}, u32[]{:S(2)}) %copy-start) | copy-done | bytes 262168
  (2 shorter events, 0.1 us)
Async XLA Ops:
  18.0 8.4 %collective-permute-start = (bf16[176,128]{1,0:T(8,128)(2,1)S(1)}, bf16[176,128]{1,0:T(8,128)(2,1)S(1)}, u32[]{:S(2)}, u32[]{:S(2)}) collective-permute-start(bf16[176,128]{1,0:T(8,128)(2,1)S(1)} %get-tuple-element.69), channel_id=1, source_target_pairs={{0,16},{16,32},{32,48},{48,64},{64,80},{80,96},{96,112},{1,17},{17... | collective-permute-start | bytes 135176 | tf_op jit(solution)/shard_map/ppermute | solution.py:288
  60.0 0.7 %copy-start = (bf16[128,1024]{1,0:T(8,128)(2,1)}, bf16[128,1024]{1,0:T(8,128)(2,1)S(1)}, u32[]{:S(2)}) copy-start(bf16[128,1024]{1,0:T(8,128)(2,1)S(1)} %get-tuple-element.84) | copy-start | bytes 786436

commit v6 on v5

--- a/solution.py
+++ b/solution.py
@@ -77,14 +77,12 @@
     lane = lanes(VDIM)
     values = jnp.zeros((VDIM, LANES), F32)
     keys = jnp.zeros((FEAT, LANES), F32)
-    for index, (key_rest, tail_rest, counts) in enumerate(edges):
+    for index, (key_rest, tail_rest) in enumerate(edges):
         at = 2 * index
         same = pltpu.roll(tail_rest, (LANES - EDGE + at) % LANES, 1)
         last = pltpu.roll(tail_rest, (LANES - EDGE - 1 + at) % LANES, 1)
         missing = jnp.where(lane == at, taps_ref[1] * last + taps_ref[2] * same, 0.0)
         missing = jnp.where(lane == at + 1, taps_ref[2] * same, missing)
-        if counts is not None:
-            missing = jnp.where(counts, missing, 0.0)
         values = values + missing
         moved = pltpu.roll(key_rest[:FEAT], (LANES - EDGE - 2 + at) % LANES, 1)
         place = lanes(FEAT)
@@ -191,18 +189,21 @@
     num_in_ref,
     win_in_ref,
     sent_ref,
+    pair_ref,
     edge_ref,
     num_ref,
     win_ref,
 ):
     main, rest = own_ref[0], own_ref[1]
     near_main, near_rest = unfold(near_ref[0:STATE_ROWS, :])
-    edge_main, edge_rest = edge_state(taps_ref, [(rest, near_rest, None)])
+    edge_main, edge_rest = edge_state(taps_ref, [(rest, near_rest)])
     edge_ref[0] = edge_main
     edge_ref[1] = edge_rest
-    both = fold(main + near_main + edge_main, joined(rest + near_rest + edge_rest, rest, near_rest))
-    for quad in range(sent_ref.shape[0]):
-        sent_ref[quad] = both
+    main = main + near_main + edge_main
+    rest = joined(rest + near_rest + edge_rest, rest, near_rest)
+    pair_ref[0] = main
+    pair_ref[1] = rest
+    sent_ref[...] = fold(main, rest)
     taps = [taps_ref[index] for index in range(TAPS)]
     raw = near_ref[STATE_ROWS + FEAT :, :].astype(F32)
     before_value = convolve(taps, raw, jnp.zeros((VDIM, BLK), F32))
@@ -217,18 +218,30 @@
     )
 
 
-def late_kernel(quad_ref, others_ref, near_ref, taps_ref, *refs):
-    quads = others_ref.shape[0]
-    parts = [unfold(others_ref[quad]) for quad in range(quads)]
-    main, rest = unfold(near_ref[0:STATE_ROWS, :])
-    edges = []
-    for quad in range(quads - 1):
-        reached = quad < quad_ref[0]
-        main = main + jnp.where(reached, parts[quad][0], 0.0)
-        rest = rest + jnp.where(reached, parts[quad][1], 0.0)
-        edges.append((parts[quad + 1][1], parts[quad][1], reached))
-    edge_main, edge_rest = edge_state(taps_ref, edges)
-    finish(main + edge_main, rest + edge_rest, taps_ref, *refs)
+def join_kernel(quad_ref, pair_ref, recv_ref, taps_ref, sent_ref):
+    lowest = quad_ref[0] == 0
+    main, rest = pair_ref[0], pair_ref[1]
+    recv_main, recv_rest = unfold(recv_ref[...])
+    lower = jnp.where(lowest, rest, recv_rest)
+    upper = jnp.where(lowest, recv_rest, rest)
+    edge_main, edge_rest = edge_state(taps_ref, [(upper, lower)])
+    sent_ref[...] = fold(
+        main + recv_main + edge_main, joined(rest + recv_rest + edge_rest, upper, lower)
+    )
+
+
+def late_kernel(quad_ref, pair_recv_ref, below_ref, low_ref, near_ref, taps_ref, *refs):
+    second = quad_ref[0] == 1
+    near_main, near_rest = unfold(near_ref[0:STATE_ROWS, :])
+    one_main, one_rest = unfold(pair_recv_ref[...])
+    two_main, two_rest = unfold(below_ref[...])
+    below_main = jnp.where(second, one_main, two_main)
+    below_rest = jnp.where(second, one_rest, two_rest)
+    low_main, low_rest = unfold(low_ref[...])
+    above_low = jnp.where(quad_ref[0] == 2, near_rest, below_rest)
+    edge_main, edge_rest = edge_state(taps_ref, [(near_rest, below_rest), (above_low, low_rest)])
+    main = near_main + below_main + low_main + edge_main
+    finish(main, near_rest + below_rest + low_rest + edge_rest, taps_ref, *refs)
 
 
 def early_kernel(near_ref, taps_ref, *refs):
@@ -282,7 +295,6 @@
     stack = ("quad", "half")
     members = lax.axis_size(group)
     groups = lax.axis_size(stack)
-    quads = lax.axis_size("quad")
 
     def upward(value):
         return lax.ppermute(value, stack, [(i, i + 1) for i in range(groups - 1)])
@@ -319,10 +331,11 @@
         [],
         [mine, conv],
     )
-    sent, edge, num, win = call(
+    sent, pair, edge, num, win = call(
         merge_kernel,
         [
-            pltpu.VMEM((quads, STATE_ROWS, LANES), BF16),
+            pltpu.VMEM((STATE_ROWS, LANES), BF16),
+            pltpu.VMEM((2, VDIM, LANES), F32),
             pltpu.VMEM((2, VDIM, LANES), F32),
             pltpu.VMEM((members, *block), F32),
             pltpu.VMEM((members, *block), F32),
@@ -330,29 +343,44 @@
         [scalar(lax.axis_index(stack) == 0)],
         [],
         [own, near, taps, mine, num, win],
-        {5: 2, 6: 3},
+        {5: 3, 6: 4},
     )
     quad = lax.axis_index("quad")
     parts = [near, taps, edge, num, win, phi]
 
     def returned(kernel, scalars, arrays):
         done = call(kernel, [pltpu.VMEM((members, *block), BF16)], scalars, [], arrays)
-        heads = lax.all_to_all(done, group, 0, 0)
-        return call(unpack_kernel, [jax.ShapeDtypeStruct((BLK, HEADS * VDIM), BF16)], [], [], [heads])
-
-    def early(sent):
-        return sent, returned(early_kernel, [], parts)
-
-    def nothing(sent):
-        return sent, jnp.zeros((BLK, HEADS * VDIM), BF16)
-
-    sent, out = lax.cond(quad == 0, early, nothing, sent)
-    others = lax.all_to_all(sent, "quad", 0, 0)
-
-    def late(out):
-        return returned(late_kernel, [scalar(quad)], [others, *parts])
-
-    return lax.cond(quad == 0, lambda out: out, late, out)
+        return lax.all_to_all(done, group, 0, 0)
+
+    heads = lax.cond(
+        quad == 0,
+        lambda: returned(early_kernel, [], parts),
+        lambda: jnp.zeros((HEADS, *block), BF16),
+    )
+    below = lax.ppermute(sent, "quad", [(2, 3)])
+
+    def lower_pair(sent):
+        recv = lax.ppermute(sent, "quad", [(0, 1), (1, 0)])
+        both = call(
+            join_kernel,
+            [pltpu.VMEM((STATE_ROWS, LANES), BF16)],
+            [scalar(quad)],
+            [],
+            [pair, recv, taps],
+        )
+        return both, recv
+
+    ready, heads = lax.optimization_barrier((sent, heads))
+    both, pair_recv = lax.cond(quad < 2, lower_pair, lambda sent: (sent, sent), ready)
+    low = lax.ppermute(both, "quad", [(0, 2), (1, 3)])
+    heads = lax.cond(
+        quad == 0,
+        lambda heads: heads,
+        lambda heads: returned(late_kernel, [scalar(quad)], [pair_recv, below, low, *parts]),
+        heads,
+    )
+    out = jax.ShapeDtypeStruct((BLK, HEADS * VDIM), BF16)
+    return call(unpack_kernel, [out], [], [], [heads])
 
 
 def solution(mesh):

time: 61 us -> 65.2 us (1.069)
  the two profiles are of different devices: /device:TPU:209 before, /device:TPU:345 now
where the time goes in v6:
time: 65.2 us; the launch traced here: 64.9 us
  blocking collectives  26.8 us (41%)
  waiting for transfers between devices  20.8 us (32%)
  Pallas kernels  8.7 us (13%)
  starting transfers between devices  7.81 us (12%)
    ppermute x1, waiting for transfers between devices, on_device(): low = lax.ppermute(both, 'quad', [(0, 2), (1, 3)])  20.8 us
    all_to_all x1, blocking collectives, on_device(): mine = lax.all_to_all(packed, group, 0, 0)  14.1 us
    all_to_all x1, blocking collectives, returned(): return lax.all_to_all(done, group, 0, 0)  12.7 us
    pallas_call x6, Pallas kernels, call(): pl.pallas_call(kernel, out_shape=outs[0] if single else tuple(outs), in_s...  8.7 us
    ppermute x1, starting transfers between devices, on_device(): below = lax.ppermute(sent, 'quad', [(2, 3)])  3.44 us
    ppermute x1, starting transfers between devices, upward(): return lax.ppermute(value, stack, [(i, i + 1) for i in range(groups - 1)])  3.1 us
  transfers between devices with their start and end apart: 3, of which 1 were waited for; matrix products, arithmetic and copies ran while one was open for 0% of the time, Pallas kernels for 5%

profile of v6, /device:TPU:345, one launch (start us, length us, event | category | flops | bytes accessed | tf_op | source)
XLA Modules:
  0.0 64.9 jit_solution(115633614209836628)
XLA Ops:
  0.0 2.3 %shard_map.55 = (bf16[16,96,128]{2,1,0:T(8,128)(2,1)S(1)}, f32[4,64,128]{2,1,0:T(8,128)S(1)}) custom-call(s32[1]{0:T(128)} %bitcast.3.head_ref, bf16[128,256]{1,0:T(8,128)(2,1)} %q_ref.1, bf16[128,256]{1,0:T(8,128)(2,1)} %k_ref.1, bf16[128,1024]{1,0:T(8,128)(2,1)} %v_ref.1, f32[3,1024]{1,0:T(4,128)} %w_ref.1, f32[1,1024]{1,0:T(1,128)} %bitcast.5), custom_call_target="tpu_custom_call" | custom-call | tf_op jit(solution)/shard_map/pallas_call | solution.py:279
  2.3 14.1 %all_to_all.15.x_ref = bf16[16,96,128]{2,1,0:T(8,128)(2,1)S(1)} all-to-all(bf16[16,96,128]{2,1,0:T(8,128)(2,1)S(1)} %get-tuple-element.90), channel_id=1, replica_groups=mesh['dp'=4,'quad'=4,'half'=2,'pair'=2,'core'=2,'inner'=4] {'pair','core..., dimensions={0} | all-to-all | bytes 786432 | tf_op jit(solution)/shard_map/all_to_all | solution.py:309
  16.4 0.7 %shard_map.56 = (bf16[176,128]{1,0:T(8,128)(2,1)S(1)}, f32[2,64,128]{2,1,0:T(8,128)S(1)}, bf16[16,64,128]{2,1,0:T(8,128)(2,1)S(1)}) custom-call(bf16[16,96,128]{2,1,0:T(8,128)(2,1)S(1)} %all_to_all.15.x_ref, f32[4,64,128]{2,1,0:T(8,128)S(1)} %get-tuple-element.91.taps_ref), custom_call_target="tpu_custom_call" | custom-call | tf_op jit(solution)/shard_map/pallas_call | solution.py:279
  17.1 3.1 %collective-permute-start.1 = (bf16[176,128]{1,0:T(8,128)(2,1)S(1)}, bf16[176,128]{1,0:T(8,128)(2,1)S(1)}, u32[]{:S(2)}, u32[]{:S(2)}) collective-permute-start(bf16[176,128]{1,0:T(8,128)(2,1)S(1)} %get-tuple-element.93), channel_id=1, source_target_pairs={{0,16},{16,32},{32,48},{48,64},{64,80},{80,96},{96,112},{1,17},{17... | collective-permute-start | bytes 135176 | tf_op jit(solution)/shard_map/ppermute | solution.py:300
  20.3 3.1 %shard_map.57 = (f32[16,64,128]{2,1,0:T(8,128)S(1)}, f32[16,64,128]{2,1,0:T(8,128)S(1)}, bf16[160,2048]{1,0:T(8,128)(2,1)S(1)}) custom-call(bf16[16,96,128]{2,1,0:T(8,128)(2,1)S(1)} %all_to_all.15.x_ref, bf16[16,64,128]{2,1,0:T(8,128)(2,1)S(1)} %get-tuple-element.94.conv_ref), custom_call_target="tpu_custom_call" | custom-call | tf_op jit(solution)/shard_map/pallas_call | solution.py:279
  23.4 0.0 collective-permute-done.1.near_ref
  23.4 0.4 shard_map.58
  23.8 0.1 conditional.3
  23.9 0.6 conditional.4
  23.9 0.6 copy.13
  24.5 1.3 %collective-permute-start.3 = (bf16[96,128]{1,0:T(8,128)(2,1)S(1)}, bf16[96,128]{1,0:T(8,128)(2,1)S(1)}, u32[]{:S(2)}, u32[]{:S(2)}) collective-permute-start(bf16[96,128]{1,0:T(8,128)(2,1)S(1)} %get-tuple-element.105), channel_id=1, source_target_pairs={{0,64},{32,96},{1,65},{33,97},{2,66},{34,98},{3,67},{35,99},{4,68}... | collective-permute-start | bytes 73736 | tf_op jit(solution)/shard_map/ppermute | solution.py:375
  25.8 3.4 %collective-permute-start.2 = (bf16[96,128]{1,0:T(8,128)(2,1)S(1)}, bf16[96,128]{1,0:T(8,128)(2,1)S(1)}, u32[]{:S(2)}, u32[]{:S(2)}) collective-permute-start(bf16[96,128]{1,0:T(8,128)(2,1)S(1)} %get-tuple-element.102), channel_id=1, source_target_pairs={{64,96},{65,97},{66,98},{67,99},{68,100},{69,101},{70,102},{71,103... | collective-permute-start | bytes 73736 | tf_op jit(solution)/shard_map/ppermute | solution.py:360
  29.3 20.8 %collective-permute-done.3 = bf16[96,128]{1,0:T(8,128)(2,1)S(1)} collective-permute-done((bf16[96,128]{1,0:T(8,128)(2,1)S(1)}, bf16[96,128]{1,0:T(8,128)(2,1)S(1)}, u32[]{:S(2)}, u32[]{:S(2)}) %collective-permute-start.3) | collective-permute-done | bytes 24608 | tf_op jit(solution)/shard_map/ppermute | solution.py:375
  50.0 0.0 collective-permute-done.2
  50.0 14.0 %conditional.5 = (bf16[16,64,128]{2,1,0:T(8,128)(2,1)S(1)}) conditional(s32[]{:T(128)} %convert_element_type.8, (s32[]{:T(128)}, bf16[96,128]{1,0:T(8,128)(2,1)}, bf16[96,128]{1,0:T(8,128)(2,1)S(1)}, bf16[96,128]{1,0:T(8,128)(2,1)S(1)}, bf16[176,128]{1,0:T(8,128)(2,1)S(1)}, /*index=5*/f32[4,64,128]{2,1,0:T(8,128)S(1)}, f32[2,64,128]{2,1,0:T(8,128)S(1)}, ...), branch_computations={%region_4.0_spmd, %region_5.0_spmd} | conditional | bytes 524296 | solution.py:376
  50.0 1.3 %branch_0_fun.1 = bf16[16,64,128]{2,1,0:T(8,128)(2,1)S(1)} custom-call(s32[1]{0:T(128)} %bitcast.1.quad_ref, bf16[96,128]{1,0:T(8,128)(2,1)} %get-tuple-element.64.pair_recv_ref, bf16[96,128]{1,0:T(8,128)(2,1)S(1)} %get-tuple-element.65.below_ref, bf16[96,128]{1,0:T(8,128)(2,1)S(1)} %get-tuple-element.66.low_ref, ...), custom_call_target="tpu_custom_call" | custom-call | tf_op jit(solution)/shard_map/cond/branch_0_fun/pallas_call | solution.py:279
  51.4 12.7 %all_to_all.14 = bf16[16,64,128]{2,1,0:T(8,128)(2,1)S(1)} all-to-all(bf16[16,64,128]{2,1,0:T(8,128)(2,1)S(1)} %branch_0_fun.1), channel_id=1, replica_groups=mesh['dp'=4,'quad'=4,'half'=2,'pair'=2,'core'=2,'inner'=4] {'pair','core..., dimensions={0} | all-to-all | bytes 524288 | tf_op jit(solution)/shard_map/cond/branch_0_fun/all_to_all | solution.py:353
  64.0 0.8 %shard_map.59 = bf16[128,1024]{1,0:T(8,128)(2,1)} custom-call(bf16[16,64,128]{2,1,0:T(8,128)(2,1)S(1)} %get-tuple-element.112.x_ref), custom_call_target="tpu_custom_call" | custom-call | tf_op jit(solution)/shard_map/pallas_call | solution.py:279
  (2 shorter events, 0.0 us)
Async XLA Ops:
  17.1 6.3 %collective-permute-start.1 = (bf16[176,128]{1,0:T(8,128)(2,1)S(1)}, bf16[176,128]{1,0:T(8,128)(2,1)S(1)}, u32[]{:S(2)}, u32[]{:S(2)}) collective-permute-start(bf16[176,128]{1,0:T(8,128)(2,1)S(1)} %get-tuple-element.93), channel_id=1, source_target_pairs={{0,16},{16,32},{32,48},{48,64},{64,80},{80,96},{96,112},{1,17},{17... | collective-permute-start | bytes 135176 | tf_op jit(solution)/shard_map/ppermute | solution.py:300
  24.5 25.5 %collective-permute-start.3 = (bf16[96,128]{1,0:T(8,128)(2,1)S(1)}, bf16[96,128]{1,0:T(8,128)(2,1)S(1)}, u32[]{:S(2)}, u32[]{:S(2)}) collective-permute-start(bf16[96,128]{1,0:T(8,128)(2,1)S(1)} %get-tuple-element.105), channel_id=1, source_target_pairs={{0,64},{32,96},{1,65},{33,97},{2,66},{34,98},{3,67},{35,99},{4,68}... | collective-permute-start | bytes 73736 | tf_op jit(solution)/shard_map/ppermute | solution.py:375
  25.8 24.2 %collective-permute-start.2 = (bf16[96,128]{1,0:T(8,128)(2,1)S(1)}, bf16[96,128]{1,0:T(8,128)(2,1)S(1)}, u32[]{:S(2)}, u32[]{:S(2)}) collective-permute-start(bf16[96,128]{1,0:T(8,128)(2,1)S(1)} %get-tuple-element.102), channel_id=1, source_target_pairs={{64,96},{65,97},{66,98},{67,99},{68,100},{69,101},{70,102},{71,103... | collective-permute-start | bytes 73736 | tf_op jit(solution)/shard_map/ppermute | solution.py:360

commit v7 on v6

--- a/solution.py
+++ b/solution.py
@@ -218,7 +218,8 @@
     )
 
 
-def join_kernel(quad_ref, pair_ref, recv_ref, taps_ref, sent_ref):
+def join_kernel(quad_ref, pair_ref, recv_ref, taps_ref, sent_ref, copy_ref):
+    copy_ref[...] = recv_ref[...]
     lowest = quad_ref[0] == 0
     main, rest = pair_ref[0], pair_ref[1]
     recv_main, recv_rest = unfold(recv_ref[...])
@@ -230,7 +231,19 @@
     )
 
 
-def late_kernel(quad_ref, pair_recv_ref, below_ref, low_ref, near_ref, taps_ref, *refs):
+def final_kernel(
+    quad_ref,
+    pair_recv_ref,
+    below_ref,
+    low_ref,
+    near_ref,
+    taps_ref,
+    edge_ref,
+    num_ref,
+    win_ref,
+    phi_ref,
+    out_ref,
+):
     second = quad_ref[0] == 1
     near_main, near_rest = unfold(near_ref[0:STATE_ROWS, :])
     one_main, one_rest = unfold(pair_recv_ref[...])
@@ -241,15 +254,7 @@
     above_low = jnp.where(quad_ref[0] == 2, near_rest, below_rest)
     edge_main, edge_rest = edge_state(taps_ref, [(near_rest, below_rest), (above_low, low_rest)])
     main = near_main + below_main + low_main + edge_main
-    finish(main, near_rest + below_rest + low_rest + edge_rest, taps_ref, *refs)
-
-
-def early_kernel(near_ref, taps_ref, *refs):
-    main, rest = unfold(near_ref[0:STATE_ROWS, :])
-    finish(main, rest, taps_ref, *refs)
-
-
-def finish(main, rest, taps_ref, edge_ref, num_ref, win_ref, phi_ref, out_ref):
+    rest = near_rest + below_rest + low_rest + edge_rest
     state = jnp.concatenate([main, rest[:, :EDGE]], axis=1)
     group_edge = jnp.concatenate([edge_ref[0], edge_ref[1][:, :EDGE]], axis=1)
     later = (state + group_edge).astype(BF16)
@@ -346,39 +351,29 @@
         {5: 3, 6: 4},
     )
     quad = lax.axis_index("quad")
-    parts = [near, taps, edge, num, win, phi]
-
-    def returned(kernel, scalars, arrays):
-        done = call(kernel, [pltpu.VMEM((members, *block), BF16)], scalars, [], arrays)
-        return lax.all_to_all(done, group, 0, 0)
-
-    heads = lax.cond(
-        quad == 0,
-        lambda: returned(early_kernel, [], parts),
-        lambda: jnp.zeros((HEADS, *block), BF16),
-    )
+
     below = lax.ppermute(sent, "quad", [(2, 3)])
 
     def lower_pair(sent):
         recv = lax.ppermute(sent, "quad", [(0, 1), (1, 0)])
-        both = call(
+        return call(
             join_kernel,
-            [pltpu.VMEM((STATE_ROWS, LANES), BF16)],
+            [pltpu.VMEM((STATE_ROWS, LANES), BF16), pltpu.VMEM((STATE_ROWS, LANES), BF16)],
             [scalar(quad)],
             [],
             [pair, recv, taps],
         )
-        return both, recv
-
-    ready, heads = lax.optimization_barrier((sent, heads))
-    both, pair_recv = lax.cond(quad < 2, lower_pair, lambda sent: (sent, sent), ready)
+
+    both, pair_recv = lax.cond(quad < 2, lower_pair, lambda sent: (sent, sent), sent)
     low = lax.ppermute(both, "quad", [(0, 2), (1, 3)])
-    heads = lax.cond(
-        quad == 0,
-        lambda heads: heads,
-        lambda heads: returned(late_kernel, [scalar(quad)], [pair_recv, below, low, *parts]),
-        heads,
-    )
+    done = call(
+        final_kernel,
+        [pltpu.VMEM((members, *block), BF16)],
+        [scalar(quad)],
+        [],
+        [pair_recv, below, low, near, taps, edge, num, win, phi],
+    )
+    heads = lax.all_to_all(done, group, 0, 0)
     out = jax.ShapeDtypeStruct((BLK, HEADS * VDIM), BF16)
     return call(unpack_kernel, [out], [], [], [heads])
 

time: 65.2 us -> 56.8 us (0.87)
  the two profiles are of different devices: /device:TPU:345 before, /device:TPU:1 now
where the time goes in v7:
time: 56.8 us; the launch traced here: 56.5 us
  blocking collectives  31.6 us (56%)
  starting transfers between devices  15 us (26%)
  Pallas kernels  8.3 us (15%)
  waiting for transfers between devices  1.46 us (3%)
    all_to_all x1, blocking collectives, on_device(): mine = lax.all_to_all(packed, group, 0, 0)  18.3 us
    all_to_all x1, blocking collectives, on_device(): heads = lax.all_to_all(done, group, 0, 0)  13.4 us
    ppermute x1, starting transfers between devices, lower_pair(): recv = lax.ppermute(sent, 'quad', [(0, 1), (1, 0)])  8.81 us
    pallas_call x7, Pallas kernels, call(): pl.pallas_call(kernel, out_shape=outs[0] if single else tuple(outs), in_s...  8.3 us
    ppermute x1, starting transfers between devices, on_device(): low = lax.ppermute(both, 'quad', [(0, 2), (1, 3)])  3.05 us
    ppermute x1, starting transfers between devices, upward(): return lax.ppermute(value, stack, [(i, i + 1) for i in range(groups - 1)])  2.48 us
    ppermute x1, waiting for transfers between devices, lower_pair(): recv = lax.ppermute(sent, 'quad', [(0, 1), (1, 0)])  1.2 us
  transfers between devices with their start and end apart: 4, of which 2 were waited for; matrix products, arithmetic and copies ran while one was open for 0% of the time, Pallas kernels for 6%

profile of v7, /device:TPU:1, one launch (start us, length us, event | category | flops | bytes accessed | tf_op | source)
XLA Modules:
  0.0 56.5 jit_solution(15763276325003936386)
XLA Ops:
  0.0 2.3 %shard_map.55 = (bf16[16,96,128]{2,1,0:T(8,128)(2,1)S(1)}, f32[4,64,128]{2,1,0:T(8,128)S(1)}) custom-call(s32[1]{0:T(128)} %bitcast.3.head_ref, bf16[128,256]{1,0:T(8,128)(2,1)} %q_ref.1, bf16[128,256]{1,0:T(8,128)(2,1)} %k_ref.1, bf16[128,1024]{1,0:T(8,128)(2,1)} %v_ref.1, f32[3,1024]{1,0:T(4,128)} %w_ref.1, f32[1,1024]{1,0:T(1,128)} %bitcast.5), custom_call_target="tpu_custom_call" | custom-call | tf_op jit(solution)/shard_map/pallas_call | solution.py:284
  2.3 18.3 %all_to_all.10.x_ref = bf16[16,96,128]{2,1,0:T(8,128)(2,1)S(1)} all-to-all(bf16[16,96,128]{2,1,0:T(8,128)(2,1)S(1)} %get-tuple-element.33), channel_id=1, replica_groups=mesh['dp'=4,'quad'=4,'half'=2,'pair'=2,'core'=2,'inner'=4] {'pair','core..., dimensions={0} | all-to-all | bytes 786432 | tf_op jit(solution)/shard_map/all_to_all | solution.py:314
  20.6 0.7 %shard_map.56 = (bf16[176,128]{1,0:T(8,128)(2,1)S(1)}, f32[2,64,128]{2,1,0:T(8,128)S(1)}, bf16[16,64,128]{2,1,0:T(8,128)(2,1)S(1)}) custom-call(bf16[16,96,128]{2,1,0:T(8,128)(2,1)S(1)} %all_to_all.10.x_ref, f32[4,64,128]{2,1,0:T(8,128)S(1)} %get-tuple-element.34.taps_ref), custom_call_target="tpu_custom_call" | custom-call | tf_op jit(solution)/shard_map/pallas_call | solution.py:284
  21.3 2.5 %collective-permute-start.1 = (bf16[176,128]{1,0:T(8,128)(2,1)S(1)}, bf16[176,128]{1,0:T(8,128)(2,1)S(1)}, u32[]{:S(2)}, u32[]{:S(2)}) collective-permute-start(bf16[176,128]{1,0:T(8,128)(2,1)S(1)} %get-tuple-element.36), channel_id=1, source_target_pairs={{0,16},{16,32},{32,48},{48,64},{64,80},{80,96},{96,112},{1,17},{17... | collective-permute-start | bytes 135176 | tf_op jit(solution)/shard_map/ppermute | solution.py:305
  23.8 3.1 %shard_map.57 = (f32[16,64,128]{2,1,0:T(8,128)S(1)}, f32[16,64,128]{2,1,0:T(8,128)S(1)}, bf16[160,2048]{1,0:T(8,128)(2,1)S(1)}) custom-call(bf16[16,96,128]{2,1,0:T(8,128)(2,1)S(1)} %all_to_all.10.x_ref, bf16[16,64,128]{2,1,0:T(8,128)(2,1)S(1)} %get-tuple-element.37.conv_ref), custom_call_target="tpu_custom_call" | custom-call | tf_op jit(solution)/shard_map/pallas_call | solution.py:284
  26.9 0.0 collective-permute-done.1.near_ref
  27.0 0.4 shard_map.58
  27.3 10.4 %conditional.1 = ((bf16[96,128]{1,0:T(8,128)(2,1)S(1)}, bf16[96,128]{1,0:T(8,128)(2,1)S(1)})) conditional(s32[]{:T(128)} %convert_element_type.4, bf16[96,128]{1,0:T(8,128)(2,1)S(1)} %get-tuple-element.40, (s32[]{:T(128)}, bf16[96,128]{1,0:T(8,128)(2,1)S(1)}, f32[2,64,128]{2,1,0:T(8,128)S(1)}, f32[4,64,128]{2,1,0:T(8,128)S(1)}) %tuple.12), branch_computations={%region_0.0_spmd, %region_1.0_spmd} | conditional | bytes 98352 | solution.py:367
  27.4 8.8 %collective-permute-start = (bf16[96,128]{1,0:T(8,128)(2,1)S(1)}, bf16[96,128]{1,0:T(8,128)(2,1)S(1)}, u32[]{:S(2)}, u32[]{:S(2)}) collective-permute-start(bf16[96,128]{1,0:T(8,128)(2,1)S(1)} %get-tuple-element.16), channel_id=1, source_target_pairs={{0,32},{32,0},{1,33},{33,1},{2,34},{34,2},{3,35},{35,3},{4,36},{36... | collective-permute-start | bytes 73736 | tf_op jit(solution)/shard_map/cond/branch_1_fun/ppermute | solution.py:358
  36.2 1.2 %collective-permute-done.recv_ref = bf16[96,128]{1,0:T(8,128)(2,1)S(1)} collective-permute-done((bf16[96,128]{1,0:T(8,128)(2,1)S(1)}, bf16[96,128]{1,0:T(8,128)(2,1)S(1)}, u32[]{:S(2)}, u32[]{:S(2)}) %collective-permute-start) | collective-permute-done | bytes 24608 | tf_op jit(solution)/shard_map/cond/branch_1_fun/ppermute | solution.py:358
  37.4 0.3 branch_1_fun.1
  37.7 3.1 %collective-permute-start.3 = (bf16[96,128]{1,0:T(8,128)(2,1)S(1)}, bf16[96,128]{1,0:T(8,128)(2,1)S(1)}, u32[]{:S(2)}, u32[]{:S(2)}) collective-permute-start(bf16[96,128]{1,0:T(8,128)(2,1)S(1)} %get-tuple-element.43), channel_id=1, source_target_pairs={{0,64},{32,96},{1,65},{33,97},{2,66},{34,98},{3,67},{35,99},{4,68}... | collective-permute-start | bytes 73736 | tf_op jit(solution)/shard_map/ppermute | solution.py:368
  40.8 0.7 %collective-permute-start.2 = (bf16[96,128]{1,0:T(8,128)(2,1)S(1)}, bf16[96,128]{1,0:T(8,128)(2,1)S(1)}, u32[]{:S(2)}, u32[]{:S(2)}) collective-permute-start(bf16[96,128]{1,0:T(8,128)(2,1)S(1)} %get-tuple-element.40), channel_id=1, source_target_pairs={{64,96},{65,97},{66,98},{67,99},{68,100},{69,101},{70,102},{71,103... | collective-permute-start | bytes 73736 | tf_op jit(solution)/shard_map/ppermute | solution.py:355
  41.5 0.3 collective-permute-done.3.low_ref
  41.7 0.0 collective-permute-done.2.below_ref
  41.7 0.6 %shard_map.59 = bf16[16,64,128]{2,1,0:T(8,128)(2,1)S(1)} custom-call(s32[1]{0:T(128)} %bitcast.1.quad_ref, bf16[96,128]{1,0:T(8,128)(2,1)S(1)} %get-tuple-element.42.pair_recv_ref, bf16[96,128]{1,0:T(8,128)(2,1)S(1)} %collective-permute-done.2.below_ref, bf16[96,128]{1,0:T(8,128)(2,1)S(1)} %collective-permute-done.3.low_ref, ...), custom_call_target="tpu_custom_call" | custom-call | tf_op jit(solution)/shard_map/pallas_call | solution.py:284
  42.3 13.4 %all_to_all.11.x_ref = bf16[16,64,128]{2,1,0:T(8,128)(2,1)S(1)} all-to-all(bf16[16,64,128]{2,1,0:T(8,128)(2,1)S(1)} %shard_map.59), channel_id=1, replica_groups=mesh['dp'=4,'quad'=4,'half'=2,'pair'=2,'core'=2,'inner'=4] {'pair','core..., dimensions={0} | all-to-all | bytes 524288 | tf_op jit(solution)/shard_map/all_to_all | solution.py:376
  55.7 0.8 %shard_map.60 = bf16[128,1024]{1,0:T(8,128)(2,1)} custom-call(bf16[16,64,128]{2,1,0:T(8,128)(2,1)S(1)} %all_to_all.11.x_ref), custom_call_target="tpu_custom_call" | custom-call | tf_op jit(solution)/shard_map/pallas_call | solution.py:284
Async XLA Ops:
  21.3 5.7 %collective-permute-start.1 = (bf16[176,128]{1,0:T(8,128)(2,1)S(1)}, bf16[176,128]{1,0:T(8,128)(2,1)S(1)}, u32[]{:S(2)}, u32[]{:S(2)}) collective-permute-start(bf16[176,128]{1,0:T(8,128)(2,1)S(1)} %get-tuple-element.36), channel_id=1, source_target_pairs={{0,16},{16,32},{32,48},{48,64},{64,80},{80,96},{96,112},{1,17},{17... | collective-permute-start | bytes 135176 | tf_op jit(solution)/shard_map/ppermute | solution.py:305
  27.4 10.0 %collective-permute-start = (bf16[96,128]{1,0:T(8,128)(2,1)S(1)}, bf16[96,128]{1,0:T(8,128)(2,1)S(1)}, u32[]{:S(2)}, u32[]{:S(2)}) collective-permute-start(bf16[96,128]{1,0:T(8,128)(2,1)S(1)} %get-tuple-element.16), channel_id=1, source_target_pairs={{0,32},{32,0},{1,33},{33,1},{2,34},{34,2},{3,35},{35,3},{4,36},{36... | collective-permute-start | bytes 73736 | tf_op jit(solution)/shard_map/cond/branch_1_fun/ppermute | solution.py:358
  37.7 4.0 %collective-permute-start.3 = (bf16[96,128]{1,0:T(8,128)(2,1)S(1)}, bf16[96,128]{1,0:T(8,128)(2,1)S(1)}, u32[]{:S(2)}, u32[]{:S(2)}) collective-permute-start(bf16[96,128]{1,0:T(8,128)(2,1)S(1)} %get-tuple-element.43), channel_id=1, source_target_pairs={{0,64},{32,96},{1,65},{33,97},{2,66},{34,98},{3,67},{35,99},{4,68}... | collective-permute-start | bytes 73736 | tf_op jit(solution)/shard_map/ppermute | solution.py:368
  40.8 0.9 %collective-permute-start.2 = (bf16[96,128]{1,0:T(8,128)(2,1)S(1)}, bf16[96,128]{1,0:T(8,128)(2,1)S(1)}, u32[]{:S(2)}, u32[]{:S(2)}) collective-permute-start(bf16[96,128]{1,0:T(8,128)(2,1)S(1)} %get-tuple-element.40), channel_id=1, source_target_pairs={{64,96},{65,97},{66,98},{67,99},{68,100},{69,101},{70,102},{71,103... | collective-permute-start | bytes 73736 | tf_op jit(solution)/shard_map/ppermute | solution.py:355

commit v8 on v7

--- a/solution.py
+++ b/solution.py
@@ -161,61 +161,55 @@
     return nn(value, weights), window / row_sum
 
 
-def local_kernel(x_ref, conv_ref, num_ref, win_ref, phi_ref):
+def local_blocks(first_ref, x_ref, conv_ref, near_ref, taps_ref, num_ref, win_ref, phi_ref):
     count = x_ref.shape[0]
     inside = inside_window(None)
     state = jnp.zeros((VDIM, NPHI), F32)
+    taps = [taps_ref[index] for index in range(TAPS)]
+    before_raw = near_ref[STATE_ROWS + FEAT :, :].astype(F32)
+    before_value = convolve(taps, before_raw, jnp.zeros((VDIM, BLK), F32))
+    before_key = near_ref[STATE_ROWS : STATE_ROWS + FEAT, :]
     for blk in range(count):
         query = x_ref[blk, 0:FEAT, :]
         key = x_ref[blk, FEAT : 2 * FEAT, :]
-        value = conv_ref[blk]
+        if blk == 0:
+            value = convolve(taps, x_ref[0, 2 * FEAT :, :].astype(F32), before_raw)
+        else:
+            value = conv_ref[blk]
         phi_query = features(query.astype(F32), False)
         phi_ref[:, blk * BLK : (blk + 1) * BLK] = phi_query
-        if blk > 0:
-            own, win = block_parts(query, key, value, before_key, before_value, inside)
-            num_ref[blk] = own + nn(state.astype(BF16), phi_query)
-            win_ref[blk] = win
+        mask = inside if blk > 0 or first_ref is None else inside_window(first_ref[0])
+        own, win = block_parts(query, key, value, before_key, before_value, mask)
+        num_ref[blk] = own + nn(state.astype(BF16), phi_query) if blk > 0 else own
+        win_ref[blk] = win
         if blk + 1 < count:
             state = state + nt(value, features(key.astype(F32), True))
         before_key, before_value = key, value
 
 
-def merge_kernel(
-    first_ref,
-    own_ref,
-    near_ref,
-    taps_ref,
-    x_ref,
-    num_in_ref,
-    win_in_ref,
-    sent_ref,
-    pair_ref,
-    edge_ref,
-    num_ref,
-    win_ref,
-):
+def lower_local_kernel(first_ref, *refs):
+    local_blocks(first_ref, *refs)
+
+
+def unwritten_kernel(num_ref, win_ref, phi_ref):
+    pass
+
+
+def upper_local_kernel(quad_ref, x_ref, conv_ref, near_ref, taps_ref, *refs):
+    @pl.when(quad_ref[0] > 1)
+    def _():
+        local_blocks(None, x_ref, conv_ref, near_ref, taps_ref, *refs[3:])
+
+
+def merge_kernel(own_ref, near_ref, taps_ref, sent_ref, pair_ref):
     main, rest = own_ref[0], own_ref[1]
     near_main, near_rest = unfold(near_ref[0:STATE_ROWS, :])
     edge_main, edge_rest = edge_state(taps_ref, [(rest, near_rest)])
-    edge_ref[0] = edge_main
-    edge_ref[1] = edge_rest
     main = main + near_main + edge_main
     rest = joined(rest + near_rest + edge_rest, rest, near_rest)
     pair_ref[0] = main
     pair_ref[1] = rest
     sent_ref[...] = fold(main, rest)
-    taps = [taps_ref[index] for index in range(TAPS)]
-    raw = near_ref[STATE_ROWS + FEAT :, :].astype(F32)
-    before_value = convolve(taps, raw, jnp.zeros((VDIM, BLK), F32))
-    value = convolve(taps, x_ref[0, 2 * FEAT :, :].astype(F32), raw)
-    num_ref[0], win_ref[0] = block_parts(
-        x_ref[0, 0:FEAT, :],
-        x_ref[0, FEAT : 2 * FEAT, :],
-        value,
-        near_ref[STATE_ROWS : STATE_ROWS + FEAT, :],
-        before_value,
-        inside_window(first_ref[0]),
-    )
 
 
 def join_kernel(quad_ref, pair_ref, recv_ref, taps_ref, sent_ref, copy_ref):
@@ -238,7 +232,6 @@
     low_ref,
     near_ref,
     taps_ref,
-    edge_ref,
     num_ref,
     win_ref,
     phi_ref,
@@ -255,14 +248,11 @@
     edge_main, edge_rest = edge_state(taps_ref, [(near_rest, below_rest), (above_low, low_rest)])
     main = near_main + below_main + low_main + edge_main
     rest = near_rest + below_rest + low_rest + edge_rest
-    state = jnp.concatenate([main, rest[:, :EDGE]], axis=1)
-    group_edge = jnp.concatenate([edge_ref[0], edge_ref[1][:, :EDGE]], axis=1)
-    later = (state + group_edge).astype(BF16)
-    state = state.astype(BF16)
+    state = jnp.concatenate([main, rest[:, :EDGE]], axis=1).astype(BF16)
     gain = taps_ref[TAPS]
     for blk in range(num_ref.shape[0]):
         phi = phi_ref[:, blk * BLK : (blk + 1) * BLK]
-        num = num_ref[blk] + nn(state if blk == 0 else later, phi)
+        num = num_ref[blk] + nn(state, phi)
         mean_square = jnp.sum(num * num, axis=0, keepdims=True) * (1.0 / VDIM)
         linear = num * lax.rsqrt(mean_square + 1e-06) * gain
         out_ref[blk] = (linear + win_ref[blk]).astype(BF16)
@@ -325,53 +315,54 @@
     )
     near = upward(sent)
     block = (VDIM, BLK)
-    num, win, phi = call(
-        local_kernel,
-        [
-            pltpu.VMEM((members, *block), F32),
-            pltpu.VMEM((members, *block), F32),
-            pltpu.VMEM((NPHI, members * BLK), BF16),
-        ],
-        [],
-        [],
-        [mine, conv],
-    )
-    sent, pair, edge, num, win = call(
+    sent, pair = call(
         merge_kernel,
-        [
-            pltpu.VMEM((STATE_ROWS, LANES), BF16),
-            pltpu.VMEM((2, VDIM, LANES), F32),
-            pltpu.VMEM((2, VDIM, LANES), F32),
-            pltpu.VMEM((members, *block), F32),
-            pltpu.VMEM((members, *block), F32),
-        ],
-        [scalar(lax.axis_index(stack) == 0)],
-        [],
-        [own, near, taps, mine, num, win],
-        {5: 3, 6: 4},
+        [pltpu.VMEM((STATE_ROWS, LANES), BF16), pltpu.VMEM((2, VDIM, LANES), F32)],
+        [],
+        [],
+        [own, near, taps],
     )
     quad = lax.axis_index("quad")
-
-    below = lax.ppermute(sent, "quad", [(2, 3)])
-
-    def lower_pair(sent):
+    first = scalar(lax.axis_index(stack) == 0)
+    local_shapes = [
+        pltpu.VMEM((members, *block), F32),
+        pltpu.VMEM((members, *block), F32),
+        pltpu.VMEM((NPHI, members * BLK), BF16),
+    ]
+    local_arrays = [mine, conv, near, taps]
+
+    def lower(sent):
         recv = lax.ppermute(sent, "quad", [(0, 1), (1, 0)])
-        return call(
+        local = call(lower_local_kernel, local_shapes, [first], [], local_arrays)
+        both, recv = call(
             join_kernel,
             [pltpu.VMEM((STATE_ROWS, LANES), BF16), pltpu.VMEM((STATE_ROWS, LANES), BF16)],
             [scalar(quad)],
             [],
             [pair, recv, taps],
         )
-
-    both, pair_recv = lax.cond(quad < 2, lower_pair, lambda sent: (sent, sent), sent)
-    low = lax.ppermute(both, "quad", [(0, 2), (1, 3)])
+        return both, recv, *local
+
+    def upper(sent):
+        return sent, sent, *call(unwritten_kernel, local_shapes, [], [], [])
+
+    both, pair_recv, *local = lax.cond(quad < 2, lower, upper, sent)
+    low = lax.ppermute(both, "quad", [(1, 2), (0, 3)])
+    below = lax.ppermute(sent, "quad", [(2, 3)])
+    num, win, phi = call(
+        upper_local_kernel,
+        local_shapes,
+        [scalar(quad)],
+        [],
+        [*local_arrays, *local],
+        {5: 0, 6: 1, 7: 2},
+    )
     done = call(
         final_kernel,
         [pltpu.VMEM((members, *block), BF16)],
         [scalar(quad)],
         [],
-        [pair_recv, below, low, near, taps, edge, num, win, phi],
+        [pair_recv, below, low, near, taps, num, win, phi],
     )
     heads = lax.all_to_all(done, group, 0, 0)
     out = jax.ShapeDtypeStruct((BLK, HEADS * VDIM), BF16)

time: 56.8 us -> 56 us (0.986)
  starting transfers between devices: 15 us -> 14.1 us
    ppermute x2, waiting for transfers between devices: 1.46 us -> 0.24 us  [the longest x1 0.24 us: on_device(): low = lax.ppermute(both, 'quad', [(1, 2), (0, 3)])]
    ppermute x1, waiting for transfers between devices: 0.01 us -> 1.11 us  [upward(): return lax.ppermute(value, stack, [(i, i + 1) for i in range(groups - 1)])]
    ppermute x2, starting transfers between devices: 11.9 us -> 11 us  [the longest x1 9.72 us: lower(): recv = lax.ppermute(sent, 'quad', [(0, 1), (1, 0)])]
    pallas_call x7 -> x8, Pallas kernels: 8.3 us -> 8.54 us  [call(): pl.pallas_call(kernel, out_shape=outs[0] if single else tuple(outs), in_s...]
where the time goes in v8:
time: 56 us; the launch traced here: 55.7 us
  blocking collectives  31.6 us (56%)
  starting transfers between devices  14.1 us (25%)
  Pallas kernels  8.54 us (15%)
  waiting for transfers between devices  1.35 us (2%)
    all_to_all x1, blocking collectives, on_device(): mine = lax.all_to_all(packed, group, 0, 0)  18.3 us
    all_to_all x1, blocking collectives, on_device(): heads = lax.all_to_all(done, group, 0, 0)  13.4 us
    ppermute x1, starting transfers between devices, lower(): recv = lax.ppermute(sent, 'quad', [(0, 1), (1, 0)])  9.72 us
    pallas_call x8, Pallas kernels, call(): pl.pallas_call(kernel, out_shape=outs[0] if single else tuple(outs), in_s...  8.54 us
    ppermute x1, starting transfers between devices, upward(): return lax.ppermute(value, stack, [(i, i + 1) for i in range(groups - 1)])  2.48 us
    ppermute x1, starting transfers between devices, on_device(): low = lax.ppermute(both, 'quad', [(1, 2), (0, 3)])  1.28 us
  transfers between devices with their start and end apart: 4, of which 2 were waited for; matrix products, arithmetic and copies ran while one was open for 0% of the time, Pallas kernels for 6%

profile of v8, /device:TPU:1, one launch (start us, length us, event | category | flops | bytes accessed | tf_op | source)
XLA Modules:
  0.0 55.7 jit_solution(13869422908993577644)
XLA Ops:
  0.0 2.3 %shard_map.55 = (bf16[16,96,128]{2,1,0:T(8,128)(2,1)S(1)}, f32[4,64,128]{2,1,0:T(8,128)S(1)}) custom-call(s32[1]{0:T(128)} %bitcast.3.head_ref, bf16[128,256]{1,0:T(8,128)(2,1)} %q_ref.1, bf16[128,256]{1,0:T(8,128)(2,1)} %k_ref.1, bf16[128,1024]{1,0:T(8,128)(2,1)} %v_ref.1, f32[3,1024]{1,0:T(4,128)} %w_ref.1, f32[1,1024]{1,0:T(1,128)} %bitcast.5), custom_call_target="tpu_custom_call" | custom-call | tf_op jit(solution)/shard_map/pallas_call | solution.py:274
  2.3 18.3 %all_to_all.10.x_ref = bf16[16,96,128]{2,1,0:T(8,128)(2,1)S(1)} all-to-all(bf16[16,96,128]{2,1,0:T(8,128)(2,1)S(1)} %get-tuple-element.54), channel_id=1, replica_groups=mesh['dp'=4,'quad'=4,'half'=2,'pair'=2,'core'=2,'inner'=4] {'pair','core..., dimensions={0} | all-to-all | bytes 786432 | tf_op jit(solution)/shard_map/all_to_all | solution.py:304
  20.6 0.7 %shard_map.56 = (bf16[176,128]{1,0:T(8,128)(2,1)S(1)}, f32[2,64,128]{2,1,0:T(8,128)S(1)}, bf16[16,64,128]{2,1,0:T(8,128)(2,1)S(1)}) custom-call(bf16[16,96,128]{2,1,0:T(8,128)(2,1)S(1)} %all_to_all.10.x_ref, f32[4,64,128]{2,1,0:T(8,128)S(1)} %get-tuple-element.55.taps_ref), custom_call_target="tpu_custom_call" | custom-call | tf_op jit(solution)/shard_map/pallas_call | solution.py:274
  21.3 2.5 %collective-permute-start.1 = (bf16[176,128]{1,0:T(8,128)(2,1)S(1)}, bf16[176,128]{1,0:T(8,128)(2,1)S(1)}, u32[]{:S(2)}, u32[]{:S(2)}) collective-permute-start(bf16[176,128]{1,0:T(8,128)(2,1)S(1)} %get-tuple-element.57), channel_id=1, source_target_pairs={{0,16},{16,32},{32,48},{48,64},{64,80},{80,96},{96,112},{1,17},{17... | collective-permute-start | bytes 135176 | tf_op jit(solution)/shard_map/ppermute | solution.py:295
  23.8 1.1 %collective-permute-done.1.near_ref = bf16[176,128]{1,0:T(8,128)(2,1)S(1)} collective-permute-done((bf16[176,128]{1,0:T(8,128)(2,1)S(1)}, bf16[176,128]{1,0:T(8,128)(2,1)S(1)}, u32[]{:S(2)}, u32[]{:S(2)}) %collective-permute-start.1) | collective-permute-done | bytes 45088 | tf_op jit(solution)/shard_map/ppermute | solution.py:295
  24.9 0.3 shard_map.57
  25.2 13.5 %conditional.1 = (bf16[96,128]{1,0:T(8,128)(2,1)S(1)}, bf16[96,128]{1,0:T(8,128)(2,1)S(1)}, f32[16,64,128]{2,1,0:T(8,128)S(1)}, f32[16,64,128]{2,1,0:T(8,128)S(1)}, bf16[160,2048]{1,0:T(8,128)(2,1)S(1)}) conditional(s32[]{:T(128)} %convert_element_type.6, bf16[96,128]{1,0:T(8,128)(2,1)S(1)} %get-tuple-element.58, (s32[]{:T(128)}, ...), branch_computations={%region_0.0_spmd, %region_1.0_spmd} | conditional | bytes 98384 | solution.py:349
  25.2 9.7 %collective-permute-start = (bf16[96,128]{1,0:T(8,128)(2,1)S(1)}, bf16[96,128]{1,0:T(8,128)(2,1)S(1)}, u32[]{:S(2)}, u32[]{:S(2)}) collective-permute-start(bf16[96,128]{1,0:T(8,128)(2,1)S(1)} %get-tuple-element.28), channel_id=1, source_target_pairs={{0,32},{32,0},{1,33},{33,1},{2,34},{34,2},{3,35},{35,3},{4,36},{36... | collective-permute-start | bytes 73736 | tf_op jit(solution)/shard_map/cond/branch_1_fun/ppermute | solution.py:335
  35.0 3.4 %branch_1_fun.3 = (f32[16,64,128]{2,1,0:T(8,128)S(1)}, f32[16,64,128]{2,1,0:T(8,128)S(1)}, bf16[160,2048]{1,0:T(8,128)(2,1)S(1)}) custom-call(s32[1]{0:T(128)} %bitcast.1.first_ref, bf16[16,96,128]{2,1,0:T(8,128)(2,1)S(1)} %get-tuple-element.33.refs_0_, bf16[16,64,128]{2,1,0:T(8,128)(2,1)S(1)} %get-tuple-element.34.refs_1_, ...), custom_call_target="tpu_custom_call" | custom-call | tf_op jit(solution)/shard_map/cond/branch_1_fun/pallas_call | solution.py:274
  38.4 0.0 collective-permute-done.recv_ref
  38.4 0.3 branch_1_fun.2
  38.7 1.3 %collective-permute-start.3 = (bf16[96,128]{1,0:T(8,128)(2,1)S(1)}, bf16[96,128]{1,0:T(8,128)(2,1)S(1)}, u32[]{:S(2)}, u32[]{:S(2)}) collective-permute-start(bf16[96,128]{1,0:T(8,128)(2,1)S(1)} %get-tuple-element.62), channel_id=1, source_target_pairs={{32,64},{0,96},{33,65},{1,97},{34,66},{2,98},{35,67},{3,99},{36,68... | collective-permute-start | bytes 73736 | tf_op jit(solution)/shard_map/ppermute | solution.py:350
  40.0 0.7 %collective-permute-start.2 = (bf16[96,128]{1,0:T(8,128)(2,1)S(1)}, bf16[96,128]{1,0:T(8,128)(2,1)S(1)}, u32[]{:S(2)}, u32[]{:S(2)}) collective-permute-start(bf16[96,128]{1,0:T(8,128)(2,1)S(1)} %get-tuple-element.58), channel_id=1, source_target_pairs={{64,96},{65,97},{66,98},{67,99},{68,100},{69,101},{70,102},{71,103... | collective-permute-start | bytes 73736 | tf_op jit(solution)/shard_map/ppermute | solution.py:351
  40.7 0.2 collective-permute-done.3.low_ref
  40.9 0.0 collective-permute-done.2.below_ref
  40.9 0.6 %shard_map.59 = bf16[16,64,128]{2,1,0:T(8,128)(2,1)S(1)} custom-call(s32[1]{0:T(128)} %bitcast.2.quad_ref, bf16[96,128]{1,0:T(8,128)(2,1)S(1)} %get-tuple-element.61.pair_recv_ref, bf16[96,128]{1,0:T(8,128)(2,1)S(1)} %collective-permute-done.2.below_ref, bf16[96,128]{1,0:T(8,128)(2,1)S(1)} %collective-permute-done.3.low_ref, ...), custom_call_target="tpu_custom_call" | custom-call | tf_op jit(solution)/shard_map/pallas_call | solution.py:274
  41.6 13.4 %all_to_all.11.x_ref = bf16[16,64,128]{2,1,0:T(8,128)(2,1)S(1)} all-to-all(bf16[16,64,128]{2,1,0:T(8,128)(2,1)S(1)} %shard_map.59), channel_id=1, replica_groups=mesh['dp'=4,'quad'=4,'half'=2,'pair'=2,'core'=2,'inner'=4] {'pair','core..., dimensions={0} | all-to-all | bytes 524288 | tf_op jit(solution)/shard_map/all_to_all | solution.py:367
  54.9 0.8 %shard_map.60 = bf16[128,1024]{1,0:T(8,128)(2,1)} custom-call(bf16[16,64,128]{2,1,0:T(8,128)(2,1)S(1)} %all_to_all.11.x_ref), custom_call_target="tpu_custom_call" | custom-call | tf_op jit(solution)/shard_map/pallas_call | solution.py:274
  (1 shorter events, 0.0 us)
Async XLA Ops:
  21.3 3.6 %collective-permute-start.1 = (bf16[176,128]{1,0:T(8,128)(2,1)S(1)}, bf16[176,128]{1,0:T(8,128)(2,1)S(1)}, u32[]{:S(2)}, u32[]{:S(2)}) collective-permute-start(bf16[176,128]{1,0:T(8,128)(2,1)S(1)} %get-tuple-element.57), channel_id=1, source_target_pairs={{0,16},{16,32},{32,48},{48,64},{64,80},{80,96},{96,112},{1,17},{17... | collective-permute-start | bytes 135176 | tf_op jit(solution)/shard_map/ppermute | solution.py:295
  25.2 13.1 %collective-permute-start = (bf16[96,128]{1,0:T(8,128)(2,1)S(1)}, bf16[96,128]{1,0:T(8,128)(2,1)S(1)}, u32[]{:S(2)}, u32[]{:S(2)}) collective-permute-start(bf16[96,128]{1,0:T(8,128)(2,1)S(1)} %get-tuple-element.28), channel_id=1, source_target_pairs={{0,32},{32,0},{1,33},{33,1},{2,34},{34,2},{3,35},{35,3},{4,36},{36... | collective-permute-start | bytes 73736 | tf_op jit(solution)/shard_map/cond/branch_1_fun/ppermute | solution.py:335
  38.7 2.2 %collective-permute-start.3 = (bf16[96,128]{1,0:T(8,128)(2,1)S(1)}, bf16[96,128]{1,0:T(8,128)(2,1)S(1)}, u32[]{:S(2)}, u32[]{:S(2)}) collective-permute-start(bf16[96,128]{1,0:T(8,128)(2,1)S(1)} %get-tuple-element.62), channel_id=1, source_target_pairs={{32,64},{0,96},{33,65},{1,97},{34,66},{2,98},{35,67},{3,99},{36,68... | collective-permute-start | bytes 73736 | tf_op jit(solution)/shard_map/ppermute | solution.py:350
  40.0 0.9 %collective-permute-start.2 = (bf16[96,128]{1,0:T(8,128)(2,1)S(1)}, bf16[96,128]{1,0:T(8,128)(2,1)S(1)}, u32[]{:S(2)}, u32[]{:S(2)}) collective-permute-start(bf16[96,128]{1,0:T(8,128)(2,1)S(1)} %get-tuple-element.58), channel_id=1, source_target_pairs={{64,96},{65,97},{66,98},{67,99},{68,100},{69,101},{70,102},{71,103... | collective-permute-start | bytes 73736 | tf_op jit(solution)/shard_map/ppermute | solution.py:351

commit v9 on v8

--- a/solution.py
+++ b/solution.py
@@ -17,6 +17,8 @@
 EDGE = NPHI - LANES
 HALF = VDIM // 2
 STATE_ROWS = VDIM + HALF
+HALO_ROWS = STATE_ROWS + HALF
+PIECES = 4
 PART = FEAT + FEAT + VDIM
 F32 = jnp.float32
 BF16 = jnp.bfloat16
@@ -97,10 +99,49 @@
     return jnp.where(lane < EDGE, rest, jnp.where(lane < EDGE + 2, tail_rest, key_rest))
 
 
-def pack_kernel(head_ref, q_ref, k_ref, v_ref, w_ref, gain_ref, out_ref, taps_ref):
+def pack_kernel(
+    head_ref,
+    q_hbm,
+    k_hbm,
+    v_hbm,
+    w_hbm,
+    gain_hbm,
+    out_ref,
+    taps_ref,
+    q_ref,
+    k_ref,
+    v_ref,
+    w_ref,
+    gain_ref,
+    sems,
+):
+    def copy(source, target, index):
+        return pltpu.make_async_copy(source, target, sems.at[index])
+
+    width = HEADS * VDIM // PIECES
+    heads = HEADS // PIECES
+    pieces = [
+        copy(
+            v_hbm.at[:, pl.ds(piece * width, width)],
+            v_ref.at[:, pl.ds(piece * width, width)],
+            4 + piece,
+        )
+        for piece in range(PIECES)
+    ]
+    query, key = copy(q_hbm, q_ref, 0), copy(k_hbm, k_ref, 1)
+    conv, gain = copy(w_hbm, w_ref, 2), copy(gain_hbm, gain_ref, 3)
+    for started in (query, key, *pieces, conv, gain):
+        started.start()
+    query.wait()
     out_ref[:, 0:FEAT, :] = q_ref[...].T.reshape(HEADS, FEAT, BLK)
+    key.wait()
     out_ref[:, FEAT : 2 * FEAT, :] = k_ref[...].T.reshape(HEADS, FEAT, BLK)
-    out_ref[:, 2 * FEAT :, :] = v_ref[...].T.reshape(HEADS, VDIM, BLK)
+    for piece in range(PIECES):
+        pieces[piece].wait()
+        turned = v_ref[:, piece * width : (piece + 1) * width].T.reshape(heads, VDIM, BLK)
+        out_ref[piece * heads : (piece + 1) * heads, 2 * FEAT :, :] = turned
+    conv.wait()
+    gain.wait()
     rows = jnp.concatenate([w_ref[...], gain_ref[...], jnp.zeros((4, HEADS * VDIM), F32)], axis=0)
     mine = jnp.zeros((8, VDIM), F32)
     for head in range(HEADS):
@@ -134,7 +175,10 @@
     own_ref[0] = main
     own_ref[1] = rest
     sent_ref[0:STATE_ROWS, :] = fold(main, rest)
-    sent_ref[STATE_ROWS:, :] = x_ref[count - 1, FEAT:, :]
+    wide = conv.astype(F32)
+    upper = pltpu.roll(wide[:HALF], WIN, 1)
+    sent_ref[STATE_ROWS:HALO_ROWS, :] = jnp.where(lanes(HALF) < WIN, upper, wide[HALF:]).astype(BF16)
+    sent_ref[HALO_ROWS:, :] = x_ref[count - 1, FEAT : 2 * FEAT, :]
 
 
 def inside_window(first):
@@ -166,9 +210,10 @@
     inside = inside_window(None)
     state = jnp.zeros((VDIM, NPHI), F32)
     taps = [taps_ref[index] for index in range(TAPS)]
-    before_raw = near_ref[STATE_ROWS + FEAT :, :].astype(F32)
-    before_value = convolve(taps, before_raw, jnp.zeros((VDIM, BLK), F32))
-    before_key = near_ref[STATE_ROWS : STATE_ROWS + FEAT, :]
+    before_raw = pltpu.roll(unfold(near_ref[0:STATE_ROWS, :])[1], LANES - EDGE - 2, 1)
+    halves = near_ref[STATE_ROWS:HALO_ROWS, :].astype(F32)
+    before_value = jnp.concatenate([pltpu.roll(halves, WIN, 1), halves], axis=0).astype(BF16)
+    before_key = near_ref[HALO_ROWS:, :]
     for blk in range(count):
         query = x_ref[blk, 0:FEAT, :]
         key = x_ref[blk, FEAT : 2 * FEAT, :]
@@ -266,19 +311,17 @@
 VMEM = pl.BlockSpec(memory_space=pltpu.VMEM)
 
 
-def call(kernel, outs, scalars, outer_arrays, arrays, aliases=None):
-    limit = None if outer_arrays else 8 * 1024 * 1024
+def call(kernel, outs, scalars, arrays, aliases=None):
     arrays = [pltpu.with_memory_space_constraint(array, pltpu.VMEM) for array in arrays]
-    count = len(outer_arrays) + len(arrays)
     single = len(outs) == 1
     return pl.pallas_call(
         kernel,
         out_shape=outs[0] if single else tuple(outs),
-        in_specs=[SMEM] * len(scalars) + [VMEM] * count,
+        in_specs=[SMEM] * len(scalars) + [VMEM] * len(arrays),
         out_specs=VMEM if single else tuple(VMEM for _ in outs),
         input_output_aliases=aliases or {},
-        compiler_params=pltpu.CompilerParams(vmem_limit_bytes=limit),
-    )(*scalars, *outer_arrays, *arrays)
+        compiler_params=pltpu.CompilerParams(vmem_limit_bytes=8 * 1024 * 1024),
+    )(*scalars, *arrays)
 
 
 def scalar(value):
@@ -294,22 +337,26 @@
     def upward(value):
         return lax.ppermute(value, stack, [(i, i + 1) for i in range(groups - 1)])
 
-    packed, taps = call(
+    rows = [query_rows, key_rows, value_rows, conv_weight, norm_gain.reshape(1, HEADS * VDIM)]
+    packed, taps = pl.pallas_call(
         pack_kernel,
-        [pltpu.VMEM((HEADS, PART, BLK), BF16), pltpu.VMEM((TAPS + 1, VDIM, LANES), F32)],
-        [scalar(lax.axis_index(group))],
-        [query_rows, key_rows, value_rows, conv_weight, norm_gain.reshape(1, HEADS * VDIM)],
-        [],
-    )
+        out_shape=(
+            pltpu.VMEM((HEADS, PART, BLK), BF16),
+            pltpu.VMEM((TAPS + 1, VDIM, LANES), F32),
+        ),
+        in_specs=[SMEM] + [pl.BlockSpec(memory_space=pl.ANY)] * len(rows),
+        out_specs=(VMEM, VMEM),
+        scratch_shapes=[pltpu.VMEM(array.shape, array.dtype) for array in rows]
+        + [pltpu.SemaphoreType.DMA((4 + PIECES,))],
+    )(scalar(lax.axis_index(group)), *rows)
     mine = lax.all_to_all(packed, group, 0, 0)
     sent, own, conv = call(
         state_kernel,
         [
-            pltpu.VMEM((STATE_ROWS + FEAT + VDIM, BLK), BF16),
+            pltpu.VMEM((HALO_ROWS + FEAT, BLK), BF16),
             pltpu.VMEM((2, VDIM, LANES), F32),
             pltpu.VMEM((members, VDIM, BLK), BF16),
         ],
-        [],
         [],
         [mine, taps],
     )
@@ -318,7 +365,6 @@
     sent, pair = call(
         merge_kernel,
         [pltpu.VMEM((STATE_ROWS, LANES), BF16), pltpu.VMEM((2, VDIM, LANES), F32)],
-        [],
         [],
         [own, near, taps],
     )
@@ -333,18 +379,17 @@
 
     def lower(sent):
         recv = lax.ppermute(sent, "quad", [(0, 1), (1, 0)])
-        local = call(lower_local_kernel, local_shapes, [first], [], local_arrays)
+        local = call(lower_local_kernel, local_shapes, [first], local_arrays)
         both, recv = call(
             join_kernel,
             [pltpu.VMEM((STATE_ROWS, LANES), BF16), pltpu.VMEM((STATE_ROWS, LANES), BF16)],
             [scalar(quad)],
-            [],
             [pair, recv, taps],
         )
         return both, recv, *local
 
     def upper(sent):
-        return sent, sent, *call(unwritten_kernel, local_shapes, [], [], [])
+        return sent, sent, *call(unwritten_kernel, local_shapes, [], [])
 
     both, pair_recv, *local = lax.cond(quad < 2, lower, upper, sent)
     low = lax.ppermute(both, "quad", [(1, 2), (0, 3)])
@@ -353,7 +398,6 @@
         upper_local_kernel,
         local_shapes,
         [scalar(quad)],
-        [],
         [*local_arrays, *local],
         {5: 0, 6: 1, 7: 2},
     )
@@ -361,12 +405,11 @@
         final_kernel,
         [pltpu.VMEM((members, *block), BF16)],
         [scalar(quad)],
-        [],
         [pair_recv, below, low, near, taps, num, win, phi],
     )
     heads = lax.all_to_all(done, group, 0, 0)
     out = jax.ShapeDtypeStruct((BLK, HEADS * VDIM), BF16)
-    return call(unpack_kernel, [out], [], [], [heads])
+    return call(unpack_kernel, [out], [], [heads])
 
 
 def solution(mesh):

time: 56 us -> 56.1 us (level)
    pallas_call x0 -> x1, Pallas kernels: none -> 2.65 us  [on_device(): pl.pallas_call(pack_kernel, out_shape=(pltpu.VMEM((HEADS, PART, BLK), BF1...]
    pallas_call x8 -> x7, Pallas kernels: 8.54 us -> 6.21 us  [call(): pl.pallas_call(kernel, out_shape=outs[0] if single else tuple(outs), in_s...]
where the time goes in v9:
time: 56.1 us; the launch traced here: 55.8 us
  blocking collectives  31.5 us (56%)
  starting transfers between devices  14.1 us (25%)
  Pallas kernels  8.86 us (16%)
  waiting for transfers between devices  1.27 us (2%)
    all_to_all x1, blocking collectives, on_device(): mine = lax.all_to_all(packed, group, 0, 0)  18.3 us
    all_to_all x1, blocking collectives, on_device(): heads = lax.all_to_all(done, group, 0, 0)  13.2 us
    ppermute x1, starting transfers between devices, lower(): recv = lax.ppermute(sent, 'quad', [(0, 1), (1, 0)])  9.69 us
    pallas_call x7, Pallas kernels, call(): pl.pallas_call(kernel, out_shape=outs[0] if single else tuple(outs), in_s...  6.21 us
    pallas_call x1, Pallas kernels, on_device(): pl.pallas_call(pack_kernel, out_shape=(pltpu.VMEM((HEADS, PART, BLK), BF1...  2.65 us
    ppermute x1, starting transfers between devices, upward(): return lax.ppermute(value, stack, [(i, i + 1) for i in range(groups - 1)])  2.48 us
    ppermute x1, starting transfers between devices, on_device(): low = lax.ppermute(both, 'quad', [(1, 2), (0, 3)])  1.28 us
  transfers between devices with their start and end apart: 4, of which 2 were waited for; matrix products, arithmetic and copies ran while one was open for 0% of the time, Pallas kernels for 6%

profile of v9, /device:TPU:1, one launch (start us, length us, event | category | flops | bytes accessed | tf_op | source)
XLA Modules:
  0.0 55.8 jit_solution(13519098228667793720)
XLA Ops:
  0.0 2.6 %shard_map.55 = (bf16[16,96,128]{2,1,0:T(8,128)(2,1)S(1)}, f32[4,64,128]{2,1,0:T(8,128)S(1)}) custom-call(s32[1]{0:T(128)} %bitcast.3.head_ref, bf16[128,256]{1,0:T(8,128)(2,1)} %q_hbm.1, bf16[128,256]{1,0:T(8,128)(2,1)} %k_hbm.1, bf16[128,1024]{1,0:T(8,128)(2,1)} %v_hbm.1, f32[3,1024]{1,0:T(4,128)} %w_hbm.1, f32[1,1024]{1,0:T(1,128)} %bitcast.5), custom_call_target="tpu_custom_call" | custom-call | tf_op jit(solution)/shard_map/pallas_call | solution.py:341
  2.7 18.3 %all_to_all.10.x_ref = bf16[16,96,128]{2,1,0:T(8,128)(2,1)S(1)} all-to-all(bf16[16,96,128]{2,1,0:T(8,128)(2,1)S(1)} %get-tuple-element.54), channel_id=1, replica_groups=mesh['dp'=4,'quad'=4,'half'=2,'pair'=2,'core'=2,'inner'=4] {'pair','core..., dimensions={0} | all-to-all | bytes 786432 | tf_op jit(solution)/shard_map/all_to_all | solution.py:352
  20.9 0.7 %shard_map.56 = (bf16[144,128]{1,0:T(8,128)(2,1)S(1)}, f32[2,64,128]{2,1,0:T(8,128)S(1)}, bf16[16,64,128]{2,1,0:T(8,128)(2,1)S(1)}) custom-call(bf16[16,96,128]{2,1,0:T(8,128)(2,1)S(1)} %all_to_all.10.x_ref, f32[4,64,128]{2,1,0:T(8,128)S(1)} %get-tuple-element.55.taps_ref), custom_call_target="tpu_custom_call" | custom-call | tf_op jit(solution)/shard_map/pallas_call | solution.py:317
  21.6 2.5 %collective-permute-start.1 = (bf16[144,128]{1,0:T(8,128)(2,1)S(1)}, bf16[144,128]{1,0:T(8,128)(2,1)S(1)}, u32[]{:S(2)}, u32[]{:S(2)}) collective-permute-start(bf16[144,128]{1,0:T(8,128)(2,1)S(1)} %get-tuple-element.57), channel_id=1, source_target_pairs={{0,16},{16,32},{32,48},{48,64},{64,80},{80,96},{96,112},{1,17},{17... | collective-permute-start | bytes 110600 | tf_op jit(solution)/shard_map/ppermute | solution.py:338
  24.1 1.0 %collective-permute-done.1.near_ref = bf16[144,128]{1,0:T(8,128)(2,1)S(1)} collective-permute-done((bf16[144,128]{1,0:T(8,128)(2,1)S(1)}, bf16[144,128]{1,0:T(8,128)(2,1)S(1)}, u32[]{:S(2)}, u32[]{:S(2)}) %collective-permute-start.1) | collective-permute-done | bytes 36896 | tf_op jit(solution)/shard_map/ppermute | solution.py:338
  25.2 0.3 shard_map.57
  25.5 13.4 %conditional.1 = (bf16[96,128]{1,0:T(8,128)(2,1)S(1)}, bf16[96,128]{1,0:T(8,128)(2,1)S(1)}, f32[16,64,128]{2,1,0:T(8,128)S(1)}, f32[16,64,128]{2,1,0:T(8,128)S(1)}, bf16[160,2048]{1,0:T(8,128)(2,1)S(1)}) conditional(s32[]{:T(128)} %convert_element_type.6, bf16[96,128]{1,0:T(8,128)(2,1)S(1)} %get-tuple-element.58, (s32[]{:T(128)}, ...), branch_computations={%region_0.0_spmd, %region_1.0_spmd} | conditional | bytes 98384 | solution.py:394
  25.5 9.7 %collective-permute-start = (bf16[96,128]{1,0:T(8,128)(2,1)S(1)}, bf16[96,128]{1,0:T(8,128)(2,1)S(1)}, u32[]{:S(2)}, u32[]{:S(2)}) collective-permute-start(bf16[96,128]{1,0:T(8,128)(2,1)S(1)} %get-tuple-element.28), channel_id=1, source_target_pairs={{0,32},{32,0},{1,33},{33,1},{2,34},{34,2},{3,35},{35,3},{4,36},{36... | collective-permute-start | bytes 73736 | tf_op jit(solution)/shard_map/cond/branch_1_fun/ppermute | solution.py:381
  35.2 3.4 %branch_1_fun.3 = (f32[16,64,128]{2,1,0:T(8,128)S(1)}, f32[16,64,128]{2,1,0:T(8,128)S(1)}, bf16[160,2048]{1,0:T(8,128)(2,1)S(1)}) custom-call(s32[1]{0:T(128)} %bitcast.1.first_ref, bf16[16,96,128]{2,1,0:T(8,128)(2,1)S(1)} %get-tuple-element.33.refs_0_, bf16[16,64,128]{2,1,0:T(8,128)(2,1)S(1)} %get-tuple-element.34.refs_1_, ...), custom_call_target="tpu_custom_call" | custom-call | tf_op jit(solution)/shard_map/cond/branch_1_fun/pallas_call | solution.py:317
  38.6 0.0 collective-permute-done.recv_ref
  38.6 0.3 branch_1_fun.2
  39.0 1.3 %collective-permute-start.3 = (bf16[96,128]{1,0:T(8,128)(2,1)S(1)}, bf16[96,128]{1,0:T(8,128)(2,1)S(1)}, u32[]{:S(2)}, u32[]{:S(2)}) collective-permute-start(bf16[96,128]{1,0:T(8,128)(2,1)S(1)} %get-tuple-element.62), channel_id=1, source_target_pairs={{32,64},{0,96},{33,65},{1,97},{34,66},{2,98},{35,67},{3,99},{36,68... | collective-permute-start | bytes 73736 | tf_op jit(solution)/shard_map/ppermute | solution.py:395
  40.2 0.7 %collective-permute-start.2 = (bf16[96,128]{1,0:T(8,128)(2,1)S(1)}, bf16[96,128]{1,0:T(8,128)(2,1)S(1)}, u32[]{:S(2)}, u32[]{:S(2)}) collective-permute-start(bf16[96,128]{1,0:T(8,128)(2,1)S(1)} %get-tuple-element.58), channel_id=1, source_target_pairs={{64,96},{65,97},{66,98},{67,99},{68,100},{69,101},{70,102},{71,103... | collective-permute-start | bytes 73736 | tf_op jit(solution)/shard_map/ppermute | solution.py:396
  40.9 0.2 collective-permute-done.3.low_ref
  41.2 0.0 collective-permute-done.2.below_ref
  41.2 0.6 %shard_map.59 = bf16[16,64,128]{2,1,0:T(8,128)(2,1)S(1)} custom-call(s32[1]{0:T(128)} %bitcast.2.quad_ref, bf16[96,128]{1,0:T(8,128)(2,1)S(1)} %get-tuple-element.61.pair_recv_ref, bf16[96,128]{1,0:T(8,128)(2,1)S(1)} %collective-permute-done.2.below_ref, bf16[96,128]{1,0:T(8,128)(2,1)S(1)} %collective-permute-done.3.low_ref, ...), custom_call_target="tpu_custom_call" | custom-call | tf_op jit(solution)/shard_map/pallas_call | solution.py:317
  41.8 13.2 %all_to_all.11.x_ref = bf16[16,64,128]{2,1,0:T(8,128)(2,1)S(1)} all-to-all(bf16[16,64,128]{2,1,0:T(8,128)(2,1)S(1)} %shard_map.59), channel_id=1, replica_groups=mesh['dp'=4,'quad'=4,'half'=2,'pair'=2,'core'=2,'inner'=4] {'pair','core..., dimensions={0} | all-to-all | bytes 524288 | tf_op jit(solution)/shard_map/all_to_all | solution.py:410
  55.0 0.8 %shard_map.60 = bf16[128,1024]{1,0:T(8,128)(2,1)} custom-call(bf16[16,64,128]{2,1,0:T(8,128)(2,1)S(1)} %all_to_all.11.x_ref), custom_call_target="tpu_custom_call" | custom-call | tf_op jit(solution)/shard_map/pallas_call | solution.py:317
  (1 shorter events, 0.0 us)
Async XLA Ops:
  21.6 3.5 %collective-permute-start.1 = (bf16[144,128]{1,0:T(8,128)(2,1)S(1)}, bf16[144,128]{1,0:T(8,128)(2,1)S(1)}, u32[]{:S(2)}, u32[]{:S(2)}) collective-permute-start(bf16[144,128]{1,0:T(8,128)(2,1)S(1)} %get-tuple-element.57), channel_id=1, source_target_pairs={{0,16},{16,32},{32,48},{48,64},{64,80},{80,96},{96,112},{1,17},{17... | collective-permute-start | bytes 110600 | tf_op jit(solution)/shard_map/ppermute | solution.py:338
  25.5 13.1 %collective-permute-start = (bf16[96,128]{1,0:T(8,128)(2,1)S(1)}, bf16[96,128]{1,0:T(8,128)(2,1)S(1)}, u32[]{:S(2)}, u32[]{:S(2)}) collective-permute-start(bf16[96,128]{1,0:T(8,128)(2,1)S(1)} %get-tuple-element.28), channel_id=1, source_target_pairs={{0,32},{32,0},{1,33},{33,1},{2,34},{34,2},{3,35},{35,3},{4,36},{36... | collective-permute-start | bytes 73736 | tf_op jit(solution)/shard_map/cond/branch_1_fun/ppermute | solution.py:381
  39.0 2.2 %collective-permute-start.3 = (bf16[96,128]{1,0:T(8,128)(2,1)S(1)}, bf16[96,128]{1,0:T(8,128)(2,1)S(1)}, u32[]{:S(2)}, u32[]{:S(2)}) collective-permute-start(bf16[96,128]{1,0:T(8,128)(2,1)S(1)} %get-tuple-element.62), channel_id=1, source_target_pairs={{32,64},{0,96},{33,65},{1,97},{34,66},{2,98},{35,67},{3,99},{36,68... | collective-permute-start | bytes 73736 | tf_op jit(solution)/shard_map/ppermute | solution.py:395
  40.2 0.9 %collective-permute-start.2 = (bf16[96,128]{1,0:T(8,128)(2,1)S(1)}, bf16[96,128]{1,0:T(8,128)(2,1)S(1)}, u32[]{:S(2)}, u32[]{:S(2)}) collective-permute-start(bf16[96,128]{1,0:T(8,128)(2,1)S(1)} %get-tuple-element.58), channel_id=1, source_target_pairs={{64,96},{65,97},{66,98},{67,99},{68,100},{69,101},{70,102},{71,103... | collective-permute-start | bytes 73736 | tf_op jit(solution)/shard_map/ppermute | solution.py:396

commit v10 on v8

--- a/solution.py
+++ b/solution.py
@@ -17,6 +17,7 @@
 EDGE = NPHI - LANES
 HALF = VDIM // 2
 STATE_ROWS = VDIM + HALF
+HALO_ROWS = STATE_ROWS + HALF
 PART = FEAT + FEAT + VDIM
 F32 = jnp.float32
 BF16 = jnp.bfloat16
@@ -101,13 +102,14 @@
     out_ref[:, 0:FEAT, :] = q_ref[...].T.reshape(HEADS, FEAT, BLK)
     out_ref[:, FEAT : 2 * FEAT, :] = k_ref[...].T.reshape(HEADS, FEAT, BLK)
     out_ref[:, 2 * FEAT :, :] = v_ref[...].T.reshape(HEADS, VDIM, BLK)
-    rows = jnp.concatenate([w_ref[...], gain_ref[...], jnp.zeros((4, HEADS * VDIM), F32)], axis=0)
-    mine = jnp.zeros((8, VDIM), F32)
-    for head in range(HEADS):
-        mine = jnp.where(head_ref[0] == head, rows[:, head * VDIM : (head + 1) * VDIM], mine)
-    columns = mine.T
+    head = head_ref[0]
+    start = pl.multiple_of(head // 2 * LANES, LANES)
+    odd = head % 2 == 1
     for index in range(TAPS + 1):
-        taps_ref[index] = jnp.broadcast_to(columns[:, index : index + 1], (VDIM, LANES))
+        source, at = (w_ref, index) if index < TAPS else (gain_ref, 0)
+        row = source[at : at + 1, pl.ds(start, LANES)]
+        both = jnp.broadcast_to(row, (LANES, LANES)).T
+        taps_ref[index] = jnp.where(odd, both[VDIM:], both[:VDIM])
 
 
 def state_kernel(x_ref, taps_ref, sent_ref, own_ref, conv_ref):
@@ -134,7 +136,10 @@
     own_ref[0] = main
     own_ref[1] = rest
     sent_ref[0:STATE_ROWS, :] = fold(main, rest)
-    sent_ref[STATE_ROWS:, :] = x_ref[count - 1, FEAT:, :]
+    wide = conv.astype(F32)
+    upper = pltpu.roll(wide[:HALF], WIN, 1)
+    sent_ref[STATE_ROWS:HALO_ROWS, :] = jnp.where(lanes(HALF) < WIN, upper, wide[HALF:]).astype(BF16)
+    sent_ref[HALO_ROWS:, :] = x_ref[count - 1, FEAT : 2 * FEAT, :]
 
 
 def inside_window(first):
@@ -166,9 +171,10 @@
     inside = inside_window(None)
     state = jnp.zeros((VDIM, NPHI), F32)
     taps = [taps_ref[index] for index in range(TAPS)]
-    before_raw = near_ref[STATE_ROWS + FEAT :, :].astype(F32)
-    before_value = convolve(taps, before_raw, jnp.zeros((VDIM, BLK), F32))
-    before_key = near_ref[STATE_ROWS : STATE_ROWS + FEAT, :]
+    before_raw = pltpu.roll(unfold(near_ref[0:STATE_ROWS, :])[1], LANES - EDGE - 2, 1)
+    halves = near_ref[STATE_ROWS:HALO_ROWS, :].astype(F32)
+    before_value = jnp.concatenate([pltpu.roll(halves, WIN, 1), halves], axis=0).astype(BF16)
+    before_key = near_ref[HALO_ROWS:, :]
     for blk in range(count):
         query = x_ref[blk, 0:FEAT, :]
         key = x_ref[blk, FEAT : 2 * FEAT, :]
@@ -187,12 +193,10 @@
         before_key, before_value = key, value
 
 
-def lower_local_kernel(first_ref, *refs):
-    local_blocks(first_ref, *refs)
-
-
-def unwritten_kernel(num_ref, win_ref, phi_ref):
-    pass
+def second_local_kernel(quad_ref, x_ref, conv_ref, near_ref, taps_ref, *refs):
+    @pl.when(quad_ref[0] == 1)
+    def _():
+        local_blocks(None, x_ref, conv_ref, near_ref, taps_ref, *refs[3:])
 
 
 def upper_local_kernel(quad_ref, x_ref, conv_ref, near_ref, taps_ref, *refs):
@@ -201,7 +205,20 @@
         local_blocks(None, x_ref, conv_ref, near_ref, taps_ref, *refs[3:])
 
 
-def merge_kernel(own_ref, near_ref, taps_ref, sent_ref, pair_ref):
+def merge_kernel(
+    quad_ref,
+    first_ref,
+    own_ref,
+    x_ref,
+    conv_ref,
+    near_ref,
+    taps_ref,
+    sent_ref,
+    pair_ref,
+    num_ref,
+    win_ref,
+    phi_ref,
+):
     main, rest = own_ref[0], own_ref[1]
     near_main, near_rest = unfold(near_ref[0:STATE_ROWS, :])
     edge_main, edge_rest = edge_state(taps_ref, [(rest, near_rest)])
@@ -211,18 +228,26 @@
     pair_ref[1] = rest
     sent_ref[...] = fold(main, rest)
 
+    @pl.when(quad_ref[0] == 0)
+    def _():
+        local_blocks(first_ref, x_ref, conv_ref, near_ref, taps_ref, num_ref, win_ref, phi_ref)
+
 
 def join_kernel(quad_ref, pair_ref, recv_ref, taps_ref, sent_ref, copy_ref):
-    copy_ref[...] = recv_ref[...]
-    lowest = quad_ref[0] == 0
-    main, rest = pair_ref[0], pair_ref[1]
-    recv_main, recv_rest = unfold(recv_ref[...])
-    lower = jnp.where(lowest, rest, recv_rest)
-    upper = jnp.where(lowest, recv_rest, rest)
-    edge_main, edge_rest = edge_state(taps_ref, [(upper, lower)])
-    sent_ref[...] = fold(
-        main + recv_main + edge_main, joined(rest + recv_rest + edge_rest, upper, lower)
-    )
+    @pl.when(quad_ref[0] == 1)
+    def _():
+        main, rest = pair_ref[0], pair_ref[1]
+        recv_main, recv_rest = unfold(recv_ref[...])
+        edge_main, edge_rest = edge_state(taps_ref, [(rest, recv_rest)])
+        copy_ref[...] = recv_ref[...]
+        sent_ref[...] = fold(
+            main + recv_main + edge_main, joined(rest + recv_rest + edge_rest, rest, recv_rest)
+        )
+
+    @pl.when(quad_ref[0] != 1)
+    def _():
+        copy_ref[...] = recv_ref[...]
+        sent_ref[...] = recv_ref[...]
 
 
 def final_kernel(
@@ -244,8 +269,7 @@
     below_main = jnp.where(second, one_main, two_main)
     below_rest = jnp.where(second, one_rest, two_rest)
     low_main, low_rest = unfold(low_ref[...])
-    above_low = jnp.where(quad_ref[0] == 2, near_rest, below_rest)
-    edge_main, edge_rest = edge_state(taps_ref, [(near_rest, below_rest), (above_low, low_rest)])
+    edge_main, edge_rest = edge_state(taps_ref, [(near_rest, below_rest), (below_rest, low_rest)])
     main = near_main + below_main + low_main + edge_main
     rest = near_rest + below_rest + low_rest + edge_rest
     state = jnp.concatenate([main, rest[:, :EDGE]], axis=1).astype(BF16)
@@ -266,19 +290,17 @@
 VMEM = pl.BlockSpec(memory_space=pltpu.VMEM)
 
 
-def call(kernel, outs, scalars, outer_arrays, arrays, aliases=None):
-    limit = None if outer_arrays else 8 * 1024 * 1024
+def call(kernel, outs, scalars, arrays, aliases=None):
     arrays = [pltpu.with_memory_space_constraint(array, pltpu.VMEM) for array in arrays]
-    count = len(outer_arrays) + len(arrays)
     single = len(outs) == 1
     return pl.pallas_call(
         kernel,
         out_shape=outs[0] if single else tuple(outs),
-        in_specs=[SMEM] * len(scalars) + [VMEM] * count,
+        in_specs=[SMEM] * len(scalars) + [VMEM] * len(arrays),
         out_specs=VMEM if single else tuple(VMEM for _ in outs),
         input_output_aliases=aliases or {},
-        compiler_params=pltpu.CompilerParams(vmem_limit_bytes=limit),
-    )(*scalars, *outer_arrays, *arrays)
+        compiler_params=pltpu.CompilerParams(vmem_limit_bytes=8 * 1024 * 1024),
+    )(*scalars, *arrays)
 
 
 def scalar(value):
@@ -294,34 +316,35 @@
     def upward(value):
         return lax.ppermute(value, stack, [(i, i + 1) for i in range(groups - 1)])
 
-    packed, taps = call(
+    packed, taps = pl.pallas_call(
         pack_kernel,
-        [pltpu.VMEM((HEADS, PART, BLK), BF16), pltpu.VMEM((TAPS + 1, VDIM, LANES), F32)],
-        [scalar(lax.axis_index(group))],
-        [query_rows, key_rows, value_rows, conv_weight, norm_gain.reshape(1, HEADS * VDIM)],
-        [],
+        out_shape=(
+            pltpu.VMEM((HEADS, PART, BLK), BF16),
+            pltpu.VMEM((TAPS + 1, VDIM, LANES), F32),
+        ),
+        in_specs=[SMEM] + [VMEM] * 5,
+        out_specs=(VMEM, VMEM),
+    )(
+        scalar(lax.axis_index(group)),
+        query_rows,
+        key_rows,
+        value_rows,
+        conv_weight,
+        norm_gain.reshape(1, HEADS * VDIM),
     )
     mine = lax.all_to_all(packed, group, 0, 0)
     sent, own, conv = call(
         state_kernel,
         [
-            pltpu.VMEM((STATE_ROWS + FEAT + VDIM, BLK), BF16),
+            pltpu.VMEM((HALO_ROWS + FEAT, BLK), BF16),
             pltpu.VMEM((2, VDIM, LANES), F32),
             pltpu.VMEM((members, VDIM, BLK), BF16),
         ],
         [],
-        [],
         [mine, taps],
     )
     near = upward(sent)
     block = (VDIM, BLK)
-    sent, pair = call(
-        merge_kernel,
-        [pltpu.VMEM((STATE_ROWS, LANES), BF16), pltpu.VMEM((2, VDIM, LANES), F32)],
-        [],
-        [],
-        [own, near, taps],
-    )
     quad = lax.axis_index("quad")
     first = scalar(lax.axis_index(stack) == 0)
     local_shapes = [
@@ -330,43 +353,53 @@
         pltpu.VMEM((NPHI, members * BLK), BF16),
     ]
     local_arrays = [mine, conv, near, taps]
-
-    def lower(sent):
-        recv = lax.ppermute(sent, "quad", [(0, 1), (1, 0)])
-        local = call(lower_local_kernel, local_shapes, [first], [], local_arrays)
+    sent, pair, *local = call(
+        merge_kernel,
+        [
+            pltpu.VMEM((STATE_ROWS, LANES), BF16),
+            pltpu.VMEM((2, VDIM, LANES), F32),
+            *local_shapes,
+        ],
+        [scalar(quad), first],
+        [own, *local_arrays],
+    )
+    in_place = {5: 0, 6: 1, 7: 2}
+
+    def lower(sent, *local):
+        recv = lax.ppermute(sent, "quad", [(0, 1)])
+        local = call(
+            second_local_kernel, local_shapes, [scalar(quad)], [*local_arrays, *local], in_place
+        )
         both, recv = call(
             join_kernel,
             [pltpu.VMEM((STATE_ROWS, LANES), BF16), pltpu.VMEM((STATE_ROWS, LANES), BF16)],
             [scalar(quad)],
-            [],
             [pair, recv, taps],
         )
         return both, recv, *local
 
-    def upper(sent):
-        return sent, sent, *call(unwritten_kernel, local_shapes, [], [], [])
-
-    both, pair_recv, *local = lax.cond(quad < 2, lower, upper, sent)
-    low = lax.ppermute(both, "quad", [(1, 2), (0, 3)])
-    below = lax.ppermute(sent, "quad", [(2, 3)])
+    def upper(sent, *local):
+        return sent, sent, *local
+
+    both, pair_recv, *local = lax.cond(quad < 2, lower, upper, sent, *local)
+    low = lax.ppermute(both, "quad", [(1, 3)])
+    below = lax.ppermute(both, "quad", [(1, 2), (2, 3)])
     num, win, phi = call(
         upper_local_kernel,
         local_shapes,
         [scalar(quad)],
-        [],
         [*local_arrays, *local],
-        {5: 0, 6: 1, 7: 2},
+        in_place,
     )
     done = call(
         final_kernel,
         [pltpu.VMEM((members, *block), BF16)],
         [scalar(quad)],
-        [],
         [pair_recv, below, low, near, taps, num, win, phi],
     )
     heads = lax.all_to_all(done, group, 0, 0)
     out = jax.ShapeDtypeStruct((BLK, HEADS * VDIM), BF16)
-    return call(unpack_kernel, [out], [], [], [heads])
+    return call(unpack_kernel, [out], [], [heads])
 
 
 def solution(mesh):

time: 56 us -> 54 us (0.964)
  the two profiles are of different devices: /device:TPU:1 before, /device:TPU:473 now
where the time goes in v10:
time: 54 us; the launch traced here: 53.8 us
  blocking collectives  28.3 us (52%)
  waiting for transfers between devices  14.4 us (27%)
  Pallas kernels  7.16 us (13%)
  starting transfers between devices  3.87 us (7%)
    all_to_all x1, blocking collectives, on_device(): heads = lax.all_to_all(done, group, 0, 0)  14.2 us
    all_to_all x1, blocking collectives, on_device(): mine = lax.all_to_all(packed, group, 0, 0)  14.1 us
    ppermute x1, waiting for transfers between devices, on_device(): low = lax.ppermute(both, 'quad', [(1, 3)])  10.1 us
    pallas_call x5, Pallas kernels, call(): pl.pallas_call(kernel, out_shape=outs[0] if single else tuple(outs), in_s...  5.88 us
    ppermute x1, waiting for transfers between devices, upward(): return lax.ppermute(value, stack, [(i, i + 1) for i in range(groups - 1)])  4.31 us
    ppermute x1, starting transfers between devices, on_device(): low = lax.ppermute(both, 'quad', [(1, 3)])  1.29 us
    ppermute x1, starting transfers between devices, on_device(): below = lax.ppermute(both, 'quad', [(1, 2), (2, 3)])  1.29 us
    ppermute x1, starting transfers between devices, upward(): return lax.ppermute(value, stack, [(i, i + 1) for i in range(groups - 1)])  1.29 us
  transfers between devices with their start and end apart: 3, of which 2 were waited for; matrix products, arithmetic and copies ran while one was open for 0% of the time, Pallas kernels for 6%

profile of v10, /device:TPU:473, one launch (start us, length us, event | category | flops | bytes accessed | tf_op | source)
XLA Modules:
  0.0 53.8 jit_solution(17868028007967554687)
XLA Ops:
  0.0 1.3 %shard_map.55 = (bf16[16,96,128]{2,1,0:T(8,128)(2,1)S(1)}, f32[4,64,128]{2,1,0:T(8,128)S(1)}) custom-call(s32[1]{0:T(128)} %bitcast.3.head_ref, bf16[128,256]{1,0:T(8,128)(2,1)} %q_ref.1, bf16[128,256]{1,0:T(8,128)(2,1)} %k_ref.1, bf16[128,1024]{1,0:T(8,128)(2,1)} %v_ref.1, f32[3,1024]{1,0:T(4,128)} %w_ref.1, f32[1,1024]{1,0:T(1,128)} %bitcast.5), custom_call_target="tpu_custom_call" | custom-call | tf_op jit(solution)/shard_map/pallas_call | solution.py:319
  1.3 14.1 %all_to_all.10.x_ref = bf16[16,96,128]{2,1,0:T(8,128)(2,1)S(1)} all-to-all(bf16[16,96,128]{2,1,0:T(8,128)(2,1)S(1)} %get-tuple-element.70), channel_id=1, replica_groups=mesh['dp'=4,'quad'=4,'half'=2,'pair'=2,'core'=2,'inner'=4] {'pair','core..., dimensions={0} | all-to-all | bytes 786432 | tf_op jit(solution)/shard_map/all_to_all | solution.py:335
  15.4 0.7 %shard_map.56 = (bf16[144,128]{1,0:T(8,128)(2,1)S(1)}, f32[2,64,128]{2,1,0:T(8,128)S(1)}, bf16[16,64,128]{2,1,0:T(8,128)(2,1)S(1)}) custom-call(bf16[16,96,128]{2,1,0:T(8,128)(2,1)S(1)} %all_to_all.10.x_ref, f32[4,64,128]{2,1,0:T(8,128)S(1)} %get-tuple-element.71.taps_ref), custom_call_target="tpu_custom_call" | custom-call | tf_op jit(solution)/shard_map/pallas_call | solution.py:296
  16.1 1.3 %collective-permute-start.1 = (bf16[144,128]{1,0:T(8,128)(2,1)S(1)}, bf16[144,128]{1,0:T(8,128)(2,1)S(1)}, u32[]{:S(2)}, u32[]{:S(2)}) collective-permute-start(bf16[144,128]{1,0:T(8,128)(2,1)S(1)} %get-tuple-element.74), channel_id=1, source_target_pairs={{0,16},{16,32},{32,48},{48,64},{64,80},{80,96},{96,112},{1,17},{17... | collective-permute-start | bytes 110600 | tf_op jit(solution)/shard_map/ppermute | solution.py:317
  17.4 4.3 %collective-permute-done.1.near_ref = bf16[144,128]{1,0:T(8,128)(2,1)S(1)} collective-permute-done((bf16[144,128]{1,0:T(8,128)(2,1)S(1)}, bf16[144,128]{1,0:T(8,128)(2,1)S(1)}, u32[]{:S(2)}, u32[]{:S(2)}) %collective-permute-start.1) | collective-permute-done | bytes 36896 | tf_op jit(solution)/shard_map/ppermute | solution.py:317
  21.7 0.3 shard_map.57
  22.1 1.3 %collective-permute-start.3 = (bf16[96,128]{1,0:T(8,128)(2,1)S(1)}, bf16[96,128]{1,0:T(8,128)(2,1)S(1)}, u32[]{:S(2)}, u32[]{:S(2)}) collective-permute-start(bf16[96,128]{1,0:T(8,128)(2,1)S(1)} %get-tuple-element.81), channel_id=1, source_target_pairs={{32,96},{33,97},{34,98},{35,99},{36,100},{37,101},{38,102},{39,103... | collective-permute-start | bytes 73736 | tf_op jit(solution)/shard_map/ppermute | solution.py:385
  23.4 1.3 %collective-permute-start.2 = (bf16[96,128]{1,0:T(8,128)(2,1)S(1)}, bf16[96,128]{1,0:T(8,128)(2,1)S(1)}, u32[]{:S(2)}, u32[]{:S(2)}) collective-permute-start(bf16[96,128]{1,0:T(8,128)(2,1)S(1)} %get-tuple-element.81), channel_id=1, source_target_pairs={{32,64},{64,96},{33,65},{65,97},{34,66},{66,98},{35,67},{67,99},{3... | collective-permute-start | bytes 73736 | tf_op jit(solution)/shard_map/ppermute | solution.py:386
  24.7 3.4 %shard_map.58 = (f32[16,64,128]{2,1,0:T(8,128)S(1)}, f32[16,64,128]{2,1,0:T(8,128)S(1)}, bf16[160,2048]{1,0:T(8,128)(2,1)S(1)}) custom-call(s32[1]{0:T(128)} %bitcast.1.quad_ref, bf16[16,96,128]{2,1,0:T(8,128)(2,1)S(1)} %all_to_all.10.x_ref, ...), custom_call_target="tpu_custom_call", output_to_operand_aliasing={{0}: (5, {}), {1}: (6, {}), {2}: (7, {})} | custom-call | tf_op jit(solution)/shard_map/pallas_call | solution.py:296
  28.1 10.1 %collective-permute-done.3.low_ref = bf16[96,128]{1,0:T(8,128)(2,1)S(1)} collective-permute-done((bf16[96,128]{1,0:T(8,128)(2,1)S(1)}, bf16[96,128]{1,0:T(8,128)(2,1)S(1)}, u32[]{:S(2)}, u32[]{:S(2)}) %collective-permute-start.3) | collective-permute-done | bytes 24608 | tf_op jit(solution)/shard_map/ppermute | solution.py:385
  38.2 0.0 collective-permute-done.2.below_ref
  38.2 0.6 %shard_map.59 = bf16[16,64,128]{2,1,0:T(8,128)(2,1)S(1)} custom-call(s32[1]{0:T(128)} %bitcast.1.quad_ref, bf16[96,128]{1,0:T(8,128)(2,1)S(1)} %get-tuple-element.80.pair_recv_ref, bf16[96,128]{1,0:T(8,128)(2,1)S(1)} %collective-permute-done.2.below_ref, bf16[96,128]{1,0:T(8,128)(2,1)S(1)} %collective-permute-done.3.low_ref, ...), custom_call_target="tpu_custom_call" | custom-call | tf_op jit(solution)/shard_map/pallas_call | solution.py:296
  38.8 14.2 %all_to_all.11.x_ref = bf16[16,64,128]{2,1,0:T(8,128)(2,1)S(1)} all-to-all(bf16[16,64,128]{2,1,0:T(8,128)(2,1)S(1)} %shard_map.59), channel_id=1, replica_groups=mesh['dp'=4,'quad'=4,'half'=2,'pair'=2,'core'=2,'inner'=4] {'pair','core..., dimensions={0} | all-to-all | bytes 524288 | tf_op jit(solution)/shard_map/all_to_all | solution.py:400
  53.0 0.8 %shard_map.60 = bf16[128,1024]{1,0:T(8,128)(2,1)} custom-call(bf16[16,64,128]{2,1,0:T(8,128)(2,1)S(1)} %all_to_all.11.x_ref), custom_call_target="tpu_custom_call" | custom-call | tf_op jit(solution)/shard_map/pallas_call | solution.py:296
  (2 shorter events, 0.0 us)
Async XLA Ops:
  16.1 5.6 %collective-permute-start.1 = (bf16[144,128]{1,0:T(8,128)(2,1)S(1)}, bf16[144,128]{1,0:T(8,128)(2,1)S(1)}, u32[]{:S(2)}, u32[]{:S(2)}) collective-permute-start(bf16[144,128]{1,0:T(8,128)(2,1)S(1)} %get-tuple-element.74), channel_id=1, source_target_pairs={{0,16},{16,32},{32,48},{48,64},{64,80},{80,96},{96,112},{1,17},{17... | collective-permute-start | bytes 110600 | tf_op jit(solution)/shard_map/ppermute | solution.py:317
  22.1 16.1 %collective-permute-start.3 = (bf16[96,128]{1,0:T(8,128)(2,1)S(1)}, bf16[96,128]{1,0:T(8,128)(2,1)S(1)}, u32[]{:S(2)}, u32[]{:S(2)}) collective-permute-start(bf16[96,128]{1,0:T(8,128)(2,1)S(1)} %get-tuple-element.81), channel_id=1, source_target_pairs={{32,96},{33,97},{34,98},{35,99},{36,100},{37,101},{38,102},{39,103... | collective-permute-start | bytes 73736 | tf_op jit(solution)/shard_map/ppermute | solution.py:385
  23.4 14.8 %collective-permute-start.2 = (bf16[96,128]{1,0:T(8,128)(2,1)S(1)}, bf16[96,128]{1,0:T(8,128)(2,1)S(1)}, u32[]{:S(2)}, u32[]{:S(2)}) collective-permute-start(bf16[96,128]{1,0:T(8,128)(2,1)S(1)} %get-tuple-element.81), channel_id=1, source_target_pairs={{32,64},{64,96},{33,65},{65,97},{34,66},{66,98},{35,67},{67,99},{3... | collective-permute-start | bytes 73736 | tf_op jit(solution)/shard_map/ppermute | solution.py:386

commit v11 on v10

--- a/solution.py
+++ b/solution.py
@@ -193,19 +193,21 @@
         before_key, before_value = key, value
 
 
-def second_local_kernel(quad_ref, x_ref, conv_ref, near_ref, taps_ref, *refs):
-    @pl.when(quad_ref[0] == 1)
-    def _():
-        local_blocks(None, x_ref, conv_ref, near_ref, taps_ref, *refs[3:])
-
-
 def upper_local_kernel(quad_ref, x_ref, conv_ref, near_ref, taps_ref, *refs):
     @pl.when(quad_ref[0] > 1)
     def _():
         local_blocks(None, x_ref, conv_ref, near_ref, taps_ref, *refs[3:])
 
 
-def merge_kernel(
+def paired(own_ref, near_ref, taps_ref):
+    main, rest = own_ref[0], own_ref[1]
+    near_main, near_rest = unfold(near_ref[0:STATE_ROWS, :])
+    edge_main, edge_rest = edge_state(taps_ref, [(rest, near_rest)])
+    main = main + near_main + edge_main
+    return main, joined(rest + near_rest + edge_rest, rest, near_rest)
+
+
+def lowest_kernel(
     quad_ref,
     first_ref,
     own_ref,
@@ -214,47 +216,75 @@
     near_ref,
     taps_ref,
     sent_ref,
+    num_ref,
+    win_ref,
+    phi_ref,
+):
+    @pl.when(quad_ref[0] == 0)
+    def _():
+        sent_ref[...] = fold(*paired(own_ref, near_ref, taps_ref))
+        local_blocks(first_ref, x_ref, conv_ref, near_ref, taps_ref, num_ref, win_ref, phi_ref)
+
+
+def second_kernel(
+    quad_ref,
+    own_ref,
+    x_ref,
+    conv_ref,
+    near_ref,
+    taps_ref,
+    num_in_ref,
+    win_in_ref,
+    phi_in_ref,
+    sent_ref,
     pair_ref,
     num_ref,
     win_ref,
     phi_ref,
 ):
-    main, rest = own_ref[0], own_ref[1]
-    near_main, near_rest = unfold(near_ref[0:STATE_ROWS, :])
-    edge_main, edge_rest = edge_state(taps_ref, [(rest, near_rest)])
-    main = main + near_main + edge_main
-    rest = joined(rest + near_rest + edge_rest, rest, near_rest)
-    pair_ref[0] = main
-    pair_ref[1] = rest
-    sent_ref[...] = fold(main, rest)
-
-    @pl.when(quad_ref[0] == 0)
-    def _():
-        local_blocks(first_ref, x_ref, conv_ref, near_ref, taps_ref, num_ref, win_ref, phi_ref)
-
-
-def join_kernel(quad_ref, pair_ref, recv_ref, taps_ref, sent_ref, copy_ref):
+    @pl.when(quad_ref[0] == 1)
+    def _():
+        main, rest = paired(own_ref, near_ref, taps_ref)
+        pair_ref[0] = main
+        pair_ref[1] = rest
+        sent_ref[...] = fold(main, rest)
+        local_blocks(None, x_ref, conv_ref, near_ref, taps_ref, num_ref, win_ref, phi_ref)
+
+
+def join_kernel(quad_ref, pair_ref, recv_ref, taps_ref, sent_ref):
     @pl.when(quad_ref[0] == 1)
     def _():
         main, rest = pair_ref[0], pair_ref[1]
         recv_main, recv_rest = unfold(recv_ref[...])
         edge_main, edge_rest = edge_state(taps_ref, [(rest, recv_rest)])
-        copy_ref[...] = recv_ref[...]
         sent_ref[...] = fold(
             main + recv_main + edge_main, joined(rest + recv_rest + edge_rest, rest, recv_rest)
         )
 
-    @pl.when(quad_ref[0] != 1)
-    def _():
-        copy_ref[...] = recv_ref[...]
-        sent_ref[...] = recv_ref[...]
+
+def upper_kernel(
+    quad_ref, own_ref, low_ref, second_ref, upper_ref, taps_ref, both_ref, sent_ref, near_ref
+):
+    @pl.when(quad_ref[0] == 0)
+    def _():
+        near_ref[...] = low_ref[...]
+
+    @pl.when(quad_ref[0] == 1)
+    def _():
+        near_ref[...] = second_ref[...]
+        sent_ref[...] = both_ref[...]
+
+    @pl.when(quad_ref[0] > 1)
+    def _():
+        near_ref[...] = upper_ref[...]
+        sent_ref[...] = fold(*paired(own_ref, upper_ref, taps_ref))
 
 
 def final_kernel(
-    quad_ref,
-    pair_recv_ref,
+    zero_to_one_ref,
     below_ref,
-    low_ref,
+    one_to_three_ref,
+    zero_to_three_ref,
     near_ref,
     taps_ref,
     num_ref,
@@ -262,16 +292,17 @@
     phi_ref,
     out_ref,
 ):
-    second = quad_ref[0] == 1
     near_main, near_rest = unfold(near_ref[0:STATE_ROWS, :])
-    one_main, one_rest = unfold(pair_recv_ref[...])
-    two_main, two_rest = unfold(below_ref[...])
-    below_main = jnp.where(second, one_main, two_main)
-    below_rest = jnp.where(second, one_rest, two_rest)
-    low_main, low_rest = unfold(low_ref[...])
-    edge_main, edge_rest = edge_state(taps_ref, [(near_rest, below_rest), (below_rest, low_rest)])
-    main = near_main + below_main + low_main + edge_main
-    rest = near_rest + below_rest + low_rest + edge_rest
+    below = [unfold(ref[...]) for ref in (zero_to_one_ref, below_ref)]
+    below_main = below[0][0] + below[1][0]
+    below_rest = below[0][1] + below[1][1]
+    one_main, one_rest = unfold(one_to_three_ref[...])
+    zero_main, zero_rest = unfold(zero_to_three_ref[...])
+    edge_main, edge_rest = edge_state(
+        taps_ref, [(near_rest, below_rest), (below_rest, one_rest), (one_rest, zero_rest)]
+    )
+    main = near_main + below_main + one_main + zero_main + edge_main
+    rest = near_rest + below_rest + one_rest + zero_rest + edge_rest
     state = jnp.concatenate([main, rest[:, :EDGE]], axis=1).astype(BF16)
     gain = taps_ref[TAPS]
     for blk in range(num_ref.shape[0]):
@@ -312,9 +343,6 @@
     stack = ("quad", "half")
     members = lax.axis_size(group)
     groups = lax.axis_size(stack)
-
-    def upward(value):
-        return lax.ppermute(value, stack, [(i, i + 1) for i in range(groups - 1)])
 
     packed, taps = pl.pallas_call(
         pack_kernel,
@@ -343,59 +371,64 @@
         [],
         [mine, taps],
     )
-    near = upward(sent)
     block = (VDIM, BLK)
-    quad = lax.axis_index("quad")
+    quad = scalar(lax.axis_index("quad"))
     first = scalar(lax.axis_index(stack) == 0)
+    packed_state = pltpu.VMEM((STATE_ROWS, LANES), BF16)
     local_shapes = [
         pltpu.VMEM((members, *block), F32),
         pltpu.VMEM((members, *block), F32),
         pltpu.VMEM((NPHI, members * BLK), BF16),
     ]
-    local_arrays = [mine, conv, near, taps]
-    sent, pair, *local = call(
-        merge_kernel,
-        [
-            pltpu.VMEM((STATE_ROWS, LANES), BF16),
-            pltpu.VMEM((2, VDIM, LANES), F32),
-            *local_shapes,
-        ],
-        [scalar(quad), first],
-        [own, *local_arrays],
-    )
-    in_place = {5: 0, 6: 1, 7: 2}
-
-    def lower(sent, *local):
-        recv = lax.ppermute(sent, "quad", [(0, 1)])
-        local = call(
-            second_local_kernel, local_shapes, [scalar(quad)], [*local_arrays, *local], in_place
-        )
-        both, recv = call(
-            join_kernel,
-            [pltpu.VMEM((STATE_ROWS, LANES), BF16), pltpu.VMEM((STATE_ROWS, LANES), BF16)],
-            [scalar(quad)],
-            [pair, recv, taps],
-        )
-        return both, recv, *local
-
-    def upper(sent, *local):
-        return sent, sent, *local
-
-    both, pair_recv, *local = lax.cond(quad < 2, lower, upper, sent, *local)
-    low = lax.ppermute(both, "quad", [(1, 3)])
-    below = lax.ppermute(both, "quad", [(1, 2), (2, 3)])
+    low_near = lax.ppermute(sent, stack, [(0, 1)])
+    second_near = lax.ppermute(sent, stack, [(1, 2), (2, 3)])
+    upper_near = lax.ppermute(sent, stack, [(i, i + 1) for i in range(3, groups - 1)])
+    lowest, *local = call(
+        lowest_kernel,
+        [packed_state, *local_shapes],
+        [quad, first],
+        [own, mine, conv, low_near, taps],
+    )
+    zero_to_one = lax.ppermute(lowest, "quad", [(0, 1)])
+    second, pair, *local = call(
+        second_kernel,
+        [packed_state, pltpu.VMEM((2, VDIM, LANES), F32), *local_shapes],
+        [quad],
+        [own, mine, conv, second_near, taps, *local],
+        {6: 2, 7: 3, 8: 4},
+    )
+    one_to_three = lax.ppermute(second, "quad", [(1, 3)])
+    zero_to_three = lax.ppermute(lowest, "quad", [(0, 3)])
+    both = call(join_kernel, [packed_state], [quad], [pair, zero_to_one, taps])
+    upper, near = call(
+        upper_kernel,
+        [packed_state, pltpu.VMEM((HALO_ROWS + FEAT, BLK), BF16)],
+        [quad],
+        [own, low_near, second_near, upper_near, taps, both],
+    )
+    below = lax.ppermute(upper, "quad", [(1, 2), (2, 3)])
     num, win, phi = call(
         upper_local_kernel,
         local_shapes,
-        [scalar(quad)],
-        [*local_arrays, *local],
-        in_place,
+        [quad],
+        [mine, conv, near, taps, *local],
+        {5: 0, 6: 1, 7: 2},
     )
     done = call(
         final_kernel,
         [pltpu.VMEM((members, *block), BF16)],
-        [scalar(quad)],
-        [pair_recv, below, low, near, taps, num, win, phi],
+        [],
+        [
+            zero_to_one,
+            below,
+            one_to_three,
+            zero_to_three,
+            near,
+            taps,
+            num,
+            win,
+            phi,
+        ],
     )
     heads = lax.all_to_all(done, group, 0, 0)
     out = jax.ShapeDtypeStruct((BLK, HEADS * VDIM), BF16)

time: 54 us -> 50 us (0.926)
  the two profiles are of different devices: /device:TPU:473 before, /device:TPU:321 now
where the time goes in v11:
time: 50 us; the launch traced here: 49.7 us
  blocking collectives  26.4 us (53%)
  starting transfers between devices  10.4 us (21%)
  Pallas kernels  7.18 us (14%)
  waiting for transfers between devices  5.57 us (11%)
    all_to_all x1, blocking collectives, on_device(): mine = lax.all_to_all(packed, group, 0, 0)  14.1 us
    all_to_all x1, blocking collectives, on_device(): heads = lax.all_to_all(done, group, 0, 0)  12.3 us
    pallas_call x8, Pallas kernels, call(): pl.pallas_call(kernel, out_shape=outs[0] if single else tuple(outs), in_s...  5.9 us
    ppermute x1, waiting for transfers between devices, on_device(): below = lax.ppermute(upper, 'quad', [(1, 2), (2, 3)])  5.15 us
    ppermute x1, starting transfers between devices, on_device(): below = lax.ppermute(upper, 'quad', [(1, 2), (2, 3)])  4 us
    ppermute x1, starting transfers between devices, on_device(): lax.ppermute(sent, stack, [(i, i + 1) for i in range(3, groups - 1)])  3.1 us
    pallas_call x1, Pallas kernels, on_device(): pl.pallas_call(pack_kernel, out_shape=(pltpu.VMEM((HEADS, PART, BLK), BF1...  1.28 us
  transfers between devices with their start and end apart: 7, of which 2 were waited for; matrix products, arithmetic and copies ran while one was open for 0% of the time, Pallas kernels for 8%

profile of v11, /device:TPU:321, one launch (start us, length us, event | category | flops | bytes accessed | tf_op | source)
XLA Modules:
  0.0 49.7 jit_solution(12662042200847870852)
XLA Ops:
  0.0 1.3 %shard_map.55 = (bf16[16,96,128]{2,1,0:T(8,128)(2,1)S(1)}, f32[4,64,128]{2,1,0:T(8,128)S(1)}) custom-call(s32[1]{0:T(128)} %bitcast.2.head_ref, bf16[128,256]{1,0:T(8,128)(2,1)} %q_ref.1, bf16[128,256]{1,0:T(8,128)(2,1)} %k_ref.1, bf16[128,1024]{1,0:T(8,128)(2,1)} %v_ref.1, f32[3,1024]{1,0:T(4,128)} %w_ref.1, f32[1,1024]{1,0:T(1,128)} %bitcast.4), custom_call_target="tpu_custom_call" | custom-call | tf_op jit(solution)/shard_map/pallas_call | solution.py:347
  1.3 14.1 %all_to_all.10.x_ref = bf16[16,96,128]{2,1,0:T(8,128)(2,1)S(1)} all-to-all(bf16[16,96,128]{2,1,0:T(8,128)(2,1)S(1)} %get-tuple-element.24), channel_id=1, replica_groups=mesh['dp'=4,'quad'=4,'half'=2,'pair'=2,'core'=2,'inner'=4] {'pair','core..., dimensions={0} | all-to-all | bytes 786432 | tf_op jit(solution)/shard_map/all_to_all | solution.py:363
  15.4 0.7 %shard_map.56 = (bf16[144,128]{1,0:T(8,128)(2,1)S(1)}, f32[2,64,128]{2,1,0:T(8,128)S(1)}, bf16[16,64,128]{2,1,0:T(8,128)(2,1)S(1)}) custom-call(bf16[16,96,128]{2,1,0:T(8,128)(2,1)S(1)} %all_to_all.10.x_ref, f32[4,64,128]{2,1,0:T(8,128)S(1)} %get-tuple-element.25.taps_ref), custom_call_target="tpu_custom_call" | custom-call | tf_op jit(solution)/shard_map/pallas_call | solution.py:327
  16.1 0.7 %collective-permute-start = (bf16[144,128]{1,0:T(8,128)(2,1)S(1)}, bf16[144,128]{1,0:T(8,128)(2,1)S(1)}, u32[]{:S(2)}, u32[]{:S(2)}) collective-permute-start(bf16[144,128]{1,0:T(8,128)(2,1)S(1)} %get-tuple-element.28), channel_id=1, source_target_pairs={{0,16},{1,17},{2,18},{3,19},{4,20},{5,21},{6,22},{7,23},{8,24},{9,... | collective-permute-start | bytes 110600 | tf_op jit(solution)/shard_map/ppermute | solution.py:383
  16.8 0.7 %collective-permute-start.2 = (bf16[144,128]{1,0:T(8,128)(2,1)S(1)}, bf16[144,128]{1,0:T(8,128)(2,1)S(1)}, u32[]{:S(2)}, u32[]{:S(2)}) collective-permute-start(bf16[144,128]{1,0:T(8,128)(2,1)S(1)} %get-tuple-element.28), channel_id=1, source_target_pairs={{16,32},{32,48},{17,33},{33,49},{18,34},{34,50},{19,35},{35,51},{2... | collective-permute-start | bytes 110600 | tf_op jit(solution)/shard_map/ppermute | solution.py:384
  17.5 3.1 %collective-permute-start.3 = (bf16[144,128]{1,0:T(8,128)(2,1)S(1)}, bf16[144,128]{1,0:T(8,128)(2,1)S(1)}, u32[]{:S(2)}, u32[]{:S(2)}) collective-permute-start(bf16[144,128]{1,0:T(8,128)(2,1)S(1)} %get-tuple-element.28), channel_id=1, source_target_pairs={{48,64},{64,80},{80,96},{96,112},{49,65},{65,81},{81,97},{97,113},... | collective-permute-start | bytes 110600 | tf_op jit(solution)/shard_map/ppermute | solution.py:385
  20.6 0.0 collective-permute-done.near_ref.low_ref
  20.6 0.7 %collective-permute-start.1 = (bf16[96,128]{1,0:T(8,128)(2,1)S(1)}, bf16[96,128]{1,0:T(8,128)(2,1)S(1)}, u32[]{:S(2)}, u32[]{:S(2)}) collective-permute-start(bf16[96,128]{1,0:T(8,128)(2,1)S(1)} %get-tuple-element.29), channel_id=1, source_target_pairs={{0,32},{1,33},{2,34},{3,35},{4,36},{5,37},{6,38},{7,39},{8,40},{9,... | collective-permute-start | bytes 73736 | tf_op jit(solution)/shard_map/ppermute | solution.py:392
  21.3 0.7 %collective-permute-start.6 = (bf16[96,128]{1,0:T(8,128)(2,1)S(1)}, bf16[96,128]{1,0:T(8,128)(2,1)S(1)}, u32[]{:S(2)}, u32[]{:S(2)}) collective-permute-start(bf16[96,128]{1,0:T(8,128)(2,1)S(1)} %get-tuple-element.29), channel_id=1, source_target_pairs={{0,96},{1,97},{2,98},{3,99},{4,100},{5,101},{6,102},{7,103},{8,104... | collective-permute-start | bytes 73736 | tf_op jit(solution)/shard_map/ppermute | solution.py:401
  22.0 0.0 collective-permute-done.2.near_ref.second_ref
  22.0 0.7 %collective-permute-start.5 = (bf16[96,128]{1,0:T(8,128)(2,1)S(1)}, bf16[96,128]{1,0:T(8,128)(2,1)S(1)}, u32[]{:S(2)}, u32[]{:S(2)}) collective-permute-start(bf16[96,128]{1,0:T(8,128)(2,1)S(1)} %get-tuple-element.35), channel_id=1, source_target_pairs={{32,96},{33,97},{34,98},{35,99},{36,100},{37,101},{38,102},{39,103... | collective-permute-start | bytes 73736 | tf_op jit(solution)/shard_map/ppermute | solution.py:400
  22.7 0.0 collective-permute-done.1.recv_ref.zero_to_one_ref
  22.7 0.4 collective-permute-done.3.upper_ref
  23.1 0.3 shard_map.60
  23.4 4.0 %collective-permute-start.4 = (bf16[96,128]{1,0:T(8,128)(2,1)S(1)}, bf16[96,128]{1,0:T(8,128)(2,1)S(1)}, u32[]{:S(2)}, u32[]{:S(2)}) collective-permute-start(bf16[96,128]{1,0:T(8,128)(2,1)S(1)} %get-tuple-element.34), channel_id=1, source_target_pairs={{32,64},{64,96},{33,65},{65,97},{34,66},{66,98},{35,67},{67,99},{3... | collective-permute-start | bytes 73736 | tf_op jit(solution)/shard_map/ppermute | solution.py:409
  27.4 3.4 %shard_map.61 = (f32[16,64,128]{2,1,0:T(8,128)S(1)}, f32[16,64,128]{2,1,0:T(8,128)S(1)}, bf16[160,2048]{1,0:T(8,128)(2,1)S(1)}) custom-call(s32[1]{0:T(128)} %bitcast.quad_ref, bf16[16,96,128]{2,1,0:T(8,128)(2,1)S(1)} %all_to_all.10.x_ref, ...), custom_call_target="tpu_custom_call", output_to_operand_aliasing={{0}: (5, {}), {1}: (6, {}), {2}: (7, {})} | custom-call | tf_op jit(solution)/shard_map/pallas_call | solution.py:327
  30.8 0.0 collective-permute-done.5.one_to_three_ref
  30.9 0.0 collective-permute-done.6.zero_to_three_ref
  30.9 5.1 %collective-permute-done.4.below_ref = bf16[96,128]{1,0:T(8,128)(2,1)S(1)} collective-permute-done((bf16[96,128]{1,0:T(8,128)(2,1)S(1)}, bf16[96,128]{1,0:T(8,128)(2,1)S(1)}, u32[]{:S(2)}, u32[]{:S(2)}) %collective-permute-start.4) | collective-permute-done | bytes 24608 | tf_op jit(solution)/shard_map/ppermute | solution.py:409
  36.0 0.6 %shard_map.62 = bf16[16,64,128]{2,1,0:T(8,128)(2,1)S(1)} custom-call(bf16[96,128]{1,0:T(8,128)(2,1)S(1)} %collective-permute-done.1.recv_ref.zero_to_one_ref, bf16[96,128]{1,0:T(8,128)(2,1)S(1)} %collective-permute-done.4.below_ref, bf16[96,128]{1,0:T(8,128)(2,1)S(1)} %collective-permute-done.5.one_to_three_ref, ...), custom_call_target="tpu_custom_call" | custom-call | tf_op jit(solution)/shard_map/pallas_call | solution.py:327
  36.6 12.3 %all_to_all.11.x_ref = bf16[16,64,128]{2,1,0:T(8,128)(2,1)S(1)} all-to-all(bf16[16,64,128]{2,1,0:T(8,128)(2,1)S(1)} %shard_map.62), channel_id=1, replica_groups=mesh['dp'=4,'quad'=4,'half'=2,'pair'=2,'core'=2,'inner'=4] {'pair','core..., dimensions={0} | all-to-all | bytes 524288 | tf_op jit(solution)/shard_map/all_to_all | solution.py:433
  48.9 0.8 %shard_map.63 = bf16[128,1024]{1,0:T(8,128)(2,1)} custom-call(bf16[16,64,128]{2,1,0:T(8,128)(2,1)S(1)} %all_to_all.11.x_ref), custom_call_target="tpu_custom_call" | custom-call | tf_op jit(solution)/shard_map/pallas_call | solution.py:327
  (3 shorter events, 0.0 us)
Async XLA Ops:
  16.1 4.5 %collective-permute-start = (bf16[144,128]{1,0:T(8,128)(2,1)S(1)}, bf16[144,128]{1,0:T(8,128)(2,1)S(1)}, u32[]{:S(2)}, u32[]{:S(2)}) collective-permute-start(bf16[144,128]{1,0:T(8,128)(2,1)S(1)} %get-tuple-element.28), channel_id=1, source_target_pairs={{0,16},{1,17},{2,18},{3,19},{4,20},{5,21},{6,22},{7,23},{8,24},{9,... | collective-permute-start | bytes 110600 | tf_op jit(solution)/shard_map/ppermute | solution.py:383
  16.8 5.2 %collective-permute-start.2 = (bf16[144,128]{1,0:T(8,128)(2,1)S(1)}, bf16[144,128]{1,0:T(8,128)(2,1)S(1)}, u32[]{:S(2)}, u32[]{:S(2)}) collective-permute-start(bf16[144,128]{1,0:T(8,128)(2,1)S(1)} %get-tuple-element.28), channel_id=1, source_target_pairs={{16,32},{32,48},{17,33},{33,49},{18,34},{34,50},{19,35},{35,51},{2... | collective-permute-start | bytes 110600 | tf_op jit(solution)/shard_map/ppermute | solution.py:384
  17.5 5.6 %collective-permute-start.3 = (bf16[144,128]{1,0:T(8,128)(2,1)S(1)}, bf16[144,128]{1,0:T(8,128)(2,1)S(1)}, u32[]{:S(2)}, u32[]{:S(2)}) collective-permute-start(bf16[144,128]{1,0:T(8,128)(2,1)S(1)} %get-tuple-element.28), channel_id=1, source_target_pairs={{48,64},{64,80},{80,96},{96,112},{49,65},{65,81},{81,97},{97,113},... | collective-permute-start | bytes 110600 | tf_op jit(solution)/shard_map/ppermute | solution.py:385
  20.6 2.0 %collective-permute-start.1 = (bf16[96,128]{1,0:T(8,128)(2,1)S(1)}, bf16[96,128]{1,0:T(8,128)(2,1)S(1)}, u32[]{:S(2)}, u32[]{:S(2)}) collective-permute-start(bf16[96,128]{1,0:T(8,128)(2,1)S(1)} %get-tuple-element.29), channel_id=1, source_target_pairs={{0,32},{1,33},{2,34},{3,35},{4,36},{5,37},{6,38},{7,39},{8,40},{9,... | collective-permute-start | bytes 73736 | tf_op jit(solution)/shard_map/ppermute | solution.py:392
  21.3 9.6 %collective-permute-start.6 = (bf16[96,128]{1,0:T(8,128)(2,1)S(1)}, bf16[96,128]{1,0:T(8,128)(2,1)S(1)}, u32[]{:S(2)}, u32[]{:S(2)}) collective-permute-start(bf16[96,128]{1,0:T(8,128)(2,1)S(1)} %get-tuple-element.29), channel_id=1, source_target_pairs={{0,96},{1,97},{2,98},{3,99},{4,100},{5,101},{6,102},{7,103},{8,104... | collective-permute-start | bytes 73736 | tf_op jit(solution)/shard_map/ppermute | solution.py:401
  22.0 8.9 %collective-permute-start.5 = (bf16[96,128]{1,0:T(8,128)(2,1)S(1)}, bf16[96,128]{1,0:T(8,128)(2,1)S(1)}, u32[]{:S(2)}, u32[]{:S(2)}) collective-permute-start(bf16[96,128]{1,0:T(8,128)(2,1)S(1)} %get-tuple-element.35), channel_id=1, source_target_pairs={{32,96},{33,97},{34,98},{35,99},{36,100},{37,101},{38,102},{39,103... | collective-permute-start | bytes 73736 | tf_op jit(solution)/shard_map/ppermute | solution.py:400
  23.4 12.6 %collective-permute-start.4 = (bf16[96,128]{1,0:T(8,128)(2,1)S(1)}, bf16[96,128]{1,0:T(8,128)(2,1)S(1)}, u32[]{:S(2)}, u32[]{:S(2)}) collective-permute-start(bf16[96,128]{1,0:T(8,128)(2,1)S(1)} %get-tuple-element.34), channel_id=1, source_target_pairs={{32,64},{64,96},{33,65},{65,97},{34,66},{66,98},{35,67},{67,99},{3... | collective-permute-start | bytes 73736 | tf_op jit(solution)/shard_map/ppermute | solution.py:409

commit v12 on v11

--- a/solution.py
+++ b/solution.py
@@ -115,15 +115,16 @@
 def state_kernel(x_ref, taps_ref, sent_ref, own_ref, conv_ref):
     count = x_ref.shape[0]
     taps = [taps_ref[index] for index in range(TAPS)]
-    total = jnp.zeros((VDIM, NPHI), F32)
     before = jnp.zeros((VDIM, BLK), F32)
+    convs, phis = [], []
     for blk in range(count):
         raw = x_ref[blk, 2 * FEAT :, :].astype(F32)
         conv = convolve(taps, raw, before)
         conv_ref[blk] = conv
-        phi = features(x_ref[blk, FEAT : 2 * FEAT, :].astype(F32), True)
-        total = total + nt(conv, phi)
+        convs.append(conv)
+        phis.append(features(x_ref[blk, FEAT : 2 * FEAT, :].astype(F32), True))
         before = raw
+    total = nt(jnp.concatenate(convs, axis=1), jnp.concatenate(phis, axis=1))
     lane = lanes(VDIM)
     blank = jnp.zeros((VDIM, LANES - EDGE), F32)
     rest = jnp.concatenate([total[:, LANES:], blank], axis=1)
@@ -305,9 +306,9 @@
     rest = near_rest + below_rest + one_rest + zero_rest + edge_rest
     state = jnp.concatenate([main, rest[:, :EDGE]], axis=1).astype(BF16)
     gain = taps_ref[TAPS]
+    earlier = nn(state, phi_ref[...])
     for blk in range(num_ref.shape[0]):
-        phi = phi_ref[:, blk * BLK : (blk + 1) * BLK]
-        num = num_ref[blk] + nn(state, phi)
+        num = num_ref[blk] + earlier[:, blk * BLK : (blk + 1) * BLK]
         mean_square = jnp.sum(num * num, axis=0, keepdims=True) * (1.0 / VDIM)
         linear = num * lax.rsqrt(mean_square + 1e-06) * gain
         out_ref[blk] = (linear + win_ref[blk]).astype(BF16)

time: 50 us -> 49.8 us (level)
  the two profiles are of different devices: /device:TPU:321 before, /device:TPU:329 now
where the time goes in v12:
time: 49.8 us; the launch traced here: 49.6 us
  blocking collectives  26.4 us (53%)
  starting transfers between devices  10.4 us (21%)
  Pallas kernels  7.01 us (14%)
  waiting for transfers between devices  5.57 us (11%)
    all_to_all x1, blocking collectives, on_device(): mine = lax.all_to_all(packed, group, 0, 0)  14.1 us
    all_to_all x1, blocking collectives, on_device(): heads = lax.all_to_all(done, group, 0, 0)  12.3 us
    pallas_call x8, Pallas kernels, call(): pl.pallas_call(kernel, out_shape=outs[0] if single else tuple(outs), in_s...  5.73 us
    ppermute x1, waiting for transfers between devices, on_device(): below = lax.ppermute(upper, 'quad', [(1, 2), (2, 3)])  5.15 us
    ppermute x1, starting transfers between devices, on_device(): below = lax.ppermute(upper, 'quad', [(1, 2), (2, 3)])  4.01 us
    ppermute x1, starting transfers between devices, on_device(): lax.ppermute(sent, stack, [(i, i + 1) for i in range(3, groups - 1)])  3.1 us
    pallas_call x1, Pallas kernels, on_device(): pl.pallas_call(pack_kernel, out_shape=(pltpu.VMEM((HEADS, PART, BLK), BF1...  1.28 us
  transfers between devices with their start and end apart: 7, of which 2 were waited for; matrix products, arithmetic and copies ran while one was open for 0% of the time, Pallas kernels for 8%

profile of v12, /device:TPU:329, one launch (start us, length us, event | category | flops | bytes accessed | tf_op | source)
XLA Modules:
  0.0 49.6 jit_solution(8026470284280605923)
XLA Ops:
  0.0 1.3 %shard_map.55 = (bf16[16,96,128]{2,1,0:T(8,128)(2,1)S(1)}, f32[4,64,128]{2,1,0:T(8,128)S(1)}) custom-call(s32[1]{0:T(128)} %bitcast.2.head_ref, bf16[128,256]{1,0:T(8,128)(2,1)} %q_ref.1, bf16[128,256]{1,0:T(8,128)(2,1)} %k_ref.1, bf16[128,1024]{1,0:T(8,128)(2,1)} %v_ref.1, f32[3,1024]{1,0:T(4,128)} %w_ref.1, f32[1,1024]{1,0:T(1,128)} %bitcast.4), custom_call_target="tpu_custom_call" | custom-call | tf_op jit(solution)/shard_map/pallas_call | solution.py:348
  1.3 14.1 %all_to_all.10.x_ref = bf16[16,96,128]{2,1,0:T(8,128)(2,1)S(1)} all-to-all(bf16[16,96,128]{2,1,0:T(8,128)(2,1)S(1)} %get-tuple-element.24), channel_id=1, replica_groups=mesh['dp'=4,'quad'=4,'half'=2,'pair'=2,'core'=2,'inner'=4] {'pair','core..., dimensions={0} | all-to-all | bytes 786432 | tf_op jit(solution)/shard_map/all_to_all | solution.py:364
  15.4 0.6 %shard_map.56 = (bf16[144,128]{1,0:T(8,128)(2,1)S(1)}, f32[2,64,128]{2,1,0:T(8,128)S(1)}, bf16[16,64,128]{2,1,0:T(8,128)(2,1)S(1)}) custom-call(bf16[16,96,128]{2,1,0:T(8,128)(2,1)S(1)} %all_to_all.10.x_ref, f32[4,64,128]{2,1,0:T(8,128)S(1)} %get-tuple-element.25.taps_ref), custom_call_target="tpu_custom_call" | custom-call | tf_op jit(solution)/shard_map/pallas_call | solution.py:328
  16.0 0.7 %collective-permute-start = (bf16[144,128]{1,0:T(8,128)(2,1)S(1)}, bf16[144,128]{1,0:T(8,128)(2,1)S(1)}, u32[]{:S(2)}, u32[]{:S(2)}) collective-permute-start(bf16[144,128]{1,0:T(8,128)(2,1)S(1)} %get-tuple-element.28), channel_id=1, source_target_pairs={{0,16},{1,17},{2,18},{3,19},{4,20},{5,21},{6,22},{7,23},{8,24},{9,... | collective-permute-start | bytes 110600 | tf_op jit(solution)/shard_map/ppermute | solution.py:384
  16.7 0.7 %collective-permute-start.2 = (bf16[144,128]{1,0:T(8,128)(2,1)S(1)}, bf16[144,128]{1,0:T(8,128)(2,1)S(1)}, u32[]{:S(2)}, u32[]{:S(2)}) collective-permute-start(bf16[144,128]{1,0:T(8,128)(2,1)S(1)} %get-tuple-element.28), channel_id=1, source_target_pairs={{16,32},{32,48},{17,33},{33,49},{18,34},{34,50},{19,35},{35,51},{2... | collective-permute-start | bytes 110600 | tf_op jit(solution)/shard_map/ppermute | solution.py:385
  17.4 3.1 %collective-permute-start.3 = (bf16[144,128]{1,0:T(8,128)(2,1)S(1)}, bf16[144,128]{1,0:T(8,128)(2,1)S(1)}, u32[]{:S(2)}, u32[]{:S(2)}) collective-permute-start(bf16[144,128]{1,0:T(8,128)(2,1)S(1)} %get-tuple-element.28), channel_id=1, source_target_pairs={{48,64},{64,80},{80,96},{96,112},{49,65},{65,81},{81,97},{97,113},... | collective-permute-start | bytes 110600 | tf_op jit(solution)/shard_map/ppermute | solution.py:386
  20.5 0.0 collective-permute-done.near_ref.low_ref
  20.5 0.7 %collective-permute-start.1 = (bf16[96,128]{1,0:T(8,128)(2,1)S(1)}, bf16[96,128]{1,0:T(8,128)(2,1)S(1)}, u32[]{:S(2)}, u32[]{:S(2)}) collective-permute-start(bf16[96,128]{1,0:T(8,128)(2,1)S(1)} %get-tuple-element.29), channel_id=1, source_target_pairs={{0,32},{1,33},{2,34},{3,35},{4,36},{5,37},{6,38},{7,39},{8,40},{9,... | collective-permute-start | bytes 73736 | tf_op jit(solution)/shard_map/ppermute | solution.py:393
  21.2 0.7 %collective-permute-start.6 = (bf16[96,128]{1,0:T(8,128)(2,1)S(1)}, bf16[96,128]{1,0:T(8,128)(2,1)S(1)}, u32[]{:S(2)}, u32[]{:S(2)}) collective-permute-start(bf16[96,128]{1,0:T(8,128)(2,1)S(1)} %get-tuple-element.29), channel_id=1, source_target_pairs={{0,96},{1,97},{2,98},{3,99},{4,100},{5,101},{6,102},{7,103},{8,104... | collective-permute-start | bytes 73736 | tf_op jit(solution)/shard_map/ppermute | solution.py:402
  21.8 0.0 collective-permute-done.2.near_ref.second_ref
  21.9 0.7 %collective-permute-start.5 = (bf16[96,128]{1,0:T(8,128)(2,1)S(1)}, bf16[96,128]{1,0:T(8,128)(2,1)S(1)}, u32[]{:S(2)}, u32[]{:S(2)}) collective-permute-start(bf16[96,128]{1,0:T(8,128)(2,1)S(1)} %get-tuple-element.35), channel_id=1, source_target_pairs={{32,96},{33,97},{34,98},{35,99},{36,100},{37,101},{38,102},{39,103... | collective-permute-start | bytes 73736 | tf_op jit(solution)/shard_map/ppermute | solution.py:401
  22.5 0.0 collective-permute-done.1.recv_ref.zero_to_one_ref
  22.6 0.4 collective-permute-done.3.upper_ref
  23.0 0.3 shard_map.60
  23.3 4.0 %collective-permute-start.4 = (bf16[96,128]{1,0:T(8,128)(2,1)S(1)}, bf16[96,128]{1,0:T(8,128)(2,1)S(1)}, u32[]{:S(2)}, u32[]{:S(2)}) collective-permute-start(bf16[96,128]{1,0:T(8,128)(2,1)S(1)} %get-tuple-element.34), channel_id=1, source_target_pairs={{32,64},{64,96},{33,65},{65,97},{34,66},{66,98},{35,67},{67,99},{3... | collective-permute-start | bytes 73736 | tf_op jit(solution)/shard_map/ppermute | solution.py:410
  27.3 3.4 %shard_map.61 = (f32[16,64,128]{2,1,0:T(8,128)S(1)}, f32[16,64,128]{2,1,0:T(8,128)S(1)}, bf16[160,2048]{1,0:T(8,128)(2,1)S(1)}) custom-call(s32[1]{0:T(128)} %bitcast.quad_ref, bf16[16,96,128]{2,1,0:T(8,128)(2,1)S(1)} %all_to_all.10.x_ref, ...), custom_call_target="tpu_custom_call", output_to_operand_aliasing={{0}: (5, {}), {1}: (6, {}), {2}: (7, {})} | custom-call | tf_op jit(solution)/shard_map/pallas_call | solution.py:328
  30.7 0.0 collective-permute-done.5.one_to_three_ref
  30.7 0.0 collective-permute-done.6.zero_to_three_ref
  30.7 5.1 %collective-permute-done.4.below_ref = bf16[96,128]{1,0:T(8,128)(2,1)S(1)} collective-permute-done((bf16[96,128]{1,0:T(8,128)(2,1)S(1)}, bf16[96,128]{1,0:T(8,128)(2,1)S(1)}, u32[]{:S(2)}, u32[]{:S(2)}) %collective-permute-start.4) | collective-permute-done | bytes 24608 | tf_op jit(solution)/shard_map/ppermute | solution.py:410
  35.9 0.5 %shard_map.62 = bf16[16,64,128]{2,1,0:T(8,128)(2,1)S(1)} custom-call(bf16[96,128]{1,0:T(8,128)(2,1)S(1)} %collective-permute-done.1.recv_ref.zero_to_one_ref, bf16[96,128]{1,0:T(8,128)(2,1)S(1)} %collective-permute-done.4.below_ref, bf16[96,128]{1,0:T(8,128)(2,1)S(1)} %collective-permute-done.5.one_to_three_ref, ...), custom_call_target="tpu_custom_call" | custom-call | tf_op jit(solution)/shard_map/pallas_call | solution.py:328
  36.5 12.3 %all_to_all.11.x_ref = bf16[16,64,128]{2,1,0:T(8,128)(2,1)S(1)} all-to-all(bf16[16,64,128]{2,1,0:T(8,128)(2,1)S(1)} %shard_map.62), channel_id=1, replica_groups=mesh['dp'=4,'quad'=4,'half'=2,'pair'=2,'core'=2,'inner'=4] {'pair','core..., dimensions={0} | all-to-all | bytes 524288 | tf_op jit(solution)/shard_map/all_to_all | solution.py:434
  48.7 0.8 %shard_map.63 = bf16[128,1024]{1,0:T(8,128)(2,1)} custom-call(bf16[16,64,128]{2,1,0:T(8,128)(2,1)S(1)} %all_to_all.11.x_ref), custom_call_target="tpu_custom_call" | custom-call | tf_op jit(solution)/shard_map/pallas_call | solution.py:328
  (3 shorter events, 0.0 us)
Async XLA Ops:
  16.0 4.5 %collective-permute-start = (bf16[144,128]{1,0:T(8,128)(2,1)S(1)}, bf16[144,128]{1,0:T(8,128)(2,1)S(1)}, u32[]{:S(2)}, u32[]{:S(2)}) collective-permute-start(bf16[144,128]{1,0:T(8,128)(2,1)S(1)} %get-tuple-element.28), channel_id=1, source_target_pairs={{0,16},{1,17},{2,18},{3,19},{4,20},{5,21},{6,22},{7,23},{8,24},{9,... | collective-permute-start | bytes 110600 | tf_op jit(solution)/shard_map/ppermute | solution.py:384
  16.7 5.2 %collective-permute-start.2 = (bf16[144,128]{1,0:T(8,128)(2,1)S(1)}, bf16[144,128]{1,0:T(8,128)(2,1)S(1)}, u32[]{:S(2)}, u32[]{:S(2)}) collective-permute-start(bf16[144,128]{1,0:T(8,128)(2,1)S(1)} %get-tuple-element.28), channel_id=1, source_target_pairs={{16,32},{32,48},{17,33},{33,49},{18,34},{34,50},{19,35},{35,51},{2... | collective-permute-start | bytes 110600 | tf_op jit(solution)/shard_map/ppermute | solution.py:385
  17.4 5.6 %collective-permute-start.3 = (bf16[144,128]{1,0:T(8,128)(2,1)S(1)}, bf16[144,128]{1,0:T(8,128)(2,1)S(1)}, u32[]{:S(2)}, u32[]{:S(2)}) collective-permute-start(bf16[144,128]{1,0:T(8,128)(2,1)S(1)} %get-tuple-element.28), channel_id=1, source_target_pairs={{48,64},{64,80},{80,96},{96,112},{49,65},{65,81},{81,97},{97,113},... | collective-permute-start | bytes 110600 | tf_op jit(solution)/shard_map/ppermute | solution.py:386
  20.5 2.0 %collective-permute-start.1 = (bf16[96,128]{1,0:T(8,128)(2,1)S(1)}, bf16[96,128]{1,0:T(8,128)(2,1)S(1)}, u32[]{:S(2)}, u32[]{:S(2)}) collective-permute-start(bf16[96,128]{1,0:T(8,128)(2,1)S(1)} %get-tuple-element.29), channel_id=1, source_target_pairs={{0,32},{1,33},{2,34},{3,35},{4,36},{5,37},{6,38},{7,39},{8,40},{9,... | collective-permute-start | bytes 73736 | tf_op jit(solution)/shard_map/ppermute | solution.py:393
  21.2 9.6 %collective-permute-start.6 = (bf16[96,128]{1,0:T(8,128)(2,1)S(1)}, bf16[96,128]{1,0:T(8,128)(2,1)S(1)}, u32[]{:S(2)}, u32[]{:S(2)}) collective-permute-start(bf16[96,128]{1,0:T(8,128)(2,1)S(1)} %get-tuple-element.29), channel_id=1, source_target_pairs={{0,96},{1,97},{2,98},{3,99},{4,100},{5,101},{6,102},{7,103},{8,104... | collective-permute-start | bytes 73736 | tf_op jit(solution)/shard_map/ppermute | solution.py:402
  21.9 8.9 %collective-permute-start.5 = (bf16[96,128]{1,0:T(8,128)(2,1)S(1)}, bf16[96,128]{1,0:T(8,128)(2,1)S(1)}, u32[]{:S(2)}, u32[]{:S(2)}) collective-permute-start(bf16[96,128]{1,0:T(8,128)(2,1)S(1)} %get-tuple-element.35), channel_id=1, source_target_pairs={{32,96},{33,97},{34,98},{35,99},{36,100},{37,101},{38,102},{39,103... | collective-permute-start | bytes 73736 | tf_op jit(solution)/shard_map/ppermute | solution.py:401
  23.3 12.6 %collective-permute-start.4 = (bf16[96,128]{1,0:T(8,128)(2,1)S(1)}, bf16[96,128]{1,0:T(8,128)(2,1)S(1)}, u32[]{:S(2)}, u32[]{:S(2)}) collective-permute-start(bf16[96,128]{1,0:T(8,128)(2,1)S(1)} %get-tuple-element.34), channel_id=1, source_target_pairs={{32,64},{64,96},{33,65},{65,97},{34,66},{66,98},{35,67},{67,99},{3... | collective-permute-start | bytes 73736 | tf_op jit(solution)/shard_map/ppermute | solution.py:410

commit v13 on v12

--- a/solution.py
+++ b/solution.py
@@ -112,7 +112,7 @@
         taps_ref[index] = jnp.where(odd, both[VDIM:], both[:VDIM])
 
 
-def state_kernel(x_ref, taps_ref, sent_ref, own_ref, conv_ref):
+def state_kernel(x_ref, taps_ref, sent_ref, again_ref, own_ref, conv_ref):
     count = x_ref.shape[0]
     taps = [taps_ref[index] for index in range(TAPS)]
     before = jnp.zeros((VDIM, BLK), F32)
@@ -141,6 +141,7 @@
     upper = pltpu.roll(wide[:HALF], WIN, 1)
     sent_ref[STATE_ROWS:HALO_ROWS, :] = jnp.where(lanes(HALF) < WIN, upper, wide[HALF:]).astype(BF16)
     sent_ref[HALO_ROWS:, :] = x_ref[count - 1, FEAT : 2 * FEAT, :]
+    again_ref[...] = sent_ref[...]
 
 
 def inside_window(first):
@@ -223,8 +224,12 @@
 ):
     @pl.when(quad_ref[0] == 0)
     def _():
-        sent_ref[...] = fold(*paired(own_ref, near_ref, taps_ref))
+        sent_ref[0:STATE_ROWS] = fold(*paired(own_ref, near_ref, taps_ref))
         local_blocks(first_ref, x_ref, conv_ref, near_ref, taps_ref, num_ref, win_ref, phi_ref)
+
+
+def hand_on_kernel(value_ref, after_ref, out_ref):
+    pass
 
 
 def second_kernel(
@@ -256,7 +261,7 @@
     @pl.when(quad_ref[0] == 1)
     def _():
         main, rest = pair_ref[0], pair_ref[1]
-        recv_main, recv_rest = unfold(recv_ref[...])
+        recv_main, recv_rest = unfold(recv_ref[0:STATE_ROWS])
         edge_main, edge_rest = edge_state(taps_ref, [(rest, recv_rest)])
         sent_ref[...] = fold(
             main + recv_main + edge_main, joined(rest + recv_rest + edge_rest, rest, recv_rest)
@@ -294,11 +299,11 @@
     out_ref,
 ):
     near_main, near_rest = unfold(near_ref[0:STATE_ROWS, :])
-    below = [unfold(ref[...]) for ref in (zero_to_one_ref, below_ref)]
+    below = [unfold(ref[0:STATE_ROWS]) for ref in (zero_to_one_ref, below_ref)]
     below_main = below[0][0] + below[1][0]
     below_rest = below[0][1] + below[1][1]
     one_main, one_rest = unfold(one_to_three_ref[...])
-    zero_main, zero_rest = unfold(zero_to_three_ref[...])
+    zero_main, zero_rest = unfold(zero_to_three_ref[0:STATE_ROWS])
     edge_main, edge_rest = edge_state(
         taps_ref, [(near_rest, below_rest), (below_rest, one_rest), (one_rest, zero_rest)]
     )
@@ -362,9 +367,10 @@
         norm_gain.reshape(1, HEADS * VDIM),
     )
     mine = lax.all_to_all(packed, group, 0, 0)
-    sent, own, conv = call(
+    sent, again, own, conv = call(
         state_kernel,
         [
+            pltpu.VMEM((HALO_ROWS + FEAT, BLK), BF16),
             pltpu.VMEM((HALO_ROWS + FEAT, BLK), BF16),
             pltpu.VMEM((2, VDIM, LANES), F32),
             pltpu.VMEM((members, VDIM, BLK), BF16),
@@ -383,14 +389,17 @@
     ]
     low_near = lax.ppermute(sent, stack, [(0, 1)])
     second_near = lax.ppermute(sent, stack, [(1, 2), (2, 3)])
-    upper_near = lax.ppermute(sent, stack, [(i, i + 1) for i in range(3, groups - 1)])
     lowest, *local = call(
         lowest_kernel,
-        [packed_state, *local_shapes],
+        [pltpu.VMEM((144, BLK), BF16), *local_shapes],
         [quad, first],
         [own, mine, conv, low_near, taps],
     )
     zero_to_one = lax.ppermute(lowest, "quad", [(0, 1)])
+    again = call(
+        hand_on_kernel, [pltpu.VMEM((HALO_ROWS + FEAT, BLK), BF16)], [], [again, lowest], {0: 0}
+    )
+    upper_near = lax.ppermute(again, stack, [(i, i + 1) for i in range(3, groups - 1)])
     second, pair, *local = call(
         second_kernel,
         [packed_state, pltpu.VMEM((2, VDIM, LANES), F32), *local_shapes],

time: 49.8 us -> 49.9 us (level)
  the two profiles are of different devices: /device:TPU:329 before, /device:TPU:1 now
where the time goes in v13:
time: 49.9 us; the launch traced here: 49.6 us
  blocking collectives  29 us (58%)
  starting transfers between devices  11.7 us (23%)
  Pallas kernels  6.83 us (14%)
  waiting for transfers between devices  1.9 us (4%)
    all_to_all x1, blocking collectives, on_device(): mine = lax.all_to_all(packed, group, 0, 0)  18.3 us
    all_to_all x1, blocking collectives, on_device(): heads = lax.all_to_all(done, group, 0, 0)  10.7 us
    pallas_call x9, Pallas kernels, call(): pl.pallas_call(kernel, out_shape=outs[0] if single else tuple(outs), in_s...  5.55 us
    ppermute x1, starting transfers between devices, on_device(): zero_to_one = lax.ppermute(lowest, 'quad', [(0, 1)])  4.96 us
    ppermute x1, starting transfers between devices, on_device(): low_near = lax.ppermute(sent, stack, [(0, 1)])  2.48 us
    ppermute x1, starting transfers between devices, on_device(): zero_to_three = lax.ppermute(lowest, 'quad', [(0, 3)])  1.61 us
    ppermute x1, waiting for transfers between devices, on_device(): zero_to_three = lax.ppermute(lowest, 'quad', [(0, 3)])  1.52 us
    pallas_call x1, Pallas kernels, on_device(): pl.pallas_call(pack_kernel, out_shape=(pltpu.VMEM((HEADS, PART, BLK), BF1...  1.28 us
  transfers between devices with their start and end apart: 7, of which 2 were waited for; matrix products, arithmetic and copies ran while one was open for 0% of the time, Pallas kernels for 7%

profile of v13, /device:TPU:1, one launch (start us, length us, event | category | flops | bytes accessed | tf_op | source)
XLA Modules:
  0.0 49.6 jit_solution(14910960429874696338)
XLA Ops:
  0.0 1.3 %shard_map.55 = (bf16[16,96,128]{2,1,0:T(8,128)(2,1)S(1)}, f32[4,64,128]{2,1,0:T(8,128)S(1)}) custom-call(s32[1]{0:T(128)} %bitcast.2.head_ref, bf16[128,256]{1,0:T(8,128)(2,1)} %q_ref.1, bf16[128,256]{1,0:T(8,128)(2,1)} %k_ref.1, bf16[128,1024]{1,0:T(8,128)(2,1)} %v_ref.1, f32[3,1024]{1,0:T(4,128)} %w_ref.1, f32[1,1024]{1,0:T(1,128)} %bitcast.4), custom_call_target="tpu_custom_call" | custom-call | tf_op jit(solution)/shard_map/pallas_call | solution.py:353
  1.3 18.3 %all_to_all.10.x_ref = bf16[16,96,128]{2,1,0:T(8,128)(2,1)S(1)} all-to-all(bf16[16,96,128]{2,1,0:T(8,128)(2,1)S(1)} %get-tuple-element.25), channel_id=1, replica_groups=mesh['dp'=4,'quad'=4,'half'=2,'pair'=2,'core'=2,'inner'=4] {'pair','core..., dimensions={0} | all-to-all | bytes 786432 | tf_op jit(solution)/shard_map/all_to_all | solution.py:369
  19.6 0.6 %shard_map.56 = (bf16[144,128]{1,0:T(8,128)(2,1)S(1)}, bf16[144,128]{1,0:T(8,128)(2,1)S(1)}, f32[2,64,128]{2,1,0:T(8,128)S(1)}, bf16[16,64,128]{2,1,0:T(8,128)(2,1)S(1)}) custom-call(bf16[16,96,128]{2,1,0:T(8,128)(2,1)S(1)} %all_to_all.10.x_ref, f32[4,64,128]{2,1,0:T(8,128)S(1)} %get-tuple-element.26.taps_ref), custom_call_target="tpu_custom_call" | custom-call | tf_op jit(solution)/shard_map/pallas_call | solution.py:333
  20.2 2.5 %collective-permute-start = (bf16[144,128]{1,0:T(8,128)(2,1)S(1)}, bf16[144,128]{1,0:T(8,128)(2,1)S(1)}, u32[]{:S(2)}, u32[]{:S(2)}) collective-permute-start(bf16[144,128]{1,0:T(8,128)(2,1)S(1)} %get-tuple-element.29), channel_id=1, source_target_pairs={{0,16},{1,17},{2,18},{3,19},{4,20},{5,21},{6,22},{7,23},{8,24},{9,... | collective-permute-start | bytes 110600 | tf_op jit(solution)/shard_map/ppermute | solution.py:390
  22.7 0.7 %collective-permute-start.2 = (bf16[144,128]{1,0:T(8,128)(2,1)S(1)}, bf16[144,128]{1,0:T(8,128)(2,1)S(1)}, u32[]{:S(2)}, u32[]{:S(2)}) collective-permute-start(bf16[144,128]{1,0:T(8,128)(2,1)S(1)} %get-tuple-element.29), channel_id=1, source_target_pairs={{16,32},{32,48},{17,33},{33,49},{18,34},{34,50},{19,35},{35,51},{2... | collective-permute-start | bytes 110600 | tf_op jit(solution)/shard_map/ppermute | solution.py:391
  23.3 0.4 collective-permute-done.near_ref.low_ref
  23.7 3.5 %shard_map.57 = (bf16[144,128]{1,0:T(8,128)(2,1)S(1)}, f32[16,64,128]{2,1,0:T(8,128)S(1)}, f32[16,64,128]{2,1,0:T(8,128)S(1)}, bf16[160,2048]{1,0:T(8,128)(2,1)S(1)}) custom-call(s32[1]{0:T(128)} %bitcast.quad_ref, s32[1]{0:T(128)} %bitcast.1.first_ref, f32[2,64,128]{2,1,0:T(8,128)S(1)} %get-tuple-element.27.own_ref, ...), custom_call_target="tpu_custom_call" | custom-call | tf_op jit(solution)/shard_map/pallas_call | solution.py:333
  27.2 5.0 %collective-permute-start.1 = (bf16[144,128]{1,0:T(8,128)(2,1)S(1)}, bf16[144,128]{1,0:T(8,128)(2,1)S(1)}, u32[]{:S(2)}, u32[]{:S(2)}) collective-permute-start(bf16[144,128]{1,0:T(8,128)(2,1)S(1)} %get-tuple-element.30.after_ref), channel_id=1, source_target_pairs={{0,32},{1,33},{2,34},{3,35},{4,36},{5,37},{6,38},{7,39},{8,40},{9,... | collective-permute-start | bytes 110600 | tf_op jit(solution)/shard_map/ppermute | solution.py:398
  32.2 0.7 %collective-permute-start.3 = (bf16[144,128]{1,0:T(8,128)(2,1)S(1)}, bf16[144,128]{1,0:T(8,128)(2,1)S(1)}, u32[]{:S(2)}, u32[]{:S(2)}) collective-permute-start(bf16[144,128]{1,0:T(8,128)(2,1)S(1)} %shard_map.58), channel_id=1, source_target_pairs={{48,64},{64,80},{80,96},{96,112},{49,65},{65,81},{81,97},{97,113},... | collective-permute-start | bytes 110600 | tf_op jit(solution)/shard_map/ppermute | solution.py:402
  32.9 1.6 %collective-permute-start.6 = (bf16[144,128]{1,0:T(8,128)(2,1)S(1)}, bf16[144,128]{1,0:T(8,128)(2,1)S(1)}, u32[]{:S(2)}, u32[]{:S(2)}) collective-permute-start(bf16[144,128]{1,0:T(8,128)(2,1)S(1)} %get-tuple-element.30.after_ref), channel_id=1, source_target_pairs={{0,96},{1,97},{2,98},{3,99},{4,100},{5,101},{6,102},{7,103},{8,104... | collective-permute-start | bytes 110600 | tf_op jit(solution)/shard_map/ppermute | solution.py:411
  34.5 0.0 collective-permute-done.2.near_ref.second_ref
  34.5 0.7 %collective-permute-start.5 = (bf16[96,128]{1,0:T(8,128)(2,1)S(1)}, bf16[96,128]{1,0:T(8,128)(2,1)S(1)}, u32[]{:S(2)}, u32[]{:S(2)}) collective-permute-start(bf16[96,128]{1,0:T(8,128)(2,1)S(1)} %get-tuple-element.37), channel_id=1, source_target_pairs={{32,96},{33,97},{34,98},{35,99},{36,100},{37,101},{38,102},{39,103... | collective-permute-start | bytes 73736 | tf_op jit(solution)/shard_map/ppermute | solution.py:410
  35.2 0.0 collective-permute-done.1.recv_ref.zero_to_one_ref
  35.2 0.0 collective-permute-done.3.upper_ref
  35.3 0.7 %collective-permute-start.4 = (bf16[96,128]{1,0:T(8,128)(2,1)S(1)}, bf16[96,128]{1,0:T(8,128)(2,1)S(1)}, u32[]{:S(2)}, u32[]{:S(2)}) collective-permute-start(bf16[96,128]{1,0:T(8,128)(2,1)S(1)} %get-tuple-element.36), channel_id=1, source_target_pairs={{32,64},{64,96},{33,65},{65,97},{34,66},{66,98},{35,67},{67,99},{3... | collective-permute-start | bytes 73736 | tf_op jit(solution)/shard_map/ppermute | solution.py:419
  36.0 0.0 collective-permute-done.5.one_to_three_ref
  36.0 1.5 %collective-permute-done.6.zero_to_three_ref = bf16[144,128]{1,0:T(8,128)(2,1)S(1)} collective-permute-done((bf16[144,128]{1,0:T(8,128)(2,1)S(1)}, bf16[144,128]{1,0:T(8,128)(2,1)S(1)}, u32[]{:S(2)}, u32[]{:S(2)}) %collective-permute-start.6) | collective-permute-done | bytes 36896 | tf_op jit(solution)/shard_map/ppermute | solution.py:411
  37.5 0.0 collective-permute-done.4.below_ref
  37.5 0.5 %shard_map.63 = bf16[16,64,128]{2,1,0:T(8,128)(2,1)S(1)} custom-call(bf16[144,128]{1,0:T(8,128)(2,1)S(1)} %collective-permute-done.1.recv_ref.zero_to_one_ref, bf16[96,128]{1,0:T(8,128)(2,1)S(1)} %collective-permute-done.4.below_ref, bf16[96,128]{1,0:T(8,128)(2,1)S(1)} %collective-permute-done.5.one_to_three_ref, ...), custom_call_target="tpu_custom_call" | custom-call | tf_op jit(solution)/shard_map/pallas_call | solution.py:333
  38.0 10.7 %all_to_all.11.x_ref = bf16[16,64,128]{2,1,0:T(8,128)(2,1)S(1)} all-to-all(bf16[16,64,128]{2,1,0:T(8,128)(2,1)S(1)} %shard_map.63), channel_id=1, replica_groups=mesh['dp'=4,'quad'=4,'half'=2,'pair'=2,'core'=2,'inner'=4] {'pair','core..., dimensions={0} | all-to-all | bytes 524288 | tf_op jit(solution)/shard_map/all_to_all | solution.py:443
  48.8 0.8 %shard_map.64 = bf16[128,1024]{1,0:T(8,128)(2,1)} custom-call(bf16[16,64,128]{2,1,0:T(8,128)(2,1)S(1)} %all_to_all.11.x_ref), custom_call_target="tpu_custom_call" | custom-call | tf_op jit(solution)/shard_map/pallas_call | solution.py:333
  (5 shorter events, 0.1 us)
Async XLA Ops:
  20.2 3.5 %collective-permute-start = (bf16[144,128]{1,0:T(8,128)(2,1)S(1)}, bf16[144,128]{1,0:T(8,128)(2,1)S(1)}, u32[]{:S(2)}, u32[]{:S(2)}) collective-permute-start(bf16[144,128]{1,0:T(8,128)(2,1)S(1)} %get-tuple-element.29), channel_id=1, source_target_pairs={{0,16},{1,17},{2,18},{3,19},{4,20},{5,21},{6,22},{7,23},{8,24},{9,... | collective-permute-start | bytes 110600 | tf_op jit(solution)/shard_map/ppermute | solution.py:390
  22.7 11.8 %collective-permute-start.2 = (bf16[144,128]{1,0:T(8,128)(2,1)S(1)}, bf16[144,128]{1,0:T(8,128)(2,1)S(1)}, u32[]{:S(2)}, u32[]{:S(2)}) collective-permute-start(bf16[144,128]{1,0:T(8,128)(2,1)S(1)} %get-tuple-element.29), channel_id=1, source_target_pairs={{16,32},{32,48},{17,33},{33,49},{18,34},{34,50},{19,35},{35,51},{2... | collective-permute-start | bytes 110600 | tf_op jit(solution)/shard_map/ppermute | solution.py:391
  27.2 8.0 %collective-permute-start.1 = (bf16[144,128]{1,0:T(8,128)(2,1)S(1)}, bf16[144,128]{1,0:T(8,128)(2,1)S(1)}, u32[]{:S(2)}, u32[]{:S(2)}) collective-permute-start(bf16[144,128]{1,0:T(8,128)(2,1)S(1)} %get-tuple-element.30.after_ref), channel_id=1, source_target_pairs={{0,32},{1,33},{2,34},{3,35},{4,36},{5,37},{6,38},{7,39},{8,40},{9,... | collective-permute-start | bytes 110600 | tf_op jit(solution)/shard_map/ppermute | solution.py:398
  32.2 3.0 %collective-permute-start.3 = (bf16[144,128]{1,0:T(8,128)(2,1)S(1)}, bf16[144,128]{1,0:T(8,128)(2,1)S(1)}, u32[]{:S(2)}, u32[]{:S(2)}) collective-permute-start(bf16[144,128]{1,0:T(8,128)(2,1)S(1)} %shard_map.58), channel_id=1, source_target_pairs={{48,64},{64,80},{80,96},{96,112},{49,65},{65,81},{81,97},{97,113},... | collective-permute-start | bytes 110600 | tf_op jit(solution)/shard_map/ppermute | solution.py:402
  32.9 4.6 %collective-permute-start.6 = (bf16[144,128]{1,0:T(8,128)(2,1)S(1)}, bf16[144,128]{1,0:T(8,128)(2,1)S(1)}, u32[]{:S(2)}, u32[]{:S(2)}) collective-permute-start(bf16[144,128]{1,0:T(8,128)(2,1)S(1)} %get-tuple-element.30.after_ref), channel_id=1, source_target_pairs={{0,96},{1,97},{2,98},{3,99},{4,100},{5,101},{6,102},{7,103},{8,104... | collective-permute-start | bytes 110600 | tf_op jit(solution)/shard_map/ppermute | solution.py:411
  34.5 1.4 %collective-permute-start.5 = (bf16[96,128]{1,0:T(8,128)(2,1)S(1)}, bf16[96,128]{1,0:T(8,128)(2,1)S(1)}, u32[]{:S(2)}, u32[]{:S(2)}) collective-permute-start(bf16[96,128]{1,0:T(8,128)(2,1)S(1)} %get-tuple-element.37), channel_id=1, source_target_pairs={{32,96},{33,97},{34,98},{35,99},{36,100},{37,101},{38,102},{39,103... | collective-permute-start | bytes 73736 | tf_op jit(solution)/shard_map/ppermute | solution.py:410
  35.3 2.2 %collective-permute-start.4 = (bf16[96,128]{1,0:T(8,128)(2,1)S(1)}, bf16[96,128]{1,0:T(8,128)(2,1)S(1)}, u32[]{:S(2)}, u32[]{:S(2)}) collective-permute-start(bf16[96,128]{1,0:T(8,128)(2,1)S(1)} %get-tuple-element.36), channel_id=1, source_target_pairs={{32,64},{64,96},{33,65},{65,97},{34,66},{66,98},{35,67},{67,99},{3... | collective-permute-start | bytes 73736 | tf_op jit(solution)/shard_map/ppermute | solution.py:419

commit v14 on v12

--- a/solution.py
+++ b/solution.py
@@ -217,6 +217,7 @@
     near_ref,
     taps_ref,
     sent_ref,
+    three_ref,
     num_ref,
     win_ref,
     phi_ref,
@@ -224,6 +225,7 @@
     @pl.when(quad_ref[0] == 0)
     def _():
         sent_ref[...] = fold(*paired(own_ref, near_ref, taps_ref))
+        three_ref[...] = sent_ref[...]
         local_blocks(first_ref, x_ref, conv_ref, near_ref, taps_ref, num_ref, win_ref, phi_ref)
 
 
@@ -237,11 +239,13 @@
     num_in_ref,
     win_in_ref,
     phi_in_ref,
+    three_in_ref,
     sent_ref,
     pair_ref,
     num_ref,
     win_ref,
     phi_ref,
+    three_ref,
 ):
     @pl.when(quad_ref[0] == 1)
     def _():
@@ -384,22 +388,22 @@
     low_near = lax.ppermute(sent, stack, [(0, 1)])
     second_near = lax.ppermute(sent, stack, [(1, 2), (2, 3)])
     upper_near = lax.ppermute(sent, stack, [(i, i + 1) for i in range(3, groups - 1)])
-    lowest, *local = call(
+    lowest, three, *local = call(
         lowest_kernel,
-        [packed_state, *local_shapes],
+        [packed_state, packed_state, *local_shapes],
         [quad, first],
         [own, mine, conv, low_near, taps],
     )
     zero_to_one = lax.ppermute(lowest, "quad", [(0, 1)])
-    second, pair, *local = call(
+    second, pair, *local, three = call(
         second_kernel,
-        [packed_state, pltpu.VMEM((2, VDIM, LANES), F32), *local_shapes],
+        [packed_state, pltpu.VMEM((2, VDIM, LANES), F32), *local_shapes, packed_state],
         [quad],
-        [own, mine, conv, second_near, taps, *local],
-        {6: 2, 7: 3, 8: 4},
+        [own, mine, conv, second_near, taps, *local, three],
+        {6: 2, 7: 3, 8: 4, 9: 5},
     )
     one_to_three = lax.ppermute(second, "quad", [(1, 3)])
-    zero_to_three = lax.ppermute(lowest, "quad", [(0, 3)])
+    zero_to_three = lax.ppermute(three, "quad", [(0, 3)])
     both = call(join_kernel, [packed_state], [quad], [pair, zero_to_one, taps])
     upper, near = call(
         upper_kernel,

time: 49.8 us -> 50.3 us (1.010)
  the two profiles are of different devices: /device:TPU:329 before, /device:TPU:1 now
where the time goes in v14:
time: 50.3 us; the launch traced here: 50 us
  blocking collectives  30.2 us (60%)
  starting transfers between devices  12.7 us (25%)
  Pallas kernels  6.84 us (14%)
    all_to_all x1, blocking collectives, on_device(): mine = lax.all_to_all(packed, group, 0, 0)  18.3 us
    all_to_all x1, blocking collectives, on_device(): heads = lax.all_to_all(done, group, 0, 0)  11.9 us
    pallas_call x8, Pallas kernels, call(): pl.pallas_call(kernel, out_shape=outs[0] if single else tuple(outs), in_s...  5.56 us
    ppermute x1, starting transfers between devices, on_device(): zero_to_one = lax.ppermute(lowest, 'quad', [(0, 1)])  5.3 us
    ppermute x1, starting transfers between devices, on_device(): low_near = lax.ppermute(sent, stack, [(0, 1)])  2.48 us
    ppermute x1, starting transfers between devices, on_device(): zero_to_three = lax.ppermute(three, 'quad', [(0, 3)])  2.23 us
    pallas_call x1, Pallas kernels, on_device(): pl.pallas_call(pack_kernel, out_shape=(pltpu.VMEM((HEADS, PART, BLK), BF1...  1.28 us
  transfers between devices with their start and end apart: 7, of which 1 were waited for; matrix products, arithmetic and copies ran while one was open for 0% of the time, Pallas kernels for 7%

profile of v14, /device:TPU:1, one launch (start us, length us, event | category | flops | bytes accessed | tf_op | source)
XLA Modules:
  0.0 50.0 jit_solution(2650398275390088275)
XLA Ops:
  0.0 1.3 %shard_map.55 = (bf16[16,96,128]{2,1,0:T(8,128)(2,1)S(1)}, f32[4,64,128]{2,1,0:T(8,128)S(1)}) custom-call(s32[1]{0:T(128)} %bitcast.2.head_ref, bf16[128,256]{1,0:T(8,128)(2,1)} %q_ref.1, bf16[128,256]{1,0:T(8,128)(2,1)} %k_ref.1, bf16[128,1024]{1,0:T(8,128)(2,1)} %v_ref.1, f32[3,1024]{1,0:T(4,128)} %w_ref.1, f32[1,1024]{1,0:T(1,128)} %bitcast.4), custom_call_target="tpu_custom_call" | custom-call | tf_op jit(solution)/shard_map/pallas_call | solution.py:352
  1.3 18.3 %all_to_all.10.x_ref = bf16[16,96,128]{2,1,0:T(8,128)(2,1)S(1)} all-to-all(bf16[16,96,128]{2,1,0:T(8,128)(2,1)S(1)} %get-tuple-element.26), channel_id=1, replica_groups=mesh['dp'=4,'quad'=4,'half'=2,'pair'=2,'core'=2,'inner'=4] {'pair','core..., dimensions={0} | all-to-all | bytes 786432 | tf_op jit(solution)/shard_map/all_to_all | solution.py:368
  19.6 0.6 %shard_map.56 = (bf16[144,128]{1,0:T(8,128)(2,1)S(1)}, f32[2,64,128]{2,1,0:T(8,128)S(1)}, bf16[16,64,128]{2,1,0:T(8,128)(2,1)S(1)}) custom-call(bf16[16,96,128]{2,1,0:T(8,128)(2,1)S(1)} %all_to_all.10.x_ref, f32[4,64,128]{2,1,0:T(8,128)S(1)} %get-tuple-element.27.taps_ref), custom_call_target="tpu_custom_call" | custom-call | tf_op jit(solution)/shard_map/pallas_call | solution.py:332
  20.2 2.5 %collective-permute-start = (bf16[144,128]{1,0:T(8,128)(2,1)S(1)}, bf16[144,128]{1,0:T(8,128)(2,1)S(1)}, u32[]{:S(2)}, u32[]{:S(2)}) collective-permute-start(bf16[144,128]{1,0:T(8,128)(2,1)S(1)} %get-tuple-element.30), channel_id=1, source_target_pairs={{0,16},{1,17},{2,18},{3,19},{4,20},{5,21},{6,22},{7,23},{8,24},{9,... | collective-permute-start | bytes 110600 | tf_op jit(solution)/shard_map/ppermute | solution.py:388
  22.6 0.7 %collective-permute-start.2 = (bf16[144,128]{1,0:T(8,128)(2,1)S(1)}, bf16[144,128]{1,0:T(8,128)(2,1)S(1)}, u32[]{:S(2)}, u32[]{:S(2)}) collective-permute-start(bf16[144,128]{1,0:T(8,128)(2,1)S(1)} %get-tuple-element.30), channel_id=1, source_target_pairs={{16,32},{32,48},{17,33},{33,49},{18,34},{34,50},{19,35},{35,51},{2... | collective-permute-start | bytes 110600 | tf_op jit(solution)/shard_map/ppermute | solution.py:389
  23.3 0.7 %collective-permute-start.3 = (bf16[144,128]{1,0:T(8,128)(2,1)S(1)}, bf16[144,128]{1,0:T(8,128)(2,1)S(1)}, u32[]{:S(2)}, u32[]{:S(2)}) collective-permute-start(bf16[144,128]{1,0:T(8,128)(2,1)S(1)} %get-tuple-element.30), channel_id=1, source_target_pairs={{48,64},{64,80},{80,96},{96,112},{49,65},{65,81},{81,97},{97,113},... | collective-permute-start | bytes 110600 | tf_op jit(solution)/shard_map/ppermute | solution.py:390
  24.0 0.0 collective-permute-done.near_ref.low_ref
  24.0 3.5 %shard_map.57 = (bf16[96,128]{1,0:T(8,128)(2,1)S(1)}, bf16[96,128]{1,0:T(8,128)(2,1)S(1)}, f32[16,64,128]{2,1,0:T(8,128)S(1)}, f32[16,64,128]{2,1,0:T(8,128)S(1)}, bf16[160,2048]{1,0:T(8,128)(2,1)S(1)}) custom-call(s32[1]{0:T(128)} %bitcast.quad_ref, s32[1]{0:T(128)} %bitcast.1.first_ref, f32[2,64,128]{2,1,0:T(8,128)S(1)} %get-tuple-element.28.own_ref, ...), custom_call_target="tpu_custom_call" | custom-call | tf_op jit(solution)/shard_map/pallas_call | solution.py:332
  27.5 5.3 %collective-permute-start.1 = (bf16[96,128]{1,0:T(8,128)(2,1)S(1)}, bf16[96,128]{1,0:T(8,128)(2,1)S(1)}, u32[]{:S(2)}, u32[]{:S(2)}) collective-permute-start(bf16[96,128]{1,0:T(8,128)(2,1)S(1)} %get-tuple-element.31), channel_id=1, source_target_pairs={{0,32},{1,33},{2,34},{3,35},{4,36},{5,37},{6,38},{7,39},{8,40},{9,... | collective-permute-start | bytes 73736 | tf_op jit(solution)/shard_map/ppermute | solution.py:397
  32.8 0.0 collective-permute-done.2.near_ref.second_ref
  32.9 0.7 %collective-permute-start.5 = (bf16[96,128]{1,0:T(8,128)(2,1)S(1)}, bf16[96,128]{1,0:T(8,128)(2,1)S(1)}, u32[]{:S(2)}, u32[]{:S(2)}) collective-permute-start(bf16[96,128]{1,0:T(8,128)(2,1)S(1)} %get-tuple-element.38), channel_id=1, source_target_pairs={{32,96},{33,97},{34,98},{35,99},{36,100},{37,101},{38,102},{39,103... | collective-permute-start | bytes 73736 | tf_op jit(solution)/shard_map/ppermute | solution.py:405
  33.5 2.2 %collective-permute-start.6 = (bf16[96,128]{1,0:T(8,128)(2,1)S(1)}, bf16[96,128]{1,0:T(8,128)(2,1)S(1)}, u32[]{:S(2)}, u32[]{:S(2)}) collective-permute-start(bf16[96,128]{1,0:T(8,128)(2,1)S(1)} %get-tuple-element.39), channel_id=1, source_target_pairs={{0,96},{1,97},{2,98},{3,99},{4,100},{5,101},{6,102},{7,103},{8,104... | collective-permute-start | bytes 73736 | tf_op jit(solution)/shard_map/ppermute | solution.py:406
  35.8 0.0 collective-permute-done.1.recv_ref.zero_to_one_ref
  35.8 0.0 collective-permute-done.3.upper_ref
  35.9 0.7 %collective-permute-start.4 = (bf16[96,128]{1,0:T(8,128)(2,1)S(1)}, bf16[96,128]{1,0:T(8,128)(2,1)S(1)}, u32[]{:S(2)}, u32[]{:S(2)}) collective-permute-start(bf16[96,128]{1,0:T(8,128)(2,1)S(1)} %get-tuple-element.37), channel_id=1, source_target_pairs={{32,64},{64,96},{33,65},{65,97},{34,66},{66,98},{35,67},{67,99},{3... | collective-permute-start | bytes 73736 | tf_op jit(solution)/shard_map/ppermute | solution.py:414
  36.6 0.0 collective-permute-done.5.one_to_three_ref
  36.6 0.2 collective-permute-done.6.zero_to_three_ref
  36.7 0.0 collective-permute-done.4.below_ref
  36.7 0.6 %shard_map.62 = bf16[16,64,128]{2,1,0:T(8,128)(2,1)S(1)} custom-call(bf16[96,128]{1,0:T(8,128)(2,1)S(1)} %collective-permute-done.1.recv_ref.zero_to_one_ref, bf16[96,128]{1,0:T(8,128)(2,1)S(1)} %collective-permute-done.4.below_ref, bf16[96,128]{1,0:T(8,128)(2,1)S(1)} %collective-permute-done.5.one_to_three_ref, ...), custom_call_target="tpu_custom_call" | custom-call | tf_op jit(solution)/shard_map/pallas_call | solution.py:332
  37.3 11.9 %all_to_all.11.x_ref = bf16[16,64,128]{2,1,0:T(8,128)(2,1)S(1)} all-to-all(bf16[16,64,128]{2,1,0:T(8,128)(2,1)S(1)} %shard_map.62), channel_id=1, replica_groups=mesh['dp'=4,'quad'=4,'half'=2,'pair'=2,'core'=2,'inner'=4] {'pair','core..., dimensions={0} | all-to-all | bytes 524288 | tf_op jit(solution)/shard_map/all_to_all | solution.py:438
  49.2 0.8 %shard_map.63 = bf16[128,1024]{1,0:T(8,128)(2,1)} custom-call(bf16[16,64,128]{2,1,0:T(8,128)(2,1)S(1)} %all_to_all.11.x_ref), custom_call_target="tpu_custom_call" | custom-call | tf_op jit(solution)/shard_map/pallas_call | solution.py:332
  (4 shorter events, 0.1 us)
Async XLA Ops:
  20.2 3.8 %collective-permute-start = (bf16[144,128]{1,0:T(8,128)(2,1)S(1)}, bf16[144,128]{1,0:T(8,128)(2,1)S(1)}, u32[]{:S(2)}, u32[]{:S(2)}) collective-permute-start(bf16[144,128]{1,0:T(8,128)(2,1)S(1)} %get-tuple-element.30), channel_id=1, source_target_pairs={{0,16},{1,17},{2,18},{3,19},{4,20},{5,21},{6,22},{7,23},{8,24},{9,... | collective-permute-start | bytes 110600 | tf_op jit(solution)/shard_map/ppermute | solution.py:388
  22.6 10.2 %collective-permute-start.2 = (bf16[144,128]{1,0:T(8,128)(2,1)S(1)}, bf16[144,128]{1,0:T(8,128)(2,1)S(1)}, u32[]{:S(2)}, u32[]{:S(2)}) collective-permute-start(bf16[144,128]{1,0:T(8,128)(2,1)S(1)} %get-tuple-element.30), channel_id=1, source_target_pairs={{16,32},{32,48},{17,33},{33,49},{18,34},{34,50},{19,35},{35,51},{2... | collective-permute-start | bytes 110600 | tf_op jit(solution)/shard_map/ppermute | solution.py:389
  23.3 12.5 %collective-permute-start.3 = (bf16[144,128]{1,0:T(8,128)(2,1)S(1)}, bf16[144,128]{1,0:T(8,128)(2,1)S(1)}, u32[]{:S(2)}, u32[]{:S(2)}) collective-permute-start(bf16[144,128]{1,0:T(8,128)(2,1)S(1)} %get-tuple-element.30), channel_id=1, source_target_pairs={{48,64},{64,80},{80,96},{96,112},{49,65},{65,81},{81,97},{97,113},... | collective-permute-start | bytes 110600 | tf_op jit(solution)/shard_map/ppermute | solution.py:390
  27.5 8.3 %collective-permute-start.1 = (bf16[96,128]{1,0:T(8,128)(2,1)S(1)}, bf16[96,128]{1,0:T(8,128)(2,1)S(1)}, u32[]{:S(2)}, u32[]{:S(2)}) collective-permute-start(bf16[96,128]{1,0:T(8,128)(2,1)S(1)} %get-tuple-element.31), channel_id=1, source_target_pairs={{0,32},{1,33},{2,34},{3,35},{4,36},{5,37},{6,38},{7,39},{8,40},{9,... | collective-permute-start | bytes 73736 | tf_op jit(solution)/shard_map/ppermute | solution.py:397
  32.9 3.7 %collective-permute-start.5 = (bf16[96,128]{1,0:T(8,128)(2,1)S(1)}, bf16[96,128]{1,0:T(8,128)(2,1)S(1)}, u32[]{:S(2)}, u32[]{:S(2)}) collective-permute-start(bf16[96,128]{1,0:T(8,128)(2,1)S(1)} %get-tuple-element.38), channel_id=1, source_target_pairs={{32,96},{33,97},{34,98},{35,99},{36,100},{37,101},{38,102},{39,103... | collective-permute-start | bytes 73736 | tf_op jit(solution)/shard_map/ppermute | solution.py:405
  33.5 3.2 %collective-permute-start.6 = (bf16[96,128]{1,0:T(8,128)(2,1)S(1)}, bf16[96,128]{1,0:T(8,128)(2,1)S(1)}, u32[]{:S(2)}, u32[]{:S(2)}) collective-permute-start(bf16[96,128]{1,0:T(8,128)(2,1)S(1)} %get-tuple-element.39), channel_id=1, source_target_pairs={{0,96},{1,97},{2,98},{3,99},{4,100},{5,101},{6,102},{7,103},{8,104... | collective-permute-start | bytes 73736 | tf_op jit(solution)/shard_map/ppermute | solution.py:406
  35.9 0.9 %collective-permute-start.4 = (bf16[96,128]{1,0:T(8,128)(2,1)S(1)}, bf16[96,128]{1,0:T(8,128)(2,1)S(1)}, u32[]{:S(2)}, u32[]{:S(2)}) collective-permute-start(bf16[96,128]{1,0:T(8,128)(2,1)S(1)} %get-tuple-element.37), channel_id=1, source_target_pairs={{32,64},{64,96},{33,65},{65,97},{34,66},{66,98},{35,67},{67,99},{3... | collective-permute-start | bytes 73736 | tf_op jit(solution)/shard_map/ppermute | solution.py:414
